TPU v7x, 512 devices: a whole 4x8x8 slice. The times are simulated.
512 devices in a mesh: dp: 16 (over z, core), mp: 32 (over y, x).
Axes of the slice: x: 4, y: 8, z: 8, core: 2. Of those that a mesh axis runs over, the one named last changes fastest.
Arguments:
- policy_hidden: bfloat16 [1024, 3584], P('dp'), may hold values from -96 to 96
- reference_hidden: bfloat16 [1024, 3584], P('dp'), may hold values from -96 to 96
- policy_gain: float32 [3584], replicated, may hold values from 0.5 to 1.5
- reference_gain: float32 [3584], replicated, may hold values from 0.5 to 1.5
- policy_embedding: bfloat16 [131072, 3584], P(('dp', 'mp')), may hold values from -1 to 1
- reference_embedding: bfloat16 [131072, 3584], P(('dp', 'mp')), may hold values from -1 to 1
- mixture_weight: float32 [1024], replicated, may hold values from 0.1 to 0.9
- sampled_tokens: int32 [1024], replicated, may hold values from 0 to 131071
Outputs:
- mixture_shift: float32 [1024, 131072], P(None, ('dp', 'mp'))
- sampled_logprobs: float32 [3, 1024], P(None, 'dp')
All inputs are finite; a program needn't handle non-finite values.
Results may differ from a plain program's by a relative error of at most 0.002.
Values may be sent and summed in bfloat16 or wider, within the bound.
No kernel may reach another device: no remote copies, remote signals or barrier semaphores. Data moves between devices by JAX's collectives and lax.ppermute only.
A program may use at most 64 MiB of HBM per device.

v0:
```python
import jax
import jax.numpy as jnp
from jax import lax
from jax.sharding import Mesh
from jax.sharding import PartitionSpec as P

DP = ("dp_0", "dp_1")
MP = ("mp_0", "mp_1")
DP_MP = ("dp_0", "dp_1", "mp_0", "mp_1")


softcap = 30.0
epsilon = 1e-06


def by_axis(x, axes):
    for axis in axes:
        x = lax.psum(x, axis)
    return x


def normalize(hidden, gain):
    values = hidden.astype(jnp.float32)
    meansq = jnp.mean(values * values, axis=-1, keepdims=True)
    return (values * lax.rsqrt(meansq + epsilon) * gain).astype(jnp.bfloat16)


def contract(normed, embedding):
    return lax.dot_general(
        normed, embedding, (((1,), (1,)), ((), ())), preferred_element_type=jnp.float32
    )


def local(
    policy_hidden,
    reference_hidden,
    policy_gain,
    reference_gain,
    policy_embedding,
    reference_embedding,
    mixture_weight,
    sampled_tokens,
):
    seq_local = policy_hidden.shape[0]
    vocab_local = policy_embedding.shape[0]
    stacked = jnp.stack(
        [normalize(policy_hidden, policy_gain), normalize(reference_hidden, reference_gain)]
    )
    piece = lax.all_gather(stacked, DP, axis=1, tiled=True)
    raw = jnp.stack([contract(piece[0], policy_embedding), contract(piece[1], reference_embedding)])
    capped = softcap * jnp.tanh(raw / softcap)
    capped_policy = capped[0]
    capped_reference = capped[1]
    weight = mixture_weight[:, None]
    mixed = (1.0 - weight) * capped_policy + weight * capped_reference
    shard = lax.axis_index(DP) * lax.axis_size(MP) + lax.axis_index(MP)
    first = shard * vocab_local
    columns = lax.broadcasted_iota(jnp.int32, (1, vocab_local), 1)
    onehot = (sampled_tokens[:, None] - first == columns).astype(jnp.float32)
    terms = (
        jnp.sum(jnp.exp(capped_policy), axis=1),
        jnp.sum(jnp.exp(capped_reference), axis=1),
        jnp.sum(jnp.exp(mixed), axis=1),
        jnp.sum(onehot * capped_policy, axis=1),
        jnp.sum(onehot * capped_reference, axis=1),
    )
    policy_sum, reference_sum, mixture_sum, policy_pick, reference_pick = (
        by_axis(terms[0], DP_MP),
        by_axis(terms[1], DP_MP),
        by_axis(terms[2], DP_MP),
        by_axis(terms[3], DP_MP),
        by_axis(terms[4], DP_MP),
    )
    policy_total = jnp.log(policy_sum)
    reference_total = jnp.log(reference_sum)
    mixture_total = jnp.log(mixture_sum)
    mixed_pick = (1.0 - mixture_weight) * policy_pick + mixture_weight * reference_pick
    policy_logp = policy_pick - policy_total
    reference_logp = reference_pick - reference_total
    mixture_logp = mixed_pick - mixture_total
    mixture_shift = mixed - mixture_total[:, None] - (capped_policy - policy_total[:, None])
    every_logp = jnp.stack([policy_logp, reference_logp, mixture_logp])
    sampled_logprobs = lax.dynamic_slice_in_dim(
        every_logp, lax.axis_index(DP) * seq_local, seq_local, 1
    )
    return (mixture_shift, sampled_logprobs)


def solution(mesh):
    split = Mesh(mesh.devices.reshape(8, 2, 8, 4), ("dp_0", "dp_1", "mp_0", "mp_1"))
    in_specs = (P(DP, None), P(DP, None), P(), P(), P(DP_MP, None), P(DP_MP, None), P(), P())
    out_specs = (P(None, DP_MP), P(None, DP))
    return jax.shard_map(local, mesh=split, in_specs=in_specs, out_specs=out_specs, check_vma=False)
```

profile of v0, /device:TPU:4, one launch (start us, length us, event | category | flops | bytes accessed | tf_op | source)
XLA Modules:
  0.0 205.5 jit_solution(13288046181011595460)
XLA Ops:
  7.2 0.0 copy-start
  7.2 0.0 all-gather.2.cloned.1.call-start
  7.2 1.3 fusion.9
  8.6 1.2 fusion.6
  9.8 0.0 copy-start.2
  9.8 0.0 copy-start.3
  9.8 1.5 fusion.12
  11.3 1.0 pad_maximum_fusion
  12.3 0.0 all-gather.2.cloned.1.call-update
  12.4 93.7 %all-gather.2.cloned.1.call-done = bf16[2,1024,3584]{2,1,0:T(8,128)(2,1)} async-done(((bf16[2,64,3584]{2,1,0:T(8,128)(2,1)}), bf16[2,1024,3584]{2,1,0:T(8,128)(2,1)}) %all-gather.2.cloned.1.call-update) | async-done | bytes 14680080 | tf_op jit(solution)/shard_map/all_gather | solution.py:49
  106.1 5.3 %fusion.5 = f32[1,1024,256]{1,2,0:T(8,128)S(1)} fusion(bf16[256,3584]{1,0:T(8,128)(2,1)S(1)} %copy-done, bf16[2,1024,3584]{2,1,0:T(8,128)(2,1)} %all-gather.2.cloned.1.call-done), kind=kOutput, calls=%fused_computation.8 | convolution fusion | flops 1879048192 | bytes 10223616 | tf_op jit(solution)/shard_map/dot_general | solution.py:29
  111.4 1.9 copy-done.4
  113.3 0.5 copy-done.5
  113.9 2.1 %fusion.4 = f32[1,1024,256]{1,2,0:T(8,128)S(1)} fusion(bf16[256,3584]{1,0:T(8,128)(2,1)S(1)} %copy-done.5, bf16[2,1024,3584]{2,1,0:T(8,128)(2,1)S(1)} %copy-done.4), kind=kOutput, calls=%fused_computation.7 | convolution fusion | flops 1879048192 | bytes 10223616 | tf_op jit(solution)/shard_map/dot_general | solution.py:29
  115.9 0.3 fusion.3
  116.2 1.3 copy-done.1
  117.6 0.6 select_reduce_fusion
  118.2 28.2 %all-reduce.1 = (f32[1024]{0:T(1024)S(1)}, f32[1024]{0:T(1024)S(1)}, f32[1024]{0:T(1024)S(1)}, f32[1024]{0:T(1024)S(1)}, f32[1024]{0:T(1024)S(1)}) all-reduce(f32[1024]{0:T(1024)S(1)} %get-tuple-element.8, f32[1024]{0:T(1024)S(1)} %get-tuple-element.7, ...), channel_id=1, replica_groups=mesh['dp_0'=8,'dp_1'=2,'mp_0'=8,'mp_1'=4] {'dp_0'}, use_global_device_ids=true, to_apply=%region_8.0 | all-reduce | flops 5120 | bytes 40960 | tf_op jit(solution)/shard_map/psum | solution.py:18
  146.4 3.4 %all-reduce.3 = (f32[1024]{0:T(1024)S(1)}, f32[1024]{0:T(1024)S(1)}, f32[1024]{0:T(1024)S(1)}, f32[1024]{0:T(1024)S(1)}, f32[1024]{0:T(1024)S(1)}) all-reduce(f32[1024]{0:T(1024)S(1)} %get-tuple-element.14, f32[1024]{0:T(1024)S(1)} %get-tuple-element.15, ...), channel_id=1, replica_groups=mesh['dp_0'=8,'dp_1'=2,'mp_0'=8,'mp_1'=4] {'dp_1'}, use_global_device_ids=true, to_apply=%region_9.0 | all-reduce | flops 5120 | bytes 40960 | tf_op jit(solution)/shard_map/psum | solution.py:18
  149.8 29.7 %all-reduce = (f32[1024]{0:T(1024)S(1)}, f32[1024]{0:T(1024)S(1)}, f32[1024]{0:T(1024)S(1)}, f32[1024]{0:T(1024)S(1)}, f32[1024]{0:T(1024)S(1)}) all-reduce(f32[1024]{0:T(1024)S(1)} %get-tuple-element.24, f32[1024]{0:T(1024)S(1)} %get-tuple-element.25, ...), channel_id=1, replica_groups=mesh['dp_0'=8,'dp_1'=2,'mp_0'=8,'mp_1'=4] {'mp_0'}, use_global_device_ids=true, to_apply=%region_10.0 | all-reduce | flops 5120 | bytes 40960 | tf_op jit(solution)/shard_map/psum | solution.py:18
  179.5 15.4 %all-reduce.2 = (f32[1024]{0:T(1024)S(1)}, f32[1024]{0:T(1024)S(1)}, f32[1024]{0:T(1024)S(1)}, f32[1024]{0:T(1024)S(1)}, f32[1024]{0:T(1024)S(1)}) all-reduce(f32[1024]{0:T(1024)S(1)} %get-tuple-element.9, f32[1024]{0:T(1024)S(1)} %get-tuple-element.10, ...), channel_id=1, replica_groups=mesh['dp_0'=8,'dp_1'=2,'mp_0'=8,'mp_1'=4] {'mp_1'}, use_global_device_ids=true, to_apply=%region_11.0 | all-reduce | flops 5120 | bytes 40960 | tf_op jit(solution)/shard_map/psum | solution.py:18
  194.9 1.8 subtract_subtract_fusion
  196.7 1.3 copy.10
  198.0 0.7 fusion.15
  (11 shorter events, 0.0 us)
Async XLA Ops:
  7.2 98.9 %copy-start = (bf16[256,3584]{1,0:T(8,128)(2,1)S(1)}, bf16[256,3584]{1,0:T(8,128)(2,1)}, u32[]{:S(2)}) copy-start(bf16[256,3584]{1,0:T(8,128)(2,1)} %param.13) | copy-start | bytes 5505028
  7.2 98.9 %all-gather.2.cloned.1.call-start = ((), (), s32[]{:S(2)}) async-start(), calls=%async_computation | async-start | bytes 15597568 | tf_op jit(solution)/shard_map/all_gather | solution.py:49
  9.8 2.6 %copy-start.2 = (f32[1024]{0:T(1024)S(1)}, f32[1024]{0:T(1024)}, u32[]{:S(2)}) copy-start(f32[1024]{0:T(1024)} %param.14) | copy-start | bytes 12292
  9.8 2.6 %copy-start.3 = (s32[1024]{0:T(1024)S(1)}, s32[1024]{0:T(1024)}, u32[]{:S(2)}) copy-start(s32[1024]{0:T(1024)} %param.15) | copy-start | bytes 12292
  106.1 7.3 %copy-start.4 = (bf16[2,1024,3584]{2,1,0:T(8,128)(2,1)S(1)}, bf16[2,1024,3584]{2,1,0:T(8,128)(2,1)}, u32[]{:S(2)}) copy-start(bf16[2,1024,3584]{2,1,0:T(8,128)(2,1)} %all-gather.2.cloned.1.call-done) | copy-start | bytes 44040196
  106.1 7.8 %copy-start.5 = (bf16[256,3584]{1,0:T(8,128)(2,1)S(1)}, bf16[256,3584]{1,0:T(8,128)(2,1)}, u32[]{:S(2)}) copy-start(bf16[256,3584]{1,0:T(8,128)(2,1)} %param.12) | copy-start | bytes 5505028
  116.2 1.4 copy-start.1
Sparse Core Ops, SparseCore 0:
  12.5 93.5 all-gather.1
where the time goes:
time: 206 us
  waiting for transfers between devices  93.7 us (45%)
  blocking collectives  76.7 us (37%)
  between operations  14.2 us (7%)
  other arithmetic  8.41 us (4%)
  matrix products  7.39 us (4%)
  local copies, waits for them, and re-layouts  5.12 us (2%)
    all_gather x1, waiting for transfers between devices, local(): piece = lax.all_gather(stacked, DP, axis=1, tiled=True)  93.7 us
    psum x4, blocking collectives, by_axis(): x = lax.psum(x, axis)  76.7 us
    dot_general x2, matrix products, contract(): lax.dot_general(normed, embedding, (((1,), (1,)), ((), ())), preferred_el...  7.39 us
    unnamed x13, local copies, waits for them, and re-layouts  5.12 us
  transfers between devices with their start and end apart: 1, of which 1 were waited for; matrix products, arithmetic and copies ran while one was open for 0% of the time, Pallas kernels for 0%

commit v1 on v0

v1 whole, which is shorter than its diff:
```python
import jax
import jax.numpy as jnp
from jax import lax
from jax.experimental import pallas as pl
from jax.experimental.pallas import tpu as pltpu
from jax.sharding import Mesh
from jax.sharding import PartitionSpec as P

DP = ("dp_0", "dp_1")
MP = ("mp_0", "mp_1")
DP_MP = ("dp_0", "dp_1", "mp_0", "mp_1")

softcap = 30.0
epsilon = 1e-06

VMEM_LIMIT = 48 * 1024 * 1024


def normalize_kernel(half_ref, policy_ref, reference_ref, policy_gain_ref, reference_gain_ref, out_ref):
    for model, (hidden_ref, gain_ref) in enumerate(
        ((policy_ref, policy_gain_ref), (reference_ref, reference_gain_ref))
    ):
        values = hidden_ref[...].astype(jnp.float32)
        meansq = jnp.mean(values * values, axis=-1, keepdims=True)
        normed = values * lax.rsqrt(meansq + epsilon) * gain_ref[...]
        out_ref[model] = normed.astype(jnp.bfloat16)


def normalize(half, policy_hidden, reference_hidden, policy_gain, reference_gain):
    rows, width = policy_hidden.shape
    part = rows // 2
    hidden_spec = pl.BlockSpec((part, width), lambda i, half: (half[0], 0))
    gain_spec = pl.BlockSpec((1, width), lambda i, half: (0, 0))
    return pl.pallas_call(
        normalize_kernel,
        grid_spec=pltpu.PrefetchScalarGridSpec(
            num_scalar_prefetch=1,
            grid=(1,),
            in_specs=[hidden_spec, hidden_spec, gain_spec, gain_spec],
            out_specs=pl.BlockSpec((2, part, width), lambda i, half: (0, 0, 0)),
        ),
        out_shape=jax.ShapeDtypeStruct((2, part, width), jnp.bfloat16),
        compiler_params=pltpu.CompilerParams(vmem_limit_bytes=VMEM_LIMIT),
        name="normalize",
    )(half, policy_hidden, reference_hidden, policy_gain, reference_gain)


def mixture_kernel(
    hidden_ref,
    policy_own_ref,
    policy_other_ref,
    reference_own_ref,
    reference_other_ref,
    weight_ref,
    token_ref,
    diff_own_ref,
    diff_other_ref,
    sums_ref,
    policy_acc,
    reference_acc,
):
    step = pl.program_id(0)
    shards, _, part, depth = hidden_ref.shape
    vocab = policy_own_ref.shape[0]
    seqs = shards * part

    @pl.when(step == 0)
    def _():
        policy_acc[...] = jnp.zeros_like(policy_acc)
        reference_acc[...] = jnp.zeros_like(reference_acc)

    for model, (own_ref, other_ref, acc) in enumerate(
        (
            (policy_own_ref, policy_other_ref, policy_acc),
            (reference_own_ref, reference_other_ref, reference_acc),
        )
    ):
        hidden = hidden_ref[:, model].reshape(seqs, depth)
        for place, rows_ref in enumerate((own_ref, other_ref)):
            acc[pl.ds(place * vocab, vocab), :] += lax.dot_general(
                rows_ref[...], hidden, (((1,), (1,)), ((), ())), preferred_element_type=jnp.float32
            )

    @pl.when(step == pl.num_programs(0) - 1)
    def _():
        weight = weight_ref[...]
        keep = 1.0 - weight
        totals = [jnp.zeros((8, seqs), jnp.float32) for _ in range(5)]
        for place, diff_ref in enumerate((diff_own_ref, diff_other_ref)):
            token = token_ref[place : place + 1, :]

            def body(i, carry, place=place, diff_ref=diff_ref, token=token):
                row = pl.multiple_of(i * 8, 8)
                policy = softcap * jnp.tanh(policy_acc[pl.ds(place * vocab + row, 8), :] * (1.0 / softcap))
                reference = softcap * jnp.tanh(
                    reference_acc[pl.ds(place * vocab + row, 8), :] * (1.0 / softcap)
                )
                mixed = keep * policy + weight * reference
                diff_ref[pl.ds(row, 8), :] = mixed - policy
                hit = lax.broadcasted_iota(jnp.int32, (8, seqs), 0) + row == token
                return (
                    carry[0] + jnp.exp(policy),
                    carry[1] + jnp.exp(mixed),
                    carry[2] + jnp.exp(reference),
                    carry[3] + jnp.where(hit, policy, 0.0),
                    carry[4] + jnp.where(hit, reference, 0.0),
                )

            totals = lax.fori_loop(0, vocab // 8, body, tuple(totals))
        for k in range(5):
            sums_ref[k : k + 1, :] = jnp.sum(totals[k], axis=0, keepdims=True)


def mixture(hidden, policy_own, policy_other, reference_own, reference_other, weight, token):
    shards, _, part, width = hidden.shape
    vocab = policy_own.shape[0]
    seqs = shards * part
    depth = width // 7
    rows_spec = pl.BlockSpec((vocab, depth), lambda k: (0, k))
    whole = lambda *shape: pl.BlockSpec(shape, lambda k: (0,) * len(shape))
    return pl.pallas_call(
        mixture_kernel,
        grid=(width // depth,),
        in_specs=[
            pl.BlockSpec((shards, 2, part, depth), lambda k: (0, 0, 0, k)),
            rows_spec,
            rows_spec,
            rows_spec,
            rows_spec,
            whole(1, seqs),
            whole(2, seqs),
        ],
        out_specs=[whole(vocab, seqs), whole(vocab, seqs), whole(5, seqs)],
        out_shape=[
            jax.ShapeDtypeStruct((vocab, seqs), jnp.float32),
            jax.ShapeDtypeStruct((vocab, seqs), jnp.float32),
            jax.ShapeDtypeStruct((5, seqs), jnp.float32),
        ],
        scratch_shapes=[
            pltpu.VMEM((2 * vocab, seqs), jnp.float32),
            pltpu.VMEM((2 * vocab, seqs), jnp.float32),
        ],
        compiler_params=pltpu.CompilerParams(vmem_limit_bytes=VMEM_LIMIT),
        name="mixture",
    )(hidden, policy_own, policy_other, reference_own, reference_other, weight, token)


def shift_kernel(half_ref, own_ref, other_ref, delta_ref, out_ref):
    block = out_ref.shape
    for turn, diff_ref in enumerate((own_ref, other_ref)):

        @pl.when(pl.program_id(0) == turn)
        def _(turn=turn, diff_ref=diff_ref):
            shifted = diff_ref[...] + delta_ref[turn : turn + 1, :]
            out_ref[...] = shifted.T.reshape(block)


def shift(half, diff_own, diff_other, delta, shards):
    vocab, seqs = diff_own.shape
    part = seqs // shards
    chunk = 128
    per = chunk // part
    return pl.pallas_call(
        shift_kernel,
        grid_spec=pltpu.PrefetchScalarGridSpec(
            num_scalar_prefetch=1,
            grid=(2, seqs // chunk),
            in_specs=[
                pl.BlockSpec((vocab, chunk), lambda t, j, half: (0, jnp.where(t == 0, j, seqs // chunk - 1))),
                pl.BlockSpec((vocab, chunk), lambda t, j, half: (0, jnp.where(t == 0, 0, j))),
                pl.BlockSpec((2, chunk), lambda t, j, half: (0, j)),
            ],
            out_specs=pl.BlockSpec((per, 1, part, vocab), lambda t, j, half: (j, half[0] ^ t, 0, 0)),
        ),
        out_shape=jax.ShapeDtypeStruct((shards, 2, part, vocab), jnp.float32),
        compiler_params=pltpu.CompilerParams(vmem_limit_bytes=VMEM_LIMIT),
        name="shift",
    )(half, diff_own, diff_other, delta)


def partners(z, y, x):
    pairs = []
    for source in range(z * 2 * y * x):
        i, rest = divmod(source, 2 * y * x)
        c, rest = divmod(rest, y * x)
        j, k = divmod(rest, x)
        j, k = (j, k ^ 1) if c == 0 else (j ^ 1, k)
        pairs.append((source, ((i * 2 + c) * y + j) * x + k))
    return pairs


def everywhere(block, axes):
    group = lax.axis_size(axes)
    return lax.all_to_all(
        jnp.broadcast_to(block[None], (group,) + block.shape), axes, 0, 0, tiled=True
    )


def local(
    policy_hidden,
    reference_hidden,
    policy_gain,
    reference_gain,
    policy_embedding,
    reference_embedding,
    mixture_weight,
    sampled_tokens,
):
    seq_local = policy_hidden.shape[0]
    part = seq_local // 2
    vocab = policy_embedding.shape[0]
    shards = lax.axis_size(DP)
    copies = lax.axis_size(MP)
    shard = lax.axis_index(DP)
    copy = lax.axis_index(MP)
    core = lax.axis_index("dp_1")
    row = lax.axis_index("mp_0")
    column = lax.axis_index("mp_1")
    half = (row + column) % 2
    other_copy = jnp.where(
        core == 0,
        row * lax.axis_size("mp_1") + (column ^ 1),
        (row ^ 1) * lax.axis_size("mp_1") + column,
    )
    first_own = (shard * copies + copy) * vocab
    first_other = (shard * copies + other_copy) * vocab
    half_arg = half.astype(jnp.int32)[None]
    pairs = partners(lax.axis_size("dp_0"), lax.axis_size("mp_0"), lax.axis_size("mp_1"))

    normed = normalize(
        half_arg, policy_hidden, reference_hidden, policy_gain[None], reference_gain[None]
    )
    normed, policy_send, reference_send = lax.optimization_barrier(
        (normed, policy_embedding, reference_embedding)
    )
    hidden = lax.all_gather(normed, DP, axis=0)
    policy_other = lax.ppermute(policy_send, DP_MP, pairs)
    reference_other = lax.ppermute(reference_send, DP_MP, pairs)

    weights = mixture_weight.reshape(shards, 2, part)
    tokens = sampled_tokens.reshape(shards, 2, part)
    weight = lax.dynamic_index_in_dim(weights, half, 1, False).reshape(1, shards * part)
    token = lax.dynamic_index_in_dim(tokens, half, 1, False).reshape(1, shards * part)
    token = jnp.concatenate([token - first_own, token - first_other])
    diff_own, diff_send, sums = mixture(
        hidden, policy_embedding, policy_other, reference_embedding, reference_other, weight, token
    )
    diff_other = lax.ppermute(diff_send, DP_MP, pairs)

    seqs = shards * part
    sums = jnp.sum(everywhere(sums.reshape(1, 5 * seqs), DP), axis=0).reshape(5, shards, part)
    mine = lax.dynamic_index_in_dim(sums[2:], shard, 1, False)
    block = jnp.concatenate(
        [sums[:2].reshape(1, 2 * seqs), mine.reshape(1, 3 * part), jnp.zeros((1, part), jnp.float32)],
        axis=1,
    )
    blocks = everywhere(block, MP)
    index = jnp.arange(copies, dtype=jnp.int32)
    parity = (index // lax.axis_size("mp_1") + index % lax.axis_size("mp_1")) % 2
    by_half = [
        jnp.sum(jnp.where((parity == k)[:, None, None], blocks, 0.0), axis=0)[0] for k in range(2)
    ]
    totals = jnp.stack([b[: 2 * seqs] for b in by_half]).reshape(2, 2, shards, part)
    side = jnp.stack([b[2 * seqs : 2 * seqs + 3 * part] for b in by_half]).reshape(2, 3, part)
    logs = jnp.log(totals)
    delta = (logs[:, 0] - logs[:, 1]).reshape(2, seqs)
    delta = jnp.where(half == 0, delta, delta[::-1])
    mixture_shift = shift(half_arg, diff_own, diff_other, delta, shards)

    log_mine = lax.dynamic_index_in_dim(logs, shard, 2, False)
    weight_mine = lax.dynamic_index_in_dim(weights, shard, 0, False)
    policy_pick = side[:, 1]
    reference_pick = side[:, 2]
    mixed_pick = (1.0 - weight_mine) * policy_pick + weight_mine * reference_pick
    sampled_logprobs = jnp.stack(
        [
            (policy_pick - log_mine[:, 0]).reshape(seq_local),
            (reference_pick - jnp.log(side[:, 0])).reshape(seq_local),
            (mixed_pick - log_mine[:, 1]).reshape(seq_local),
        ]
    )
    return (mixture_shift.reshape(shards * seq_local, vocab), sampled_logprobs)


def solution(mesh):
    split = Mesh(mesh.devices.reshape(8, 2, 8, 4), ("dp_0", "dp_1", "mp_0", "mp_1"))
    in_specs = (P(DP, None), P(DP, None), P(), P(), P(DP_MP, None), P(DP_MP, None), P(), P())
    out_specs = (P(None, DP_MP), P(None, DP))
    return jax.shard_map(local, mesh=split, in_specs=in_specs, out_specs=out_specs, check_vma=False)
```

time: 206 us -> 132 us (0.64)
  the two profiles are of different devices: /device:TPU:4 before, /device:TPU:1 now
where the time goes in v1:
time: 132 us; the launch traced here: 131 us
  waiting for transfers between devices  70.5 us (53%)
  starting transfers between devices  22.8 us (17%)
  Pallas kernels  15.2 us (12%)
  between operations  14.3 us (11%)
  local copies, waits for them, and re-layouts  7 us (5%)
    ppermute x1, waiting for transfers between devices, local(): reference_other = lax.ppermute(reference_send, DP_MP, pairs)  19.7 us
    ppermute x1, waiting for transfers between devices, local(): policy_other = lax.ppermute(policy_send, DP_MP, pairs)  18.5 us
    all_to_all x2, waiting for transfers between devices, everywhere(): lax.all_to_all(jnp.broadcast_to(block[None], (group,) + block.shape), axe...  16.5 us
    all_gather x1, waiting for transfers between devices, local(): hidden = lax.all_gather(normed, DP, axis=0)  15.8 us
    all_to_all x2, starting transfers between devices, everywhere(): lax.all_to_all(jnp.broadcast_to(block[None], (group,) + block.shape), axe...  13.6 us
    pallas_call x1, Pallas kernels, mixture(): pl.pallas_call(mixture_kernel, grid=(width // depth,), in_specs=[pl.Block...  10.8 us
    ppermute x1, starting transfers between devices, local(): policy_other = lax.ppermute(policy_send, DP_MP, pairs)  4.05 us
    pallas_call x1, Pallas kernels, shift(): pl.pallas_call(shift_kernel, grid_spec=pltpu.PrefetchScalarGridSpec(num_s...  3.41 us
  transfers between devices with their start and end apart: 6, of which 5 were waited for; matrix products, arithmetic and copies ran while one was open for 2% of the time, Pallas kernels for 0%

profile of v1, /device:TPU:1, one launch (start us, length us, event | category | flops | bytes accessed | tf_op | source)
XLA Modules:
  0.0 130.9 jit_solution(15110397003910140803)
XLA Ops:
  7.2 0.9 broadcast_in_dim.48.policy_gain_ref
  8.1 0.7 broadcast_in_dim.49.reference_gain_ref
  8.8 1.0 copy-done.1
  9.8 1.0 copy-done.2
  10.9 1.0 normalize.1
  11.9 4.0 %collective-permute-start = (bf16[256,3584]{1,0:T(8,128)(2,1)S(1)}, bf16[256,3584]{1,0:T(8,128)(2,1)}, u32[]{:S(2)}, u32[]{:S(2)}) collective-permute-start(bf16[256,3584]{1,0:T(8,128)(2,1)S(1)} %copy-done), channel_id=1, source_target_pairs={{0,1},{1,0},{2,3},{3,2},{4,5},{5,4},{6,7},{7,6},{8,9},{9,8},{10,11... | collective-permute-start | bytes 5505032 | tf_op jit(solution)/shard_map/ppermute | solution.py:237
  15.9 1.9 %collective-permute-start.1 = (bf16[256,3584]{1,0:T(8,128)(2,1)}, bf16[256,3584]{1,0:T(8,128)(2,1)}, u32[]{:S(2)}, u32[]{:S(2)}) collective-permute-start(bf16[256,3584]{1,0:T(8,128)(2,1)} %reference_own_ref.1), channel_id=1, source_target_pairs={{0,1},{1,0},{2,3},{3,2},{4,5},{5,4},{6,7},{7,6},{8,9},{9,8},{10,11... | collective-permute-start | bytes 5505032 | tf_op jit(solution)/shard_map/ppermute | solution.py:238
  18.4 18.5 %collective-permute-done.policy_other_ref = bf16[256,3584]{1,0:T(8,128)(2,1)} collective-permute-done((bf16[256,3584]{1,0:T(8,128)(2,1)S(1)}, bf16[256,3584]{1,0:T(8,128)(2,1)}, u32[]{:S(2)}, u32[]{:S(2)}) %collective-permute-start) | collective-permute-done | bytes 1835040 | tf_op jit(solution)/shard_map/ppermute | solution.py:237
  36.9 19.7 %collective-permute-done.1.reference_other_ref = bf16[256,3584]{1,0:T(8,128)(2,1)} collective-permute-done((bf16[256,3584]{1,0:T(8,128)(2,1)}, bf16[256,3584]{1,0:T(8,128)(2,1)}, u32[]{:S(2)}, u32[]{:S(2)}) %collective-permute-start.1) | collective-permute-done | bytes 1835040 | tf_op jit(solution)/shard_map/ppermute | solution.py:238
  56.6 15.8 %all-gather.3.cloned.1.call-done = bf16[32,32,3584]{2,1,0:T(8,128)(2,1)} async-done(((bf16[2,32,3584]{2,1,0:T(8,128)(2,1)}), bf16[32,32,3584]{2,1,0:T(8,128)(2,1)}) %all-gather.3.cloned.1.call-update) | async-done | bytes 7340048 | tf_op jit(solution)/shard_map/all_gather | solution.py:236
  72.3 10.8 %mixture.1 = (f32[256,512]{1,0:T(8,128)S(1)}, f32[256,512]{1,0:T(8,128)S(1)}, f32[5,512]{1,0:T(8,128)S(1)}) custom-call(bf16[16,2,32,3584]{3,2,1,0:T(8,128)(2,1)} %bitcast.6, bf16[256,3584]{1,0:T(8,128)(2,1)S(1)} %copy-done, bf16[256,3584]{1,0:T(8,128)(2,1)} %collective-permute-done.policy_other_ref, bf16[256,3584]{1,0:T(8,128)(2,1)} %reference_own_ref.1, ...), custom_call_target="tpu_custom_call" | custom-call | tf_op jit(solution)/shard_map/mixture/pallas_call | solution.py:121
  83.2 0.8 broadcast_in_dim.52
  84.0 4.4 %all-to-all-start = ((f32[16,1,2560]{2,1,0:T(1,128)}), f32[16,1,2560]{2,1,0:T(1,128)S(1)}, u32[]{:S(2)}, u32[]{:S(2)}) async-start(f32[16,1,2560]{2,1,0:T(1,128)} %broadcast_in_dim.52), calls=%async_computation | async-start | bytes 327680 | tf_op jit(solution)/shard_map/all_to_all | solution.py:194
  88.3 9.7 %all-to-all-done = f32[16,1,2560]{2,1,0:T(1,128)S(1)} async-done(((f32[16,1,2560]{2,1,0:T(1,128)}), f32[16,1,2560]{2,1,0:T(1,128)S(1)}, u32[]{:S(2)}, u32[]{:S(2)}) %all-to-all-start) | async-done | bytes 163872 | tf_op jit(solution)/shard_map/all_to_all | solution.py:194
  98.0 0.1 reduce_sum.33
  98.3 0.1 concatenate.9
  98.5 0.7 broadcast_in_dim.55
  99.2 9.3 %all-to-all-start.1 = ((f32[32,1,1152]{2,1,0:T(1,128)}), f32[32,1,1152]{2,1,0:T(1,128)S(1)}, u32[]{:S(2)}, u32[]{:S(2)}) async-start(f32[32,1,1152]{2,1,0:T(1,128)} %broadcast_in_dim.55), calls=%async_computation.1 | async-start | bytes 294912 | tf_op jit(solution)/shard_map/all_to_all | solution.py:194
  108.6 3.1 %collective-permute-start.2 = (f32[256,512]{1,0:T(8,128)S(1)}, f32[256,512]{1,0:T(8,128)S(1)}, u32[]{:S(2)}, u32[]{:S(2)}) collective-permute-start(f32[256,512]{1,0:T(8,128)S(1)} %get-tuple-element.12), channel_id=1, source_target_pairs={{0,1},{1,0},{2,3},{3,2},{4,5},{5,4},{6,7},{7,6},{8,9},{9,8},{10,11... | collective-permute-start | bytes 1572872 | tf_op jit(solution)/shard_map/ppermute | solution.py:248
  111.7 6.9 %all-to-all-done.1 = f32[32,1,1152]{2,1,0:T(1,128)S(1)} async-done(((f32[32,1,1152]{2,1,0:T(1,128)}), f32[32,1,1152]{2,1,0:T(1,128)S(1)}, u32[]{:S(2)}, u32[]{:S(2)}) %all-to-all-start.1) | async-done | bytes 147488 | tf_op jit(solution)/shard_map/all_to_all | solution.py:194
  118.6 0.3 fusion
  120.0 0.1 rev.3
  120.1 0.6 pad_maximum_fusion
  120.7 3.4 %shift.1 = f32[16,2,32,256]{3,2,1,0:T(8,128)} custom-call(s32[1]{0:T(128)} %bitcast.half_ref, f32[256,512]{1,0:T(8,128)S(1)} %get-tuple-element.11.own_ref, f32[256,512]{1,0:T(8,128)S(1)} %collective-permute-done.2.other_ref, f32[2,512]{1,0:T(2,128)S(1)} %broadcast_select_fusion.2.delta_ref), custom_call_target="tpu_custom_call" | custom-call | tf_op jit(solution)/shard_map/shift/pallas_call | solution.py:163
  (56 shorter events, 1.9 us)
Async XLA Ops:
  7.2 4.7 %copy-start = (bf16[256,3584]{1,0:T(8,128)(2,1)S(1)}, bf16[256,3584]{1,0:T(8,128)(2,1)}, u32[]{:S(2)}) copy-start(bf16[256,3584]{1,0:T(8,128)(2,1)} %policy_own_ref.1) | copy-start | bytes 5505028
  7.2 65.2 %all-gather.3.cloned.1.call-start = ((), (), s32[]{:S(2)}) async-start(), calls=%async_computation.2 | async-start | bytes 7798784 | tf_op jit(solution)/shard_map/all_gather | solution.py:236
  8.8 1.0 copy-start.1
  9.8 1.0 copy-start.2
  10.9 7.0 %copy-start.3 = (f32[1024]{0:T(1024)S(1)}, f32[1024]{0:T(1024)}, u32[]{:S(2)}) copy-start(f32[1024]{0:T(1024)} %param.14) | copy-start | bytes 12292
  10.9 7.3 %copy-start.4 = (s32[1024]{0:T(1024)S(1)}, s32[1024]{0:T(1024)}, u32[]{:S(2)}) copy-start(s32[1024]{0:T(1024)} %param.15) | copy-start | bytes 12292
  11.9 25.0 %collective-permute-start = (bf16[256,3584]{1,0:T(8,128)(2,1)S(1)}, bf16[256,3584]{1,0:T(8,128)(2,1)}, u32[]{:S(2)}, u32[]{:S(2)}) collective-permute-start(bf16[256,3584]{1,0:T(8,128)(2,1)S(1)} %copy-done), channel_id=1, source_target_pairs={{0,1},{1,0},{2,3},{3,2},{4,5},{5,4},{6,7},{7,6},{8,9},{9,8},{10,11... | collective-permute-start | bytes 5505032 | tf_op jit(solution)/shard_map/ppermute | solution.py:237
  15.9 40.6 %collective-permute-start.1 = (bf16[256,3584]{1,0:T(8,128)(2,1)}, bf16[256,3584]{1,0:T(8,128)(2,1)}, u32[]{:S(2)}, u32[]{:S(2)}) collective-permute-start(bf16[256,3584]{1,0:T(8,128)(2,1)} %reference_own_ref.1), channel_id=1, source_target_pairs={{0,1},{1,0},{2,3},{3,2},{4,5},{5,4},{6,7},{7,6},{8,9},{9,8},{10,11... | collective-permute-start | bytes 5505032 | tf_op jit(solution)/shard_map/ppermute | solution.py:238
  84.0 14.0 %all-to-all-start = ((f32[16,1,2560]{2,1,0:T(1,128)}), f32[16,1,2560]{2,1,0:T(1,128)S(1)}, u32[]{:S(2)}, u32[]{:S(2)}) async-start(f32[16,1,2560]{2,1,0:T(1,128)} %broadcast_in_dim.52), calls=%async_computation | async-start | bytes 327680 | tf_op jit(solution)/shard_map/all_to_all | solution.py:194
  99.2 19.4 %all-to-all-start.1 = ((f32[32,1,1152]{2,1,0:T(1,128)}), f32[32,1,1152]{2,1,0:T(1,128)S(1)}, u32[]{:S(2)}, u32[]{:S(2)}) async-start(f32[32,1,1152]{2,1,0:T(1,128)} %broadcast_in_dim.55), calls=%async_computation.1 | async-start | bytes 294912 | tf_op jit(solution)/shard_map/all_to_all | solution.py:194
  108.6 12.1 %collective-permute-start.2 = (f32[256,512]{1,0:T(8,128)S(1)}, f32[256,512]{1,0:T(8,128)S(1)}, u32[]{:S(2)}, u32[]{:S(2)}) collective-permute-start(f32[256,512]{1,0:T(8,128)S(1)} %get-tuple-element.12), channel_id=1, source_target_pairs={{0,1},{1,0},{2,3},{3,2},{4,5},{5,4},{6,7},{7,6},{8,9},{9,8},{10,11... | collective-permute-start | bytes 1572872 | tf_op jit(solution)/shard_map/ppermute | solution.py:248
Sparse Core Ops, SparseCore 0:
  12.0 60.2 all-gather.2

commit v2 on v0

v2 whole, which is shorter than its diff:
```python
import functools

import jax
import jax.numpy as jnp
from jax import lax
from jax.experimental import pallas as pl
from jax.experimental.pallas import tpu as pltpu
from jax.sharding import Mesh
from jax.sharding import PartitionSpec as P

DP = ("dp_0", "dp_1")
MP = ("mp_0", "mp_1")
DP_MP = ("dp_0", "dp_1", "mp_0", "mp_1")

softcap = 30.0
epsilon = 1e-06

MIB = 1024 * 1024
HBM = pl.BlockSpec(memory_space=pltpu.HBM)
VMEM = pl.BlockSpec(memory_space=pltpu.VMEM)


def in_hbm(x):
    return pltpu.with_memory_space_constraint(x, pltpu.HBM)


def normalize_kernel(half_ref, policy_ref, reference_ref, policy_gain_ref, reference_gain_ref, out_ref, rows, in_sem):
    part = out_ref.shape[1]
    first = pl.multiple_of(half_ref[0] * part, part)
    models = ((policy_ref, policy_gain_ref), (reference_ref, reference_gain_ref))
    loads = [
        pltpu.make_async_copy(hidden_ref.at[pl.ds(first, part), :], rows.at[model], in_sem.at[model])
        for model, (hidden_ref, _) in enumerate(models)
    ]
    for load in loads:
        load.start()
    for model, (_, gain_ref) in enumerate(models):
        loads[model].wait()
        values = rows[model].astype(jnp.float32)
        meansq = jnp.mean(values * values, axis=-1, keepdims=True)
        gain = gain_ref[...].reshape(1, values.shape[1])
        normed = values * lax.rsqrt(meansq + epsilon) * gain
        out_ref[model] = normed.astype(jnp.bfloat16)


def normalize(half, policy_hidden, reference_hidden, policy_gain, reference_gain):
    rows, width = policy_hidden.shape
    part = rows // 2
    return pl.pallas_call(
        normalize_kernel,
        in_specs=[pl.BlockSpec(memory_space=pltpu.SMEM)] + [HBM] * 2 + [VMEM] * 2,
        out_specs=VMEM,
        out_shape=jax.ShapeDtypeStruct((2, part, width), jnp.bfloat16),
        scratch_shapes=[pltpu.VMEM((2, part, width), jnp.bfloat16), pltpu.SemaphoreType.DMA((2,))],
        compiler_params=pltpu.CompilerParams(vmem_limit_bytes=16 * MIB),
        name="normalize",
    )(half, in_hbm(policy_hidden), in_hbm(reference_hidden), in_hbm(policy_gain), in_hbm(reference_gain))


def stage_kernel(policy_own, policy_other, reference_own, reference_other, out_ref, sem):
    copies = [
        pltpu.make_async_copy(rows_ref, out_ref.at[place], sem.at[place])
        for place, rows_ref in enumerate((policy_own, policy_other, reference_own, reference_other))
    ]
    for copy in copies:
        copy.start()
    for copy in copies:
        copy.wait()


def stage(*embeddings):
    return pl.pallas_call(
        stage_kernel,
        in_specs=[HBM] * 4,
        out_specs=VMEM,
        out_shape=pltpu.VMEM((4,) + embeddings[0].shape, jnp.bfloat16),
        scratch_shapes=[pltpu.SemaphoreType.DMA((4,))],
        compiler_params=pltpu.CompilerParams(vmem_limit_bytes=16 * MIB),
        name="stage",
    )(*map(in_hbm, embeddings))


def mixture_kernel(
    hidden_ref,
    rows_ref,
    weight_ref,
    token_ref,
    diff_own_ref,
    diff_other_ref,
    block_ref,
    hidden,
    policy_acc,
    reference_acc,
    partial,
    sem,
):
    chunks = sem.shape[0]
    shards, _, part, width = hidden_ref.shape
    depth = width // chunks
    vocab = rows_ref.shape[1]
    seqs = shards * part

    def load(k):
        columns = pl.ds(k * depth, depth)
        return pltpu.make_async_copy(
            hidden_ref.at[:, :, :, columns], hidden.at[:, :, :, columns], sem.at[k]
        )

    for k in range(chunks):
        load(k).start()
    for k in range(chunks):
        load(k).wait()
        columns = pl.ds(k * depth, depth)
        for model, acc in enumerate((policy_acc, reference_acc)):
            left = hidden[:, model, :, columns].reshape(seqs, depth)
            for place in range(2):
                product = lax.dot_general(
                    left,
                    rows_ref[2 * model + place, :, columns],
                    (((1,), (1,)), ((), ())),
                    preferred_element_type=jnp.float32,
                )
                target = pl.ds(place * vocab, vocab)
                acc[:, target] = product if k == 0 else acc[:, target] + product

    def body(i, carry):
        rows = pl.ds(pl.multiple_of(i * 8, 8), 8)
        weight = weight_ref[rows, :]
        keep = 1.0 - weight
        sums = [jnp.zeros((8, 128), jnp.float32) for _ in range(5)]
        for place, diff_ref in enumerate((diff_own_ref, diff_other_ref)):
            token = token_ref[place, rows, :]
            for group in range(vocab // 128):
                lanes = pl.ds(place * vocab + group * 128, 128)
                policy = softcap * jnp.tanh(policy_acc[rows, lanes] * (1.0 / softcap))
                reference = softcap * jnp.tanh(reference_acc[rows, lanes] * (1.0 / softcap))
                mixed = keep * policy + weight * reference
                diff_ref[rows, pl.ds(group * 128, 128)] = mixed - policy
                hit = lax.broadcasted_iota(jnp.int32, (8, 128), 1) + group * 128 == token
                terms = (
                    jnp.exp(policy),
                    jnp.exp(mixed),
                    jnp.exp(reference),
                    jnp.where(hit, policy, 0.0),
                    jnp.where(hit, reference, 0.0),
                )
                sums = [total + term for total, term in zip(sums, terms)]
        for k in range(5):
            partial[k, rows, :] = sums[k]
        return carry

    lax.fori_loop(0, seqs // 8, body, 0, unroll=2)
    sums = [jnp.sum(partial[k].T, axis=0, keepdims=True) for k in range(5)]
    whole = jnp.concatenate(sums[:2], axis=1)
    for shard in range(shards):
        start = shard * part // 128 * 128
        block_ref[shard] = jnp.concatenate(
            [whole] + [total[:, start : start + 128] for total in sums[2:]], axis=1
        )


def mixture(hidden, rows, weight, token):
    shards, _, part, width = hidden.shape
    vocab = rows.shape[1]
    seqs = shards * part
    chunks = 7
    return pl.pallas_call(
        mixture_kernel,
        in_specs=[HBM] + [VMEM] * 3,
        out_specs=[VMEM] * 3,
        out_shape=[
            jax.ShapeDtypeStruct((seqs, vocab), jnp.float32),
            jax.ShapeDtypeStruct((seqs, vocab), jnp.float32),
            jax.ShapeDtypeStruct((shards, 1, 2 * seqs + 3 * 128), jnp.float32),
        ],
        scratch_shapes=[
            pltpu.VMEM((shards, 2, part, width), jnp.bfloat16),
            pltpu.VMEM((seqs, 2 * vocab), jnp.float32),
            pltpu.VMEM((seqs, 2 * vocab), jnp.float32),
            pltpu.VMEM((5, seqs, 128), jnp.float32),
            pltpu.SemaphoreType.DMA((chunks,)),
        ],
        compiler_params=pltpu.CompilerParams(vmem_limit_bytes=32 * MIB),
        name="mixture",
    )(in_hbm(hidden), pltpu.with_memory_space_constraint(rows, pltpu.VMEM), weight, token)


def finish_kernel(columns, place_ref, own_ref, other_ref, blocks_ref, weight_ref, shift_ref, sampled_ref, staged, sem):
    shards, _, part, vocab = shift_ref.shape
    seqs = shards * part
    half = place_ref[0]
    shard = place_ref[1]

    totals = [None, None]
    for j in range(blocks_ref.shape[0]):
        k = (j // columns + j % columns) % 2
        totals[k] = blocks_ref[j] if totals[k] is None else totals[k] + blocks_ref[j]
    logs = [jnp.log(total[:, : 2 * seqs + 128]) for total in totals]
    deltas = [log[:, :seqs] - log[:, seqs : 2 * seqs] for log in logs]
    own_first = half == 0
    turns = (
        jnp.where(own_first, deltas[0], deltas[1]),
        jnp.where(own_first, deltas[1], deltas[0]),
    )

    chunk = 128
    per = chunk // part
    stores = []
    for turn, diff_ref in enumerate((own_ref, other_ref)):
        target = half if turn == 0 else 1 - half
        for j in range(seqs // chunk):
            delta = jnp.broadcast_to(turns[turn][:, j * chunk : (j + 1) * chunk], (chunk, chunk)).T
            shards_here = pl.ds(j * per, per)
            for group in range(vocab // 128):
                lanes = pl.ds(group * 128, 128)
                shifted = diff_ref[pl.ds(j * chunk, chunk), lanes] + delta
                staged[turn, shards_here, :, lanes] = shifted.reshape(per, part, 128)
            store = pltpu.make_async_copy(
                staged.at[turn, shards_here],
                shift_ref.at[shards_here, target],
                sem.at[turn, j],
            )
            store.start()
            stores.append(store)

    mine = shard * part // 128
    picked = []
    for total, log in zip(totals, logs):
        policy = jnp.zeros((1, 128), jnp.float32)
        mixed = jnp.zeros((1, 128), jnp.float32)
        for j in range(seqs // 128):
            policy = jnp.where(mine == j, log[:, j * 128 : (j + 1) * 128], policy)
            mixed = jnp.where(mine == j, log[:, seqs + j * 128 : seqs + (j + 1) * 128], mixed)
        policy_pick = total[:, 2 * seqs + 128 : 2 * seqs + 256]
        reference_pick = total[:, 2 * seqs + 256 : 2 * seqs + 384]
        picked.append((policy_pick, reference_pick, policy, log[:, 2 * seqs :], mixed))
    lane = lax.broadcasted_iota(jnp.int32, (8, 128), 1)
    start = shard * part % 128
    values = []
    for low, high in zip(*picked):
        low = pltpu.roll(jnp.broadcast_to(low, (8, 128)), lax.rem(128 - start, 128), 1)
        high = pltpu.roll(jnp.broadcast_to(high, (8, 128)), lax.rem(128 + part - start, 128), 1)
        values.append(jnp.where(lane < part, low, high)[:1, : 2 * part])
    policy_pick, reference_pick, policy_log, reference_log, mixed_log = values
    weight = weight_ref[...]
    sampled_ref[0:1, :] = policy_pick - policy_log
    sampled_ref[1:2, :] = reference_pick - reference_log
    sampled_ref[2:3, :] = (1.0 - weight) * policy_pick + weight * reference_pick - mixed_log

    for store in stores:
        store.wait()


def finish(place, columns, diff_own, diff_other, blocks, weight, shards):
    seqs, vocab = diff_own.shape
    part = seqs // shards
    return pl.pallas_call(
        functools.partial(finish_kernel, columns),
        in_specs=[pl.BlockSpec(memory_space=pltpu.SMEM)] + [VMEM] * 4,
        out_specs=[HBM, VMEM],
        out_shape=[
            jax.ShapeDtypeStruct((shards, 2, part, vocab), jnp.float32),
            jax.ShapeDtypeStruct((3, 2 * part), jnp.float32),
        ],
        scratch_shapes=[
            pltpu.VMEM((2, shards, part, vocab), jnp.float32),
            pltpu.SemaphoreType.DMA((2, seqs // 128)),
        ],
        compiler_params=pltpu.CompilerParams(vmem_limit_bytes=16 * MIB),
        name="finish",
    )(place, diff_own, diff_other, blocks, weight)


def partners(z, y, x):
    pairs = []
    for source in range(z * 2 * y * x):
        i, rest = divmod(source, 2 * y * x)
        c, rest = divmod(rest, y * x)
        j, k = divmod(rest, x)
        j, k = (j, k ^ 1) if c == 0 else (j ^ 1, k)
        pairs.append((source, ((i * 2 + c) * y + j) * x + k))
    return pairs


def local(
    policy_hidden,
    reference_hidden,
    policy_gain,
    reference_gain,
    policy_embedding,
    reference_embedding,
    mixture_weight,
    sampled_tokens,
):
    seq_local = policy_hidden.shape[0]
    part = seq_local // 2
    vocab = policy_embedding.shape[0]
    shards = lax.axis_size(DP)
    copies = lax.axis_size(MP)
    shard = lax.axis_index(DP)
    copy = lax.axis_index(MP)
    core = lax.axis_index("dp_1")
    row = lax.axis_index("mp_0")
    column = lax.axis_index("mp_1")
    half = (row + column) % 2
    other_copy = jnp.where(
        core == 0,
        row * lax.axis_size("mp_1") + (column ^ 1),
        (row ^ 1) * lax.axis_size("mp_1") + column,
    )
    first_own = (shard * copies + copy) * vocab
    first_other = (shard * copies + other_copy) * vocab
    place = jnp.stack([half, shard]).astype(jnp.int32)
    pairs = partners(lax.axis_size("dp_0"), lax.axis_size("mp_0"), lax.axis_size("mp_1"))

    normed = normalize(place, policy_hidden, reference_hidden, policy_gain, reference_gain)
    normed, policy_send, reference_send = lax.optimization_barrier(
        (normed, policy_embedding, reference_embedding)
    )
    hidden = lax.all_gather(normed, DP, axis=0)
    policy_other = lax.ppermute(policy_send, DP_MP, pairs)
    reference_other = lax.ppermute(reference_send, DP_MP, pairs)

    seqs = shards * part
    weights = mixture_weight.reshape(shards, 2, part)
    tokens = sampled_tokens.reshape(shards, 2, part)
    weight = lax.dynamic_index_in_dim(weights, half, 1, False).reshape(seqs, 1)
    token = lax.dynamic_index_in_dim(tokens, half, 1, False).reshape(seqs, 1)
    token = jnp.stack([token - first_own, token - first_other])
    weight = jnp.broadcast_to(weight, (seqs, 128))
    token = jnp.broadcast_to(token, (2, seqs, 128))
    weight_mine = lax.dynamic_slice_in_dim(mixture_weight, shard * seq_local, seq_local)[None]
    policy_other, reference_other, weight, token = lax.optimization_barrier(
        (policy_other, reference_other, weight, token)
    )
    rows = stage(policy_embedding, policy_other, reference_embedding, reference_other)
    diff_own, diff_send, block = mixture(hidden, rows, weight, token)
    diff_other = lax.ppermute(diff_send, DP_MP, pairs)

    block = jnp.sum(lax.all_to_all(block, DP, 0, 0, tiled=True), axis=0, keepdims=True)
    block = jnp.broadcast_to(block, (copies,) + block.shape[1:])
    blocks = lax.all_to_all(block, MP, 0, 0, tiled=True)
    mixture_shift, sampled_logprobs = finish(
        place, lax.axis_size("mp_1"), diff_own, diff_other, blocks, weight_mine, shards
    )
    return (mixture_shift.reshape(shards * seq_local, vocab), sampled_logprobs)


def solution(mesh):
    split = Mesh(mesh.devices.reshape(8, 2, 8, 4), ("dp_0", "dp_1", "mp_0", "mp_1"))
    in_specs = (P(DP, None), P(DP, None), P(), P(), P(DP_MP, None), P(DP_MP, None), P(), P())
    out_specs = (P(None, DP_MP), P(None, DP))
    return jax.shard_map(local, mesh=split, in_specs=in_specs, out_specs=out_specs, check_vma=False)
```

time: 206 us -> 127 us (0.62)
  the two profiles are of different devices: /device:TPU:4 before, /device:TPU:1 now
where the time goes in v2:
time: 127 us
  waiting for transfers between devices  58 us (46%)
  starting transfers between devices  18.1 us (14%)
  Pallas kernels  15.9 us (13%)
  between operations  14.3 us (11%)
  blocking collectives  12.8 us (10%)
  local copies, waits for them, and re-layouts  7.69 us (6%)
    ppermute x1, waiting for transfers between devices, local(): reference_other = lax.ppermute(reference_send, DP_MP, pairs)  19.7 us
    ppermute x1, waiting for transfers between devices, local(): policy_other = lax.ppermute(policy_send, DP_MP, pairs)  18.5 us
    all_to_all x1, blocking collectives, local(): lax.all_to_all(block, DP, 0, 0, tiled=True)  12.8 us
    all_to_all x1, waiting for transfers between devices, local(): blocks = lax.all_to_all(block, MP, 0, 0, tiled=True)  10.4 us
    all_gather x1, waiting for transfers between devices, local(): hidden = lax.all_gather(normed, DP, axis=0)  9.41 us
    all_to_all x1, starting transfers between devices, local(): blocks = lax.all_to_all(block, MP, 0, 0, tiled=True)  8.97 us
    pallas_call x1, Pallas kernels, mixture(): pl.pallas_call(mixture_kernel, in_specs=[HBM] + [VMEM] * 3, out_specs=[VM...  7.43 us
    unnamed x10, local copies, waits for them, and re-layouts  6.11 us
  transfers between devices with their start and end apart: 5, of which 4 were waited for; matrix products, arithmetic and copies ran while one was open for 1% of the time, Pallas kernels for 3%

profile of v2, /device:TPU:1, one launch (start us, length us, event | category | flops | bytes accessed | tf_op | source)
XLA Modules:
  0.0 126.9 jit_solution(11073804361553735614)
XLA Ops:
  7.3 2.9 %normalize.1 = bf16[2,32,3584]{2,1,0:T(8,128)(2,1)} custom-call(s32[2]{0:T(128)S(1)} %pad_add_fusion.half_ref.place_ref, bf16[64,3584]{1,0:T(8,128)(2,1)} %policy_ref.1, bf16[64,3584]{1,0:T(8,128)(2,1)} %reference_ref.1, f32[3584]{0:T(1024)} %policy_gain_ref.1, f32[3584]{0:T(1024)} %reference_gain_ref.1), custom_call_target="tpu_custom_call" | custom-call | tf_op jit(solution)/shard_map/normalize/pallas_call | solution.py:49
  10.3 4.0 %collective-permute-start = (bf16[256,3584]{1,0:T(8,128)(2,1)S(1)}, bf16[256,3584]{1,0:T(8,128)(2,1)}, u32[]{:S(2)}, u32[]{:S(2)}) collective-permute-start(bf16[256,3584]{1,0:T(8,128)(2,1)S(1)} %copy-done.2), channel_id=1, source_target_pairs={{0,1},{1,0},{2,3},{3,2},{4,5},{5,4},{6,7},{7,6},{8,9},{9,8},{10,11... | collective-permute-start | bytes 5505032 | tf_op jit(solution)/shard_map/ppermute | solution.py:321
  14.3 1.9 %collective-permute-start.1 = (bf16[256,3584]{1,0:T(8,128)(2,1)}, bf16[256,3584]{1,0:T(8,128)(2,1)}, u32[]{:S(2)}, u32[]{:S(2)}) collective-permute-start(bf16[256,3584]{1,0:T(8,128)(2,1)} %reference_own.1), channel_id=1, source_target_pairs={{0,1},{1,0},{2,3},{3,2},{4,5},{5,4},{6,7},{7,6},{8,9},{9,8},{10,11... | collective-permute-start | bytes 5505032 | tf_op jit(solution)/shard_map/ppermute | solution.py:322
  16.3 0.1 reshape.54
  16.4 0.1 sub.38
  16.5 0.1 sub.41
  16.6 0.1 reshape.53
  16.7 0.1 broadcast_in_dim.23
  16.8 18.5 %collective-permute-done.policy_other = bf16[256,3584]{1,0:T(8,128)(2,1)} collective-permute-done((bf16[256,3584]{1,0:T(8,128)(2,1)S(1)}, bf16[256,3584]{1,0:T(8,128)(2,1)}, u32[]{:S(2)}, u32[]{:S(2)}) %collective-permute-start) | collective-permute-done | bytes 1835040 | tf_op jit(solution)/shard_map/ppermute | solution.py:321
  35.3 19.7 %collective-permute-done.1.reference_other = bf16[256,3584]{1,0:T(8,128)(2,1)} collective-permute-done((bf16[256,3584]{1,0:T(8,128)(2,1)}, bf16[256,3584]{1,0:T(8,128)(2,1)}, u32[]{:S(2)}, u32[]{:S(2)}) %collective-permute-start.1) | collective-permute-done | bytes 1835040 | tf_op jit(solution)/shard_map/ppermute | solution.py:322
  55.0 0.2 broadcast_in_dim.26.token_ref
  55.2 0.1 broadcast_in_dim.24.weight_ref
  55.3 3.3 %stage.1.rows_ref = bf16[4,256,3584]{2,1,0:T(8,128)(2,1)S(1)} custom-call(bf16[256,3584]{1,0:T(8,128)(2,1)} %policy_own.1, bf16[256,3584]{1,0:T(8,128)(2,1)} %collective-permute-done.policy_other, bf16[256,3584]{1,0:T(8,128)(2,1)} %reference_own.1, bf16[256,3584]{1,0:T(8,128)(2,1)} %collective-permute-done.1.reference_other), custom_call_target="tpu_custom_call" | custom-call | tf_op jit(solution)/shard_map/stage/pallas_call | solution.py:72
  58.7 3.0 %copy-done = bf16[4,256,3584]{2,1,0:T(8,128)(2,1)} copy-done((bf16[4,256,3584]{2,1,0:T(8,128)(2,1)}, bf16[4,256,3584]{2,1,0:T(8,128)(2,1)S(1)}, u32[]{:S(2)}) %copy-start) | copy-done | bytes 7340056
  61.7 9.4 %all-gather.3.cloned.1.call-done = bf16[32,32,3584]{2,1,0:T(8,128)(2,1)} async-done(((bf16[2,32,3584]{2,1,0:T(8,128)(2,1)}), bf16[32,32,3584]{2,1,0:T(8,128)(2,1)}) %all-gather.3.cloned.1.call-update) | async-done | bytes 7340048 | tf_op jit(solution)/shard_map/all_gather | solution.py:320
  71.1 3.1 %copy-done.1 = bf16[4,256,3584]{2,1,0:T(8,128)(2,1)S(1)} copy-done((bf16[4,256,3584]{2,1,0:T(8,128)(2,1)S(1)}, bf16[4,256,3584]{2,1,0:T(8,128)(2,1)}, u32[]{:S(2)}) %copy-start.1) | copy-done | bytes 7340056
  74.2 7.4 %mixture.1 = (f32[512,256]{1,0:T(8,128)S(1)}, f32[512,256]{1,0:T(8,128)S(1)}, f32[16,1,1408]{2,1,0:T(1,128)S(1)}) custom-call(bf16[16,2,32,3584]{3,2,1,0:T(8,128)(2,1)} %bitcast.10, bf16[4,256,3584]{2,1,0:T(8,128)(2,1)S(1)} %copy-done.1, f32[512,128]{1,0:T(8,128)S(1)} %broadcast_in_dim.24.weight_ref, s32[2,512,128]{2,1,0:T(8,128)S(1)} %broadcast_in_dim.26.token_ref), custom_call_target="tpu_custom_call" | custom-call | tf_op jit(solution)/shard_map/mixture/pallas_call | solution.py:167
  81.6 3.1 %collective-permute-start.2 = (f32[512,256]{1,0:T(8,128)S(1)}, f32[512,256]{1,0:T(8,128)S(1)}, u32[]{:S(2)}, u32[]{:S(2)}) collective-permute-start(f32[512,256]{1,0:T(8,128)S(1)} %get-tuple-element.22), channel_id=1, source_target_pairs={{0,1},{1,0},{2,3},{3,2},{4,5},{5,4},{6,7},{7,6},{8,9},{9,8},{10,11... | collective-permute-start | bytes 1572872 | tf_op jit(solution)/shard_map/ppermute | solution.py:338
  84.7 12.8 %all_to_all.10 = f32[16,1,1408]{2,1,0:T(1,128)S(1)} all-to-all(f32[16,1,1408]{2,1,0:T(1,128)S(1)} %get-tuple-element.23), channel_id=1, replica_groups=mesh['dp_0'=8,'dp_1'=2,'mp_0'=8,'mp_1'=4] {'dp_0','dp_1'}, dimensions={0} | all-to-all | bytes 180224 | tf_op jit(solution)/shard_map/all_to_all | solution.py:340
  97.5 0.8 broadcast_in_dim.27
  98.3 9.0 %all-to-all-start.1 = ((f32[32,1,1408]{2,1,0:T(1,128)}), f32[32,1,1408]{2,1,0:T(1,128)S(1)}, u32[]{:S(2)}, u32[]{:S(2)}) async-start(f32[32,1,1408]{2,1,0:T(1,128)} %broadcast_in_dim.27), calls=%async_computation.1 | async-start | bytes 360448 | tf_op jit(solution)/shard_map/all_to_all | solution.py:342
  107.3 0.1 dynamic-slice_bitcast_fusion.weight_ref
  107.4 10.4 %all-to-all-done.1.blocks_ref = f32[32,1,1408]{2,1,0:T(1,128)S(1)} async-done(((f32[32,1,1408]{2,1,0:T(1,128)}), f32[32,1,1408]{2,1,0:T(1,128)S(1)}, u32[]{:S(2)}, u32[]{:S(2)}) %all-to-all-start.1) | async-done | bytes 180256 | tf_op jit(solution)/shard_map/all_to_all | solution.py:342
  117.8 2.3 %finish.1 = (f32[16,2,32,256]{3,2,1,0:T(8,128)}, f32[3,64]{1,0:T(4,128)}) custom-call(s32[2]{0:T(128)S(1)} %pad_add_fusion.half_ref.place_ref, f32[512,256]{1,0:T(8,128)S(1)} %get-tuple-element.21.own_ref, f32[512,256]{1,0:T(8,128)S(1)} %collective-permute-done.2.other_ref, f32[32,1,1408]{2,1,0:T(1,128)S(1)} %all-to-all-done.1.blocks_ref, ...), custom_call_target="tpu_custom_call" | custom-call | tf_op jit(solution)/shard_map/finish/pallas_call | solution.py:257
  (16 shorter events, 0.3 us)
Async XLA Ops:
  7.2 3.1 %copy-start.2 = (bf16[256,3584]{1,0:T(8,128)(2,1)S(1)}, bf16[256,3584]{1,0:T(8,128)(2,1)}, u32[]{:S(2)}) copy-start(bf16[256,3584]{1,0:T(8,128)(2,1)} %policy_own.1) | copy-start | bytes 5505028
  7.2 9.1 %copy-start.3 = (s32[1024]{0:T(1024)S(1)}, s32[1024]{0:T(1024)}, u32[]{:S(2)}) copy-start(s32[1024]{0:T(1024)} %param.15) | copy-start | bytes 12292
  7.2 9.4 %copy-start.4 = (f32[1024]{0:T(1024)S(1)}, f32[1024]{0:T(1024)}, u32[]{:S(2)}) copy-start(f32[1024]{0:T(1024)} %param.14) | copy-start | bytes 12292
  7.2 63.9 %all-gather.3.cloned.1.call-start = ((), (), s32[]{:S(2)}) async-start(), calls=%async_computation.2 | async-start | bytes 7798784 | tf_op jit(solution)/shard_map/all_gather | solution.py:320
  10.3 25.0 %collective-permute-start = (bf16[256,3584]{1,0:T(8,128)(2,1)S(1)}, bf16[256,3584]{1,0:T(8,128)(2,1)}, u32[]{:S(2)}, u32[]{:S(2)}) collective-permute-start(bf16[256,3584]{1,0:T(8,128)(2,1)S(1)} %copy-done.2), channel_id=1, source_target_pairs={{0,1},{1,0},{2,3},{3,2},{4,5},{5,4},{6,7},{7,6},{8,9},{9,8},{10,11... | collective-permute-start | bytes 5505032 | tf_op jit(solution)/shard_map/ppermute | solution.py:321
  14.3 40.7 %collective-permute-start.1 = (bf16[256,3584]{1,0:T(8,128)(2,1)}, bf16[256,3584]{1,0:T(8,128)(2,1)}, u32[]{:S(2)}, u32[]{:S(2)}) collective-permute-start(bf16[256,3584]{1,0:T(8,128)(2,1)} %reference_own.1), channel_id=1, source_target_pairs={{0,1},{1,0},{2,3},{3,2},{4,5},{5,4},{6,7},{7,6},{8,9},{9,8},{10,11... | collective-permute-start | bytes 5505032 | tf_op jit(solution)/shard_map/ppermute | solution.py:322
  58.6 3.0 %copy-start = (bf16[4,256,3584]{2,1,0:T(8,128)(2,1)}, bf16[4,256,3584]{2,1,0:T(8,128)(2,1)S(1)}, u32[]{:S(2)}) copy-start(bf16[4,256,3584]{2,1,0:T(8,128)(2,1)S(1)} %stage.1.rows_ref) | copy-start | bytes 22020100
  71.1 3.1 %copy-start.1 = (bf16[4,256,3584]{2,1,0:T(8,128)(2,1)S(1)}, bf16[4,256,3584]{2,1,0:T(8,128)(2,1)}, u32[]{:S(2)}) copy-start(bf16[4,256,3584]{2,1,0:T(8,128)(2,1)} %copy-done) | copy-start | bytes 22020100
  81.6 36.2 %collective-permute-start.2 = (f32[512,256]{1,0:T(8,128)S(1)}, f32[512,256]{1,0:T(8,128)S(1)}, u32[]{:S(2)}, u32[]{:S(2)}) collective-permute-start(f32[512,256]{1,0:T(8,128)S(1)} %get-tuple-element.22), channel_id=1, source_target_pairs={{0,1},{1,0},{2,3},{3,2},{4,5},{5,4},{6,7},{7,6},{8,9},{9,8},{10,11... | collective-permute-start | bytes 1572872 | tf_op jit(solution)/shard_map/ppermute | solution.py:338
  98.3 19.5 %all-to-all-start.1 = ((f32[32,1,1408]{2,1,0:T(1,128)}), f32[32,1,1408]{2,1,0:T(1,128)S(1)}, u32[]{:S(2)}, u32[]{:S(2)}) async-start(f32[32,1,1408]{2,1,0:T(1,128)} %broadcast_in_dim.27), calls=%async_computation.1 | async-start | bytes 360448 | tf_op jit(solution)/shard_map/all_to_all | solution.py:342
Sparse Core Ops, SparseCore 0:
  10.7 60.2 all-gather.2

commit v3 on v2

--- a/solution.py
+++ b/solution.py
@@ -57,38 +57,19 @@
     )(half, in_hbm(policy_hidden), in_hbm(reference_hidden), in_hbm(policy_gain), in_hbm(reference_gain))
 
 
-def stage_kernel(policy_own, policy_other, reference_own, reference_other, out_ref, sem):
-    copies = [
-        pltpu.make_async_copy(rows_ref, out_ref.at[place], sem.at[place])
-        for place, rows_ref in enumerate((policy_own, policy_other, reference_own, reference_other))
-    ]
-    for copy in copies:
-        copy.start()
-    for copy in copies:
-        copy.wait()
-
-
-def stage(*embeddings):
-    return pl.pallas_call(
-        stage_kernel,
-        in_specs=[HBM] * 4,
-        out_specs=VMEM,
-        out_shape=pltpu.VMEM((4,) + embeddings[0].shape, jnp.bfloat16),
-        scratch_shapes=[pltpu.SemaphoreType.DMA((4,))],
-        compiler_params=pltpu.CompilerParams(vmem_limit_bytes=16 * MIB),
-        name="stage",
-    )(*map(in_hbm, embeddings))
-
-
 def mixture_kernel(
     hidden_ref,
-    rows_ref,
+    policy_own_ref,
+    policy_other_ref,
+    reference_own_ref,
+    reference_other_ref,
     weight_ref,
     token_ref,
     diff_own_ref,
     diff_other_ref,
     block_ref,
     hidden,
+    loaded,
     policy_acc,
     reference_acc,
     partial,
@@ -97,28 +78,30 @@
     chunks = sem.shape[0]
     shards, _, part, width = hidden_ref.shape
     depth = width // chunks
-    vocab = rows_ref.shape[1]
+    vocab = policy_own_ref.shape[0]
     seqs = shards * part
 
-    def load(k):
+    def loads(k):
         columns = pl.ds(k * depth, depth)
-        return pltpu.make_async_copy(
-            hidden_ref.at[:, :, :, columns], hidden.at[:, :, :, columns], sem.at[k]
-        )
+        rest = (policy_other_ref, reference_own_ref, reference_other_ref)
+        pairs = [(hidden_ref.at[:, :, :, columns], hidden.at[:, :, :, columns])]
+        pairs += [(ref.at[:, columns], loaded.at[i, :, columns]) for i, ref in enumerate(rest)]
+        return [pltpu.make_async_copy(*pair, sem.at[k, i]) for i, pair in enumerate(pairs)]
 
     for k in range(chunks):
-        load(k).start()
+        for load in loads(k):
+            load.start()
     for k in range(chunks):
-        load(k).wait()
+        for load in loads(k):
+            load.wait()
         columns = pl.ds(k * depth, depth)
         for model, acc in enumerate((policy_acc, reference_acc)):
             left = hidden[:, model, :, columns].reshape(seqs, depth)
             for place in range(2):
+                index = 2 * model + place
+                rows = policy_own_ref[:, columns] if index == 0 else loaded[index - 1, :, columns]
                 product = lax.dot_general(
-                    left,
-                    rows_ref[2 * model + place, :, columns],
-                    (((1,), (1,)), ((), ())),
-                    preferred_element_type=jnp.float32,
+                    left, rows, (((1,), (1,)), ((), ())), preferred_element_type=jnp.float32
                 )
                 target = pl.ds(place * vocab, vocab)
                 acc[:, target] = product if k == 0 else acc[:, target] + product
@@ -159,14 +142,14 @@
         )
 
 
-def mixture(hidden, rows, weight, token):
+def mixture(hidden, policy_own, policy_other, reference_own, reference_other, weight, token):
     shards, _, part, width = hidden.shape
-    vocab = rows.shape[1]
+    vocab = policy_own.shape[0]
     seqs = shards * part
     chunks = 7
     return pl.pallas_call(
         mixture_kernel,
-        in_specs=[HBM] + [VMEM] * 3,
+        in_specs=[HBM, VMEM] + [HBM] * 3 + [VMEM] * 2,
         out_specs=[VMEM] * 3,
         out_shape=[
             jax.ShapeDtypeStruct((seqs, vocab), jnp.float32),
@@ -175,14 +158,23 @@
         ],
         scratch_shapes=[
             pltpu.VMEM((shards, 2, part, width), jnp.bfloat16),
+            pltpu.VMEM((3, vocab, width), jnp.bfloat16),
             pltpu.VMEM((seqs, 2 * vocab), jnp.float32),
             pltpu.VMEM((seqs, 2 * vocab), jnp.float32),
             pltpu.VMEM((5, seqs, 128), jnp.float32),
-            pltpu.SemaphoreType.DMA((chunks,)),
+            pltpu.SemaphoreType.DMA((chunks, 4)),
         ],
         compiler_params=pltpu.CompilerParams(vmem_limit_bytes=32 * MIB),
         name="mixture",
-    )(in_hbm(hidden), pltpu.with_memory_space_constraint(rows, pltpu.VMEM), weight, token)
+    )(
+        in_hbm(hidden),
+        pltpu.with_memory_space_constraint(policy_own, pltpu.VMEM),
+        in_hbm(policy_other),
+        in_hbm(reference_own),
+        in_hbm(reference_other),
+        weight,
+        token,
+    )
 
 
 def finish_kernel(columns, place_ref, own_ref, other_ref, blocks_ref, weight_ref, shift_ref, sampled_ref, staged, sem):
@@ -333,11 +325,14 @@
     policy_other, reference_other, weight, token = lax.optimization_barrier(
         (policy_other, reference_other, weight, token)
     )
-    rows = stage(policy_embedding, policy_other, reference_embedding, reference_other)
-    diff_own, diff_send, block = mixture(hidden, rows, weight, token)
+    diff_own, diff_send, block = mixture(
+        hidden, policy_embedding, policy_other, reference_embedding, reference_other, weight, token
+    )
+
+    block = lax.all_to_all(block, DP, 0, 0, tiled=True)
+    block, diff_send = lax.optimization_barrier((block, diff_send))
     diff_other = lax.ppermute(diff_send, DP_MP, pairs)
-
-    block = jnp.sum(lax.all_to_all(block, DP, 0, 0, tiled=True), axis=0, keepdims=True)
+    block = jnp.sum(block, axis=0, keepdims=True)
     block = jnp.broadcast_to(block, (copies,) + block.shape[1:])
     blocks = lax.all_to_all(block, MP, 0, 0, tiled=True)
     mixture_shift, sampled_logprobs = finish(

time: 127 us -> 124 us (0.976)
  local copies, waits for them, and re-layouts: 7.69 us -> 1.58 us
  waiting for transfers between devices: 58 us -> 63.6 us
  Pallas kernels: 15.9 us -> 13.4 us
    all_gather x1, waiting for transfers between devices: 9.41 us -> 15.8 us  [local(): hidden = lax.all_gather(normed, DP, axis=0)]
    unnamed x10 -> x6, local copies, waits for them, and re-layouts: 6.11 us -> 0.01 us
    pallas_call x2 -> x1, Pallas kernels: 10.8 us -> 8.25 us  [mixture(): pl.pallas_call(mixture_kernel, in_specs=[HBM, VMEM] + [HBM] * 3 + [VMEM]...]
  transfers between devices with their start and end apart: 5 -> 5, of which waited for: 4 -> 4; matrix products, arithmetic and copies ran while one was open for 1% -> 1% of each run, Pallas kernels for 3% -> 0%
where the time goes in v3:
time: 124 us; the launch traced here: 123 us
  waiting for transfers between devices  63.6 us (51%)
  starting transfers between devices  17.5 us (14%)
  between operations  14.2 us (11%)
  Pallas kernels  13.4 us (11%)
  blocking collectives  12.5 us (10%)
  local copies, waits for them, and re-layouts  1.58 us (1%)
    ppermute x1, waiting for transfers between devices, local(): reference_other = lax.ppermute(reference_send, DP_MP, pairs)  19.7 us
    ppermute x1, waiting for transfers between devices, local(): policy_other = lax.ppermute(policy_send, DP_MP, pairs)  18.5 us
    all_gather x1, waiting for transfers between devices, local(): hidden = lax.all_gather(normed, DP, axis=0)  15.8 us
    all_to_all x1, blocking collectives, local(): block = lax.all_to_all(block, DP, 0, 0, tiled=True)  12.5 us
    all_to_all x1, waiting for transfers between devices, local(): blocks = lax.all_to_all(block, MP, 0, 0, tiled=True)  9.67 us
    all_to_all x1, starting transfers between devices, local(): blocks = lax.all_to_all(block, MP, 0, 0, tiled=True)  8.37 us
    pallas_call x1, Pallas kernels, mixture(): pl.pallas_call(mixture_kernel, in_specs=[HBM, VMEM] + [HBM] * 3 + [VMEM]...  8.25 us
    ppermute x1, starting transfers between devices, local(): policy_other = lax.ppermute(policy_send, DP_MP, pairs)  4.04 us
  transfers between devices with their start and end apart: 5, of which 4 were waited for; matrix products, arithmetic and copies ran while one was open for 1% of the time, Pallas kernels for 0%

profile of v3, /device:TPU:1, one launch (start us, length us, event | category | flops | bytes accessed | tf_op | source)
XLA Modules:
  0.0 123.0 jit_solution(7658038297104848825)
XLA Ops:
  7.3 0.1 pad_add_fusion.half_ref.place_ref
  7.3 2.9 %normalize.1 = bf16[2,32,3584]{2,1,0:T(8,128)(2,1)} custom-call(s32[2]{0:T(128)S(1)} %pad_add_fusion.half_ref.place_ref, bf16[64,3584]{1,0:T(8,128)(2,1)} %policy_ref.1, bf16[64,3584]{1,0:T(8,128)(2,1)} %reference_ref.1, f32[3584]{0:T(1024)} %policy_gain_ref.1, f32[3584]{0:T(1024)} %reference_gain_ref.1), custom_call_target="tpu_custom_call" | custom-call | tf_op jit(solution)/shard_map/normalize/pallas_call | solution.py:49
  10.3 4.0 %collective-permute-start = (bf16[256,3584]{1,0:T(8,128)(2,1)S(1)}, bf16[256,3584]{1,0:T(8,128)(2,1)}, u32[]{:S(2)}, u32[]{:S(2)}) collective-permute-start(bf16[256,3584]{1,0:T(8,128)(2,1)S(1)} %copy-done), channel_id=1, source_target_pairs={{0,1},{1,0},{2,3},{3,2},{4,5},{5,4},{6,7},{7,6},{8,9},{9,8},{10,11... | collective-permute-start | bytes 5505032 | tf_op jit(solution)/shard_map/ppermute | solution.py:313
  14.3 1.9 %collective-permute-start.1 = (bf16[256,3584]{1,0:T(8,128)(2,1)}, bf16[256,3584]{1,0:T(8,128)(2,1)}, u32[]{:S(2)}, u32[]{:S(2)}) collective-permute-start(bf16[256,3584]{1,0:T(8,128)(2,1)} %reference_own_ref.1), channel_id=1, source_target_pairs={{0,1},{1,0},{2,3},{3,2},{4,5},{5,4},{6,7},{7,6},{8,9},{9,8},{10,11... | collective-permute-start | bytes 5505032 | tf_op jit(solution)/shard_map/ppermute | solution.py:314
  16.3 0.1 reshape.54
  16.4 0.1 subtract_reduce_fusion.1
  16.4 0.1 sub.38
  16.5 0.1 sub.41
  16.6 0.1 reshape.53
  16.7 0.1 broadcast_in_dim.23
  16.8 18.5 %collective-permute-done.policy_other_ref = bf16[256,3584]{1,0:T(8,128)(2,1)} collective-permute-done((bf16[256,3584]{1,0:T(8,128)(2,1)S(1)}, bf16[256,3584]{1,0:T(8,128)(2,1)}, u32[]{:S(2)}, u32[]{:S(2)}) %collective-permute-start) | collective-permute-done | bytes 1835040 | tf_op jit(solution)/shard_map/ppermute | solution.py:313
  35.3 19.7 %collective-permute-done.1.reference_other_ref = bf16[256,3584]{1,0:T(8,128)(2,1)} collective-permute-done((bf16[256,3584]{1,0:T(8,128)(2,1)}, bf16[256,3584]{1,0:T(8,128)(2,1)}, u32[]{:S(2)}, u32[]{:S(2)}) %collective-permute-start.1) | collective-permute-done | bytes 1835040 | tf_op jit(solution)/shard_map/ppermute | solution.py:314
  55.0 0.1 broadcast_in_dim.24.weight_ref
  55.1 0.2 broadcast_in_dim.26.token_ref
  55.3 15.8 %all-gather.3.cloned.1.call-done = bf16[32,32,3584]{2,1,0:T(8,128)(2,1)} async-done(((bf16[2,32,3584]{2,1,0:T(8,128)(2,1)}), bf16[32,32,3584]{2,1,0:T(8,128)(2,1)}) %all-gather.3.cloned.1.call-update) | async-done | bytes 7340048 | tf_op jit(solution)/shard_map/all_gather | solution.py:312
  71.1 8.2 %mixture.1 = (f32[512,256]{1,0:T(8,128)S(1)}, f32[512,256]{1,0:T(8,128)}, f32[16,1,1408]{2,1,0:T(1,128)S(1)}) custom-call(bf16[16,2,32,3584]{3,2,1,0:T(8,128)(2,1)} %bitcast.10, bf16[256,3584]{1,0:T(8,128)(2,1)S(1)} %copy-done, bf16[256,3584]{1,0:T(8,128)(2,1)} %collective-permute-done.policy_other_ref, bf16[256,3584]{1,0:T(8,128)(2,1)} %reference_own_ref.1, ...), custom_call_target="tpu_custom_call" | custom-call | tf_op jit(solution)/shard_map/mixture/pallas_call | solution.py:150
  79.3 12.5 %all_to_all.10 = f32[16,1,1408]{2,1,0:T(1,128)S(1)} all-to-all(f32[16,1,1408]{2,1,0:T(1,128)S(1)} %get-tuple-element.24), channel_id=1, replica_groups=mesh['dp_0'=8,'dp_1'=2,'mp_0'=8,'mp_1'=4] {'dp_0','dp_1'}, dimensions={0} | all-to-all | bytes 180224 | tf_op jit(solution)/shard_map/all_to_all | solution.py:332
  91.8 3.1 %collective-permute-start.2 = (f32[512,256]{1,0:T(8,128)}, f32[512,256]{1,0:T(8,128)S(1)}, u32[]{:S(2)}, u32[]{:S(2)}) collective-permute-start(f32[512,256]{1,0:T(8,128)} %get-tuple-element.26), channel_id=1, source_target_pairs={{0,1},{1,0},{2,3},{3,2},{4,5},{5,4},{6,7},{7,6},{8,9},{9,8},{10,11... | collective-permute-start | bytes 1572872 | tf_op jit(solution)/shard_map/ppermute | solution.py:334
  94.9 0.1 reduce_sum.9
  95.0 0.8 broadcast_in_dim.27
  95.7 8.4 %all-to-all-start.1 = ((f32[32,1,1408]{2,1,0:T(1,128)}), f32[32,1,1408]{2,1,0:T(1,128)S(1)}, u32[]{:S(2)}, u32[]{:S(2)}) async-start(f32[32,1,1408]{2,1,0:T(1,128)} %broadcast_in_dim.27), calls=%async_computation.1 | async-start | bytes 360448 | tf_op jit(solution)/shard_map/all_to_all | solution.py:337
  104.1 0.1 dynamic-slice_bitcast_fusion.weight_ref
  104.2 9.7 %all-to-all-done.1.blocks_ref = f32[32,1,1408]{2,1,0:T(1,128)S(1)} async-done(((f32[32,1,1408]{2,1,0:T(1,128)}), f32[32,1,1408]{2,1,0:T(1,128)S(1)}, u32[]{:S(2)}, u32[]{:S(2)}) %all-to-all-start.1) | async-done | bytes 180256 | tf_op jit(solution)/shard_map/all_to_all | solution.py:337
  113.9 2.3 %finish.1 = (f32[16,2,32,256]{3,2,1,0:T(8,128)}, f32[3,64]{1,0:T(4,128)}) custom-call(s32[2]{0:T(128)S(1)} %pad_add_fusion.half_ref.place_ref, f32[512,256]{1,0:T(8,128)S(1)} %get-tuple-element.23.own_ref, f32[512,256]{1,0:T(8,128)S(1)} %collective-permute-done.2.other_ref, f32[32,1,1408]{2,1,0:T(1,128)S(1)} %all-to-all-done.1.blocks_ref, ...), custom_call_target="tpu_custom_call" | custom-call | tf_op jit(solution)/shard_map/finish/pallas_call | solution.py:249
  (11 shorter events, 0.1 us)
Async XLA Ops:
  7.2 3.1 %copy-start = (bf16[256,3584]{1,0:T(8,128)(2,1)S(1)}, bf16[256,3584]{1,0:T(8,128)(2,1)}, u32[]{:S(2)}) copy-start(bf16[256,3584]{1,0:T(8,128)(2,1)} %policy_own_ref.1) | copy-start | bytes 5505028
  7.2 9.1 %copy-start.1 = (s32[1024]{0:T(1024)S(1)}, s32[1024]{0:T(1024)}, u32[]{:S(2)}) copy-start(s32[1024]{0:T(1024)} %param.15) | copy-start | bytes 12292
  7.2 9.4 %copy-start.2 = (f32[1024]{0:T(1024)S(1)}, f32[1024]{0:T(1024)}, u32[]{:S(2)}) copy-start(f32[1024]{0:T(1024)} %param.14) | copy-start | bytes 12292
  7.2 63.9 %all-gather.3.cloned.1.call-start = ((), (), s32[]{:S(2)}) async-start(), calls=%async_computation.2 | async-start | bytes 7798784 | tf_op jit(solution)/shard_map/all_gather | solution.py:312
  10.3 25.0 %collective-permute-start = (bf16[256,3584]{1,0:T(8,128)(2,1)S(1)}, bf16[256,3584]{1,0:T(8,128)(2,1)}, u32[]{:S(2)}, u32[]{:S(2)}) collective-permute-start(bf16[256,3584]{1,0:T(8,128)(2,1)S(1)} %copy-done), channel_id=1, source_target_pairs={{0,1},{1,0},{2,3},{3,2},{4,5},{5,4},{6,7},{7,6},{8,9},{9,8},{10,11... | collective-permute-start | bytes 5505032 | tf_op jit(solution)/shard_map/ppermute | solution.py:313
  14.3 40.7 %collective-permute-start.1 = (bf16[256,3584]{1,0:T(8,128)(2,1)}, bf16[256,3584]{1,0:T(8,128)(2,1)}, u32[]{:S(2)}, u32[]{:S(2)}) collective-permute-start(bf16[256,3584]{1,0:T(8,128)(2,1)} %reference_own_ref.1), channel_id=1, source_target_pairs={{0,1},{1,0},{2,3},{3,2},{4,5},{5,4},{6,7},{7,6},{8,9},{9,8},{10,11... | collective-permute-start | bytes 5505032 | tf_op jit(solution)/shard_map/ppermute | solution.py:314
  91.8 22.1 %collective-permute-start.2 = (f32[512,256]{1,0:T(8,128)}, f32[512,256]{1,0:T(8,128)S(1)}, u32[]{:S(2)}, u32[]{:S(2)}) collective-permute-start(f32[512,256]{1,0:T(8,128)} %get-tuple-element.26), channel_id=1, source_target_pairs={{0,1},{1,0},{2,3},{3,2},{4,5},{5,4},{6,7},{7,6},{8,9},{9,8},{10,11... | collective-permute-start | bytes 1572872 | tf_op jit(solution)/shard_map/ppermute | solution.py:334
  95.7 18.1 %all-to-all-start.1 = ((f32[32,1,1408]{2,1,0:T(1,128)}), f32[32,1,1408]{2,1,0:T(1,128)S(1)}, u32[]{:S(2)}, u32[]{:S(2)}) async-start(f32[32,1,1408]{2,1,0:T(1,128)} %broadcast_in_dim.27), calls=%async_computation.1 | async-start | bytes 360448 | tf_op jit(solution)/shard_map/all_to_all | solution.py:337
Sparse Core Ops, SparseCore 0:
  10.7 60.2 all-gather.2

commit v4 on v3

--- a/solution.py
+++ b/solution.py
@@ -132,7 +132,7 @@
             partial[k, rows, :] = sums[k]
         return carry
 
-    lax.fori_loop(0, seqs // 8, body, 0, unroll=2)
+    lax.fori_loop(0, seqs // 8, body, 0, unroll=8)
     sums = [jnp.sum(partial[k].T, axis=0, keepdims=True) for k in range(5)]
     whole = jnp.concatenate(sums[:2], axis=1)
     for shard in range(shards):
@@ -177,16 +177,13 @@
     )
 
 
-def finish_kernel(columns, place_ref, own_ref, other_ref, blocks_ref, weight_ref, shift_ref, sampled_ref, staged, sem):
+def finish_kernel(place_ref, own_ref, other_ref, totals_ref, weight_ref, shift_ref, sampled_ref, staged, sem):
     shards, _, part, vocab = shift_ref.shape
     seqs = shards * part
     half = place_ref[0]
     shard = place_ref[1]
 
-    totals = [None, None]
-    for j in range(blocks_ref.shape[0]):
-        k = (j // columns + j % columns) % 2
-        totals[k] = blocks_ref[j] if totals[k] is None else totals[k] + blocks_ref[j]
+    totals = [totals_ref[k] for k in range(2)]
     logs = [jnp.log(total[:, : 2 * seqs + 128]) for total in totals]
     deltas = [log[:, :seqs] - log[:, seqs : 2 * seqs] for log in logs]
     own_first = half == 0
@@ -243,11 +240,11 @@
         store.wait()
 
 
-def finish(place, columns, diff_own, diff_other, blocks, weight, shards):
+def finish(place, diff_own, diff_other, totals, weight, shards):
     seqs, vocab = diff_own.shape
     part = seqs // shards
     return pl.pallas_call(
-        functools.partial(finish_kernel, columns),
+        finish_kernel,
         in_specs=[pl.BlockSpec(memory_space=pltpu.SMEM)] + [VMEM] * 4,
         out_specs=[HBM, VMEM],
         out_shape=[
@@ -260,7 +257,7 @@
         ],
         compiler_params=pltpu.CompilerParams(vmem_limit_bytes=16 * MIB),
         name="finish",
-    )(place, diff_own, diff_other, blocks, weight)
+    )(place, diff_own, diff_other, totals, weight)
 
 
 def partners(z, y, x):
@@ -330,13 +327,18 @@
     )
 
     block = lax.all_to_all(block, DP, 0, 0, tiled=True)
-    block, diff_send = lax.optimization_barrier((block, diff_send))
     diff_other = lax.ppermute(diff_send, DP_MP, pairs)
     block = jnp.sum(block, axis=0, keepdims=True)
     block = jnp.broadcast_to(block, (copies,) + block.shape[1:])
     blocks = lax.all_to_all(block, MP, 0, 0, tiled=True)
+    index = lax.broadcasted_iota(jnp.int32, (copies, 1, 1), 0)
+    columns = lax.axis_size("mp_1")
+    odd = (index // columns + index % columns) % 2 == 1
+    totals = jnp.stack(
+        [jnp.sum(jnp.where(odd, 0.0, blocks), axis=0), jnp.sum(jnp.where(odd, blocks, 0.0), axis=0)]
+    )
     mixture_shift, sampled_logprobs = finish(
-        place, lax.axis_size("mp_1"), diff_own, diff_other, blocks, weight_mine, shards
+        place, diff_own, diff_other, totals, weight_mine, shards
     )
     return (mixture_shift.reshape(shards * seq_local, vocab), sampled_logprobs)
 

time: 124 us -> 124 us (level)
  waiting for transfers between devices: 63.6 us -> 62.3 us
    all_to_all x1, waiting for transfers between devices: 9.67 us -> 7.28 us  [local(): blocks = lax.all_to_all(block, MP, 0, 0, tiled=True)]
  transfers between devices with their start and end apart: 5 -> 5, of which waited for: 4 -> 5; matrix products, arithmetic and copies ran while one was open for 1% -> 1% of each run, Pallas kernels for 0% -> 0%
where the time goes in v4:
time: 124 us; the launch traced here: 123 us
  waiting for transfers between devices  62.3 us (50%)
  starting transfers between devices  18.4 us (15%)
  between operations  14.3 us (12%)
  Pallas kernels  12.8 us (10%)
  blocking collectives  12.5 us (10%)
  local copies, waits for them, and re-layouts  2.39 us (2%)
    ppermute x1, waiting for transfers between devices, local(): reference_other = lax.ppermute(reference_send, DP_MP, pairs)  19.7 us
    ppermute x1, waiting for transfers between devices, local(): policy_other = lax.ppermute(policy_send, DP_MP, pairs)  18.5 us
    all_gather x1, waiting for transfers between devices, local(): hidden = lax.all_gather(normed, DP, axis=0)  15.8 us
    all_to_all x1, blocking collectives, local(): block = lax.all_to_all(block, DP, 0, 0, tiled=True)  12.5 us
    all_to_all x1, starting transfers between devices, local(): blocks = lax.all_to_all(block, MP, 0, 0, tiled=True)  9.27 us
    pallas_call x1, Pallas kernels, mixture(): pl.pallas_call(mixture_kernel, in_specs=[HBM, VMEM] + [HBM] * 3 + [VMEM]...  7.68 us
    all_to_all x1, waiting for transfers between devices, local(): blocks = lax.all_to_all(block, MP, 0, 0, tiled=True)  7.28 us
    ppermute x1, starting transfers between devices, local(): policy_other = lax.ppermute(policy_send, DP_MP, pairs)  4.04 us
  transfers between devices with their start and end apart: 5, of which 5 were waited for; matrix products, arithmetic and copies ran while one was open for 1% of the time, Pallas kernels for 0%

profile of v4, /device:TPU:1, one launch (start us, length us, event | category | flops | bytes accessed | tf_op | source)
XLA Modules:
  0.0 123.3 jit_solution(1079451133217151154)
XLA Ops:
  7.3 2.9 %normalize.1 = bf16[2,32,3584]{2,1,0:T(8,128)(2,1)} custom-call(s32[2]{0:T(128)S(1)} %pad_add_fusion.half_ref.place_ref, bf16[64,3584]{1,0:T(8,128)(2,1)} %policy_ref.1, bf16[64,3584]{1,0:T(8,128)(2,1)} %reference_ref.1, f32[3584]{0:T(1024)} %policy_gain_ref.1, f32[3584]{0:T(1024)} %reference_gain_ref.1), custom_call_target="tpu_custom_call" | custom-call | tf_op jit(solution)/shard_map/normalize/pallas_call | solution.py:49
  10.3 4.0 %collective-permute-start = (bf16[256,3584]{1,0:T(8,128)(2,1)S(1)}, bf16[256,3584]{1,0:T(8,128)(2,1)}, u32[]{:S(2)}, u32[]{:S(2)}) collective-permute-start(bf16[256,3584]{1,0:T(8,128)(2,1)S(1)} %copy-done), channel_id=1, source_target_pairs={{0,1},{1,0},{2,3},{3,2},{4,5},{5,4},{6,7},{7,6},{8,9},{9,8},{10,11... | collective-permute-start | bytes 5505032 | tf_op jit(solution)/shard_map/ppermute | solution.py:310
  14.3 1.9 %collective-permute-start.1 = (bf16[256,3584]{1,0:T(8,128)(2,1)}, bf16[256,3584]{1,0:T(8,128)(2,1)}, u32[]{:S(2)}, u32[]{:S(2)}) collective-permute-start(bf16[256,3584]{1,0:T(8,128)(2,1)} %reference_own_ref.1), channel_id=1, source_target_pairs={{0,1},{1,0},{2,3},{3,2},{4,5},{5,4},{6,7},{7,6},{8,9},{9,8},{10,11... | collective-permute-start | bytes 5505032 | tf_op jit(solution)/shard_map/ppermute | solution.py:311
  16.3 0.1 reshape.132
  16.4 0.1 sub.46
  16.5 0.1 sub.49
  16.6 0.1 reshape.131
  16.7 0.1 broadcast_in_dim.45
  16.8 18.5 %collective-permute-done.policy_other_ref = bf16[256,3584]{1,0:T(8,128)(2,1)} collective-permute-done((bf16[256,3584]{1,0:T(8,128)(2,1)S(1)}, bf16[256,3584]{1,0:T(8,128)(2,1)}, u32[]{:S(2)}, u32[]{:S(2)}) %collective-permute-start) | collective-permute-done | bytes 1835040 | tf_op jit(solution)/shard_map/ppermute | solution.py:310
  35.3 19.7 %collective-permute-done.1.reference_other_ref = bf16[256,3584]{1,0:T(8,128)(2,1)} collective-permute-done((bf16[256,3584]{1,0:T(8,128)(2,1)}, bf16[256,3584]{1,0:T(8,128)(2,1)}, u32[]{:S(2)}, u32[]{:S(2)}) %collective-permute-start.1) | collective-permute-done | bytes 1835040 | tf_op jit(solution)/shard_map/ppermute | solution.py:311
  55.0 0.2 broadcast_in_dim.48.token_ref
  55.2 0.1 broadcast_in_dim.46.weight_ref
  55.3 15.8 %all-gather.3.cloned.1.call-done = bf16[32,32,3584]{2,1,0:T(8,128)(2,1)} async-done(((bf16[2,32,3584]{2,1,0:T(8,128)(2,1)}), bf16[32,32,3584]{2,1,0:T(8,128)(2,1)}) %all-gather.3.cloned.1.call-update) | async-done | bytes 7340048 | tf_op jit(solution)/shard_map/all_gather | solution.py:309
  71.1 7.7 %mixture.1 = (f32[512,256]{1,0:T(8,128)S(1)}, f32[512,256]{1,0:T(8,128)S(1)}, f32[16,1,1408]{2,1,0:T(1,128)S(1)}) custom-call(bf16[16,2,32,3584]{3,2,1,0:T(8,128)(2,1)} %bitcast.10, bf16[256,3584]{1,0:T(8,128)(2,1)S(1)} %copy-done, bf16[256,3584]{1,0:T(8,128)(2,1)} %collective-permute-done.policy_other_ref, bf16[256,3584]{1,0:T(8,128)(2,1)} %reference_own_ref.1, ...), custom_call_target="tpu_custom_call" | custom-call | tf_op jit(solution)/shard_map/mixture/pallas_call | solution.py:150
  78.8 0.8 copy-done.1
  79.6 12.5 %all_to_all.10 = f32[16,1,1408]{2,1,0:T(1,128)S(1)} all-to-all(f32[16,1,1408]{2,1,0:T(1,128)S(1)} %get-tuple-element.23), channel_id=1, replica_groups=mesh['dp_0'=8,'dp_1'=2,'mp_0'=8,'mp_1'=4] {'dp_0','dp_1'}, dimensions={0} | all-to-all | bytes 180224 | tf_op jit(solution)/shard_map/all_to_all | solution.py:329
  92.1 0.8 broadcast_in_dim.51
  92.8 9.3 %all-to-all-start.1 = ((f32[32,1,1408]{2,1,0:T(1,128)}), f32[32,1,1408]{2,1,0:T(1,128)S(1)}, u32[]{:S(2)}, u32[]{:S(2)}) async-start(f32[32,1,1408]{2,1,0:T(1,128)} %broadcast_in_dim.51), calls=%async_computation.1 | async-start | bytes 360448 | tf_op jit(solution)/shard_map/all_to_all | solution.py:333
  102.1 3.1 %collective-permute-start.2 = (f32[512,256]{1,0:T(8,128)}, f32[512,256]{1,0:T(8,128)S(1)}, u32[]{:S(2)}, u32[]{:S(2)}) collective-permute-start(f32[512,256]{1,0:T(8,128)} %copy-done.1), channel_id=1, source_target_pairs={{0,1},{1,0},{2,3},{3,2},{4,5},{5,4},{6,7},{7,6},{8,9},{9,8},{10,11... | collective-permute-start | bytes 1572872 | tf_op jit(solution)/shard_map/ppermute | solution.py:330
  105.3 0.1 dynamic-slice_bitcast_fusion.weight_ref
  105.4 7.3 %all-to-all-done.1 = f32[32,1,1408]{2,1,0:T(1,128)S(1)} async-done(((f32[32,1,1408]{2,1,0:T(1,128)}), f32[32,1,1408]{2,1,0:T(1,128)S(1)}, u32[]{:S(2)}, u32[]{:S(2)}) %all-to-all-start.1) | async-done | bytes 180256 | tf_op jit(solution)/shard_map/all_to_all | solution.py:333
  112.7 0.4 fusion
  113.1 1.1 collective-permute-done.2.other_ref
  114.2 2.3 %finish.1 = (f32[16,2,32,256]{3,2,1,0:T(8,128)}, f32[3,64]{1,0:T(4,128)}) custom-call(s32[2]{0:T(128)S(1)} %pad_add_fusion.half_ref.place_ref, f32[512,256]{1,0:T(8,128)S(1)} %get-tuple-element.21.own_ref, f32[512,256]{1,0:T(8,128)S(1)} %collective-permute-done.2.other_ref, f32[2,1,1408]{2,1,0:T(1,128)S(1)} %pad_maximum_fusion.totals_ref, ...), custom_call_target="tpu_custom_call" | custom-call | tf_op jit(solution)/shard_map/finish/pallas_call | solution.py:246
  (18 shorter events, 0.3 us)
Async XLA Ops:
  7.2 3.1 %copy-start = (bf16[256,3584]{1,0:T(8,128)(2,1)S(1)}, bf16[256,3584]{1,0:T(8,128)(2,1)}, u32[]{:S(2)}) copy-start(bf16[256,3584]{1,0:T(8,128)(2,1)} %policy_own_ref.1) | copy-start | bytes 5505028
  7.2 9.1 %copy-start.2 = (s32[1024]{0:T(1024)S(1)}, s32[1024]{0:T(1024)}, u32[]{:S(2)}) copy-start(s32[1024]{0:T(1024)} %param.15) | copy-start | bytes 12292
  7.2 9.4 %copy-start.3 = (f32[1024]{0:T(1024)S(1)}, f32[1024]{0:T(1024)}, u32[]{:S(2)}) copy-start(f32[1024]{0:T(1024)} %param.14) | copy-start | bytes 12292
  7.2 63.9 %all-gather.3.cloned.1.call-start = ((), (), s32[]{:S(2)}) async-start(), calls=%async_computation.2 | async-start | bytes 7798784 | tf_op jit(solution)/shard_map/all_gather | solution.py:309
  10.3 25.0 %collective-permute-start = (bf16[256,3584]{1,0:T(8,128)(2,1)S(1)}, bf16[256,3584]{1,0:T(8,128)(2,1)}, u32[]{:S(2)}, u32[]{:S(2)}) collective-permute-start(bf16[256,3584]{1,0:T(8,128)(2,1)S(1)} %copy-done), channel_id=1, source_target_pairs={{0,1},{1,0},{2,3},{3,2},{4,5},{5,4},{6,7},{7,6},{8,9},{9,8},{10,11... | collective-permute-start | bytes 5505032 | tf_op jit(solution)/shard_map/ppermute | solution.py:310
  14.3 40.7 %collective-permute-start.1 = (bf16[256,3584]{1,0:T(8,128)(2,1)}, bf16[256,3584]{1,0:T(8,128)(2,1)}, u32[]{:S(2)}, u32[]{:S(2)}) collective-permute-start(bf16[256,3584]{1,0:T(8,128)(2,1)} %reference_own_ref.1), channel_id=1, source_target_pairs={{0,1},{1,0},{2,3},{3,2},{4,5},{5,4},{6,7},{7,6},{8,9},{9,8},{10,11... | collective-permute-start | bytes 5505032 | tf_op jit(solution)/shard_map/ppermute | solution.py:311
  78.8 0.8 copy-start.1
  92.8 19.8 %all-to-all-start.1 = ((f32[32,1,1408]{2,1,0:T(1,128)}), f32[32,1,1408]{2,1,0:T(1,128)S(1)}, u32[]{:S(2)}, u32[]{:S(2)}) async-start(f32[32,1,1408]{2,1,0:T(1,128)} %broadcast_in_dim.51), calls=%async_computation.1 | async-start | bytes 360448 | tf_op jit(solution)/shard_map/all_to_all | solution.py:333
  102.1 12.0 %collective-permute-start.2 = (f32[512,256]{1,0:T(8,128)}, f32[512,256]{1,0:T(8,128)S(1)}, u32[]{:S(2)}, u32[]{:S(2)}) collective-permute-start(f32[512,256]{1,0:T(8,128)} %copy-done.1), channel_id=1, source_target_pairs={{0,1},{1,0},{2,3},{3,2},{4,5},{5,4},{6,7},{7,6},{8,9},{9,8},{10,11... | collective-permute-start | bytes 1572872 | tf_op jit(solution)/shard_map/ppermute | solution.py:330
Sparse Core Ops, SparseCore 0:
  10.7 60.2 all-gather.2

commit v5 on v4

--- a/solution.py
+++ b/solution.py
@@ -177,7 +177,7 @@
     )
 
 
-def finish_kernel(place_ref, own_ref, other_ref, totals_ref, weight_ref, shift_ref, sampled_ref, staged, sem):
+def finish_kernel(place_ref, own_ref, other_ref, totals_ref, blocks_ref, weight_ref, shift_ref, sampled_ref, staged, sem):
     shards, _, part, vocab = shift_ref.shape
     seqs = shards * part
     half = place_ref[0]
@@ -187,9 +187,11 @@
     logs = [jnp.log(total[:, : 2 * seqs + 128]) for total in totals]
     deltas = [log[:, :seqs] - log[:, seqs : 2 * seqs] for log in logs]
     own_first = half == 0
+    partner = blocks_ref[place_ref[2]]
+    center = jnp.log(partner[:, :seqs]) - jnp.log(partner[:, seqs : 2 * seqs])
     turns = (
         jnp.where(own_first, deltas[0], deltas[1]),
-        jnp.where(own_first, deltas[1], deltas[0]),
+        jnp.where(own_first, deltas[1], deltas[0]) - center,
     )
 
     chunk = 128
@@ -202,7 +204,7 @@
             shards_here = pl.ds(j * per, per)
             for group in range(vocab // 128):
                 lanes = pl.ds(group * 128, 128)
-                shifted = diff_ref[pl.ds(j * chunk, chunk), lanes] + delta
+                shifted = diff_ref[pl.ds(j * chunk, chunk), lanes].astype(jnp.float32) + delta
                 staged[turn, shards_here, :, lanes] = shifted.reshape(per, part, 128)
             store = pltpu.make_async_copy(
                 staged.at[turn, shards_here],
@@ -240,12 +242,12 @@
         store.wait()
 
 
-def finish(place, diff_own, diff_other, totals, weight, shards):
+def finish(place, diff_own, diff_other, totals, blocks, weight, shards):
     seqs, vocab = diff_own.shape
     part = seqs // shards
     return pl.pallas_call(
         finish_kernel,
-        in_specs=[pl.BlockSpec(memory_space=pltpu.SMEM)] + [VMEM] * 4,
+        in_specs=[pl.BlockSpec(memory_space=pltpu.SMEM)] + [VMEM] * 5,
         out_specs=[HBM, VMEM],
         out_shape=[
             jax.ShapeDtypeStruct((shards, 2, part, vocab), jnp.float32),
@@ -257,7 +259,7 @@
         ],
         compiler_params=pltpu.CompilerParams(vmem_limit_bytes=16 * MIB),
         name="finish",
-    )(place, diff_own, diff_other, totals, weight)
+    )(place, diff_own, diff_other, totals, blocks, weight)
 
 
 def partners(z, y, x):
@@ -299,7 +301,7 @@
     )
     first_own = (shard * copies + copy) * vocab
     first_other = (shard * copies + other_copy) * vocab
-    place = jnp.stack([half, shard]).astype(jnp.int32)
+    place = jnp.stack([half, shard, other_copy]).astype(jnp.int32)
     pairs = partners(lax.axis_size("dp_0"), lax.axis_size("mp_0"), lax.axis_size("mp_1"))
 
     normed = normalize(place, policy_hidden, reference_hidden, policy_gain, reference_gain)
@@ -326,9 +328,10 @@
         hidden, policy_embedding, policy_other, reference_embedding, reference_other, weight, token
     )
 
-    block = lax.all_to_all(block, DP, 0, 0, tiled=True)
+    block = jnp.sum(lax.all_to_all(block, DP, 0, 0, tiled=True), axis=0, keepdims=True)
+    center = jnp.log(block[0, 0, :seqs]) - jnp.log(block[0, 0, seqs : 2 * seqs])
+    diff_send = (diff_send + center[:, None]).astype(jnp.bfloat16)
     diff_other = lax.ppermute(diff_send, DP_MP, pairs)
-    block = jnp.sum(block, axis=0, keepdims=True)
     block = jnp.broadcast_to(block, (copies,) + block.shape[1:])
     blocks = lax.all_to_all(block, MP, 0, 0, tiled=True)
     index = lax.broadcasted_iota(jnp.int32, (copies, 1, 1), 0)
@@ -338,7 +341,7 @@
         [jnp.sum(jnp.where(odd, 0.0, blocks), axis=0), jnp.sum(jnp.where(odd, blocks, 0.0), axis=0)]
     )
     mixture_shift, sampled_logprobs = finish(
-        place, diff_own, diff_other, totals, weight_mine, shards
+        place, diff_own, diff_other, totals, blocks, weight_mine, shards
     )
     return (mixture_shift.reshape(shards * seq_local, vocab), sampled_logprobs)
 

time: 124 us -> 124 us (level)
  blocking collectives: 12.5 us -> 0 us
  waiting for transfers between devices: 62.3 us -> 69.4 us
  starting transfers between devices: 18.4 us -> 22.9 us
    all_to_all x1 -> x0, blocking collectives: 12.5 us -> none  [local(): block = lax.all_to_all(block, DP, 0, 0, tiled=True)]
    all_to_all x0 -> x1, waiting for transfers between devices: none -> 8.23 us  [local(): lax.all_to_all(block, DP, 0, 0, tiled=True)]
    all_to_all x0 -> x1, starting transfers between devices: none -> 4.5 us  [local(): lax.all_to_all(block, DP, 0, 0, tiled=True)]
  transfers between devices with their start and end apart: 5 -> 6, of which waited for: 5 -> 5; matrix products, arithmetic and copies ran while one was open for 1% -> 1% of each run, Pallas kernels for 0% -> 0%
where the time goes in v5:
time: 124 us; the launch traced here: 123 us
  waiting for transfers between devices  69.4 us (56%)
  starting transfers between devices  22.9 us (18%)
  between operations  14.3 us (12%)
  Pallas kernels  13.5 us (11%)
  local copies, waits for them, and re-layouts  2.4 us (2%)
    ppermute x1, waiting for transfers between devices, local(): reference_other = lax.ppermute(reference_send, DP_MP, pairs)  19.7 us
    ppermute x1, waiting for transfers between devices, local(): policy_other = lax.ppermute(policy_send, DP_MP, pairs)  18.5 us
    all_gather x1, waiting for transfers between devices, local(): hidden = lax.all_gather(normed, DP, axis=0)  15.8 us
    all_to_all x1, starting transfers between devices, local(): blocks = lax.all_to_all(block, MP, 0, 0, tiled=True)  9.28 us
    pallas_call x1, Pallas kernels, mixture(): pl.pallas_call(mixture_kernel, in_specs=[HBM, VMEM] + [HBM] * 3 + [VMEM]...  8.31 us
    all_to_all x1, waiting for transfers between devices, local(): lax.all_to_all(block, DP, 0, 0, tiled=True)  8.23 us
    all_to_all x1, waiting for transfers between devices, local(): blocks = lax.all_to_all(block, MP, 0, 0, tiled=True)  7.22 us
    all_to_all x1, starting transfers between devices, local(): lax.all_to_all(block, DP, 0, 0, tiled=True)  4.5 us
  transfers between devices with their start and end apart: 6, of which 5 were waited for; matrix products, arithmetic and copies ran while one was open for 1% of the time, Pallas kernels for 0%

profile of v5, /device:TPU:1, one launch (start us, length us, event | category | flops | bytes accessed | tf_op | source)
XLA Modules:
  0.0 123.2 jit_solution(11574514103853529453)
XLA Ops:
  7.3 2.9 %normalize.1 = bf16[2,32,3584]{2,1,0:T(8,128)(2,1)} custom-call(s32[3]{0:T(128)S(1)} %pad_add_fusion.half_ref.place_ref, bf16[64,3584]{1,0:T(8,128)(2,1)} %policy_ref.1, bf16[64,3584]{1,0:T(8,128)(2,1)} %reference_ref.1, f32[3584]{0:T(1024)} %policy_gain_ref.1, f32[3584]{0:T(1024)} %reference_gain_ref.1), custom_call_target="tpu_custom_call" | custom-call | tf_op jit(solution)/shard_map/normalize/pallas_call | solution.py:49
  10.3 4.0 %collective-permute-start = (bf16[256,3584]{1,0:T(8,128)(2,1)S(1)}, bf16[256,3584]{1,0:T(8,128)(2,1)}, u32[]{:S(2)}, u32[]{:S(2)}) collective-permute-start(bf16[256,3584]{1,0:T(8,128)(2,1)S(1)} %copy-done), channel_id=1, source_target_pairs={{0,1},{1,0},{2,3},{3,2},{4,5},{5,4},{6,7},{7,6},{8,9},{9,8},{10,11... | collective-permute-start | bytes 5505032 | tf_op jit(solution)/shard_map/ppermute | solution.py:312
  14.3 1.9 %collective-permute-start.1 = (bf16[256,3584]{1,0:T(8,128)(2,1)}, bf16[256,3584]{1,0:T(8,128)(2,1)}, u32[]{:S(2)}, u32[]{:S(2)}) collective-permute-start(bf16[256,3584]{1,0:T(8,128)(2,1)} %reference_own_ref.1), channel_id=1, source_target_pairs={{0,1},{1,0},{2,3},{3,2},{4,5},{5,4},{6,7},{7,6},{8,9},{9,8},{10,11... | collective-permute-start | bytes 5505032 | tf_op jit(solution)/shard_map/ppermute | solution.py:313
  16.3 0.1 reshape.146
  16.4 0.1 sub.56
  16.6 0.1 reshape.145
  16.7 0.1 broadcast_in_dim.48
  16.8 18.5 %collective-permute-done.policy_other_ref = bf16[256,3584]{1,0:T(8,128)(2,1)} collective-permute-done((bf16[256,3584]{1,0:T(8,128)(2,1)S(1)}, bf16[256,3584]{1,0:T(8,128)(2,1)}, u32[]{:S(2)}, u32[]{:S(2)}) %collective-permute-start) | collective-permute-done | bytes 1835040 | tf_op jit(solution)/shard_map/ppermute | solution.py:312
  35.3 19.7 %collective-permute-done.1.reference_other_ref = bf16[256,3584]{1,0:T(8,128)(2,1)} collective-permute-done((bf16[256,3584]{1,0:T(8,128)(2,1)}, bf16[256,3584]{1,0:T(8,128)(2,1)}, u32[]{:S(2)}, u32[]{:S(2)}) %collective-permute-start.1) | collective-permute-done | bytes 1835040 | tf_op jit(solution)/shard_map/ppermute | solution.py:313
  55.0 0.2 broadcast_in_dim.51.token_ref
  55.2 0.1 broadcast_in_dim.49.weight_ref
  55.3 15.8 %all-gather.3.cloned.1.call-done = bf16[32,32,3584]{2,1,0:T(8,128)(2,1)} async-done(((bf16[2,32,3584]{2,1,0:T(8,128)(2,1)}), bf16[32,32,3584]{2,1,0:T(8,128)(2,1)}) %all-gather.3.cloned.1.call-update) | async-done | bytes 7340048 | tf_op jit(solution)/shard_map/all_gather | solution.py:311
  71.1 8.3 %mixture.1 = (f32[512,256]{1,0:T(8,128)S(1)}, f32[512,256]{1,0:T(8,128)S(1)}, f32[16,1,1408]{2,1,0:T(1,128)}) custom-call(bf16[16,2,32,3584]{3,2,1,0:T(8,128)(2,1)} %bitcast.12, bf16[256,3584]{1,0:T(8,128)(2,1)S(1)} %copy-done, bf16[256,3584]{1,0:T(8,128)(2,1)} %collective-permute-done.policy_other_ref, bf16[256,3584]{1,0:T(8,128)(2,1)} %reference_own_ref.1, ...), custom_call_target="tpu_custom_call" | custom-call | tf_op jit(solution)/shard_map/mixture/pallas_call | solution.py:150
  79.4 0.8 copy-done.1
  80.2 4.5 %all-to-all-start = ((f32[16,1,1408]{2,1,0:T(1,128)}), f32[16,1,1408]{2,1,0:T(1,128)S(1)}, u32[]{:S(2)}, u32[]{:S(2)}) async-start(f32[16,1,1408]{2,1,0:T(1,128)} %get-tuple-element.23), calls=%async_computation | async-start | bytes 180224 | tf_op jit(solution)/shard_map/all_to_all | solution.py:331
  84.7 0.1 dynamic-slice_bitcast_fusion.weight_ref
  84.8 8.2 %all-to-all-done = f32[16,1,1408]{2,1,0:T(1,128)S(1)} async-done(((f32[16,1,1408]{2,1,0:T(1,128)}), f32[16,1,1408]{2,1,0:T(1,128)S(1)}, u32[]{:S(2)}, u32[]{:S(2)}) %all-to-all-start) | async-done | bytes 90144 | tf_op jit(solution)/shard_map/all_to_all | solution.py:331
  93.1 0.8 broadcast_in_dim.55
  93.8 9.3 %all-to-all-start.1 = ((f32[32,1,1408]{2,1,0:T(1,128)}), f32[32,1,1408]{2,1,0:T(1,128)S(1)}, u32[]{:S(2)}, u32[]{:S(2)}) async-start(f32[32,1,1408]{2,1,0:T(1,128)} %broadcast_in_dim.55), calls=%async_computation.1 | async-start | bytes 360448 | tf_op jit(solution)/shard_map/all_to_all | solution.py:336
  103.1 0.1 add_convert_fusion
  103.3 3.1 %collective-permute-start.2 = (bf16[512,256]{1,0:T(8,128)(2,1)S(1)}, bf16[512,256]{1,0:T(8,128)(2,1)S(1)}, u32[]{:S(2)}, u32[]{:S(2)}) collective-permute-start(bf16[512,256]{1,0:T(8,128)(2,1)S(1)} %add_convert_fusion), channel_id=1, source_target_pairs={{0,1},{1,0},{2,3},{3,2},{4,5},{5,4},{6,7},{7,6},{8,9},{9,8},{10,11... | collective-permute-start | bytes 786440 | tf_op jit(solution)/shard_map/ppermute | solution.py:334
  106.4 7.2 %all-to-all-done.1.blocks_ref = f32[32,1,1408]{2,1,0:T(1,128)S(1)} async-done(((f32[32,1,1408]{2,1,0:T(1,128)}), f32[32,1,1408]{2,1,0:T(1,128)S(1)}, u32[]{:S(2)}, u32[]{:S(2)}) %all-to-all-start.1) | async-done | bytes 180256 | tf_op jit(solution)/shard_map/all_to_all | solution.py:336
  113.7 0.4 fusion
  114.1 2.3 %finish.1 = (f32[16,2,32,256]{3,2,1,0:T(8,128)}, f32[3,64]{1,0:T(4,128)}) custom-call(s32[3]{0:T(128)S(1)} %pad_add_fusion.half_ref.place_ref, f32[512,256]{1,0:T(8,128)S(1)} %copy-done.2, bf16[512,256]{1,0:T(8,128)(2,1)S(1)} %collective-permute-done.2.other_ref, f32[2,1,1408]{2,1,0:T(1,128)S(1)} %pad_maximum_fusion.totals_ref, ...), custom_call_target="tpu_custom_call" | custom-call | tf_op jit(solution)/shard_map/finish/pallas_call | solution.py:248
  (24 shorter events, 0.4 us)
Async XLA Ops:
  7.2 3.1 %copy-start = (bf16[256,3584]{1,0:T(8,128)(2,1)S(1)}, bf16[256,3584]{1,0:T(8,128)(2,1)}, u32[]{:S(2)}) copy-start(bf16[256,3584]{1,0:T(8,128)(2,1)} %policy_own_ref.1) | copy-start | bytes 5505028
  7.2 9.1 %copy-start.3 = (s32[1024]{0:T(1024)S(1)}, s32[1024]{0:T(1024)}, u32[]{:S(2)}) copy-start(s32[1024]{0:T(1024)} %param.15) | copy-start | bytes 12292
  7.2 9.4 %copy-start.4 = (f32[1024]{0:T(1024)S(1)}, f32[1024]{0:T(1024)}, u32[]{:S(2)}) copy-start(f32[1024]{0:T(1024)} %param.14) | copy-start | bytes 12292
  7.2 63.9 %all-gather.3.cloned.1.call-start = ((), (), s32[]{:S(2)}) async-start(), calls=%async_computation.2 | async-start | bytes 7798784 | tf_op jit(solution)/shard_map/all_gather | solution.py:311
  10.3 25.0 %collective-permute-start = (bf16[256,3584]{1,0:T(8,128)(2,1)S(1)}, bf16[256,3584]{1,0:T(8,128)(2,1)}, u32[]{:S(2)}, u32[]{:S(2)}) collective-permute-start(bf16[256,3584]{1,0:T(8,128)(2,1)S(1)} %copy-done), channel_id=1, source_target_pairs={{0,1},{1,0},{2,3},{3,2},{4,5},{5,4},{6,7},{7,6},{8,9},{9,8},{10,11... | collective-permute-start | bytes 5505032 | tf_op jit(solution)/shard_map/ppermute | solution.py:312
  14.3 40.7 %collective-permute-start.1 = (bf16[256,3584]{1,0:T(8,128)(2,1)}, bf16[256,3584]{1,0:T(8,128)(2,1)}, u32[]{:S(2)}, u32[]{:S(2)}) collective-permute-start(bf16[256,3584]{1,0:T(8,128)(2,1)} %reference_own_ref.1), channel_id=1, source_target_pairs={{0,1},{1,0},{2,3},{3,2},{4,5},{5,4},{6,7},{7,6},{8,9},{9,8},{10,11... | collective-permute-start | bytes 5505032 | tf_op jit(solution)/shard_map/ppermute | solution.py:313
  79.4 0.8 copy-start.1
  80.2 33.9 %copy-start.2 = (f32[512,256]{1,0:T(8,128)S(1)}, f32[512,256]{1,0:T(8,128)}, u32[]{:S(2)}) copy-start(f32[512,256]{1,0:T(8,128)} %copy-done.1) | copy-start | bytes 1572868
  80.2 12.8 %all-to-all-start = ((f32[16,1,1408]{2,1,0:T(1,128)}), f32[16,1,1408]{2,1,0:T(1,128)S(1)}, u32[]{:S(2)}, u32[]{:S(2)}) async-start(f32[16,1,1408]{2,1,0:T(1,128)} %get-tuple-element.23), calls=%async_computation | async-start | bytes 180224 | tf_op jit(solution)/shard_map/all_to_all | solution.py:331
  93.8 19.8 %all-to-all-start.1 = ((f32[32,1,1408]{2,1,0:T(1,128)}), f32[32,1,1408]{2,1,0:T(1,128)S(1)}, u32[]{:S(2)}, u32[]{:S(2)}) async-start(f32[32,1,1408]{2,1,0:T(1,128)} %broadcast_in_dim.55), calls=%async_computation.1 | async-start | bytes 360448 | tf_op jit(solution)/shard_map/all_to_all | solution.py:336
  103.3 10.8 %collective-permute-start.2 = (bf16[512,256]{1,0:T(8,128)(2,1)S(1)}, bf16[512,256]{1,0:T(8,128)(2,1)S(1)}, u32[]{:S(2)}, u32[]{:S(2)}) collective-permute-start(bf16[512,256]{1,0:T(8,128)(2,1)S(1)} %add_convert_fusion), channel_id=1, source_target_pairs={{0,1},{1,0},{2,3},{3,2},{4,5},{5,4},{6,7},{7,6},{8,9},{9,8},{10,11... | collective-permute-start | bytes 786440 | tf_op jit(solution)/shard_map/ppermute | solution.py:334
Sparse Core Ops, SparseCore 0:
  10.7 60.2 all-gather.2

commit v6 on v3

--- a/solution.py
+++ b/solution.py
@@ -24,9 +24,12 @@
     return pltpu.with_memory_space_constraint(x, pltpu.HBM)
 
 
-def normalize_kernel(half_ref, policy_ref, reference_ref, policy_gain_ref, reference_gain_ref, out_ref, rows, in_sem):
-    part = out_ref.shape[1]
-    first = pl.multiple_of(half_ref[0] * part, part)
+def normalize_kernel(
+    place_ref, policy_ref, reference_ref, policy_gain_ref, reference_gain_ref, main_ref, quarter_ref, rows, in_sem
+):
+    part, width = rows.shape[1:]
+    depth = width // 4
+    first = pl.multiple_of(place_ref[0] * part, part)
     models = ((policy_ref, policy_gain_ref), (reference_ref, reference_gain_ref))
     loads = [
         pltpu.make_async_copy(hidden_ref.at[pl.ds(first, part), :], rows.at[model], in_sem.at[model])
@@ -38,27 +41,43 @@
         loads[model].wait()
         values = rows[model].astype(jnp.float32)
         meansq = jnp.mean(values * values, axis=-1, keepdims=True)
-        gain = gain_ref[...].reshape(1, values.shape[1])
-        normed = values * lax.rsqrt(meansq + epsilon) * gain
-        out_ref[model] = normed.astype(jnp.bfloat16)
-
-
-def normalize(half, policy_hidden, reference_hidden, policy_gain, reference_gain):
+        gain = gain_ref[...].reshape(1, width)
+        normed = (values * lax.rsqrt(meansq + epsilon) * gain).astype(jnp.bfloat16)
+        if model == 0:
+            main_ref[: part // 2] = normed[: part // 2]
+            for i in range(4):
+
+                @pl.when(place_ref[2] == i)
+                def _(i=i, normed=normed):
+                    quarter_ref[...] = normed[part // 2 :, i * depth : (i + 1) * depth]
+        else:
+            main_ref[part // 2 :] = normed
+
+
+def normalize(place, policy_hidden, reference_hidden, policy_gain, reference_gain):
     rows, width = policy_hidden.shape
     part = rows // 2
     return pl.pallas_call(
         normalize_kernel,
         in_specs=[pl.BlockSpec(memory_space=pltpu.SMEM)] + [HBM] * 2 + [VMEM] * 2,
-        out_specs=VMEM,
-        out_shape=jax.ShapeDtypeStruct((2, part, width), jnp.bfloat16),
+        out_specs=[VMEM] * 2,
+        out_shape=[
+            jax.ShapeDtypeStruct((part + part // 2, width), jnp.bfloat16),
+            jax.ShapeDtypeStruct((part // 2, width // 4), jnp.bfloat16),
+        ],
         scratch_shapes=[pltpu.VMEM((2, part, width), jnp.bfloat16), pltpu.SemaphoreType.DMA((2,))],
         compiler_params=pltpu.CompilerParams(vmem_limit_bytes=16 * MIB),
         name="normalize",
-    )(half, in_hbm(policy_hidden), in_hbm(reference_hidden), in_hbm(policy_gain), in_hbm(reference_gain))
+    )(place, in_hbm(policy_hidden), in_hbm(reference_hidden), in_hbm(policy_gain), in_hbm(reference_gain))
 
 
 def mixture_kernel(
-    hidden_ref,
+    place_ref,
+    main_ref,
+    quarter_0_ref,
+    quarter_1_ref,
+    quarter_2_ref,
+    quarter_3_ref,
     policy_own_ref,
     policy_other_ref,
     reference_own_ref,
@@ -74,23 +93,37 @@
     reference_acc,
     partial,
     sem,
+    quarter_sem,
 ):
     chunks = sem.shape[0]
-    shards, _, part, width = hidden_ref.shape
+    shards, _, part, width = hidden.shape
     depth = width // chunks
     vocab = policy_own_ref.shape[0]
     seqs = shards * part
 
     def loads(k):
         columns = pl.ds(k * depth, depth)
+        low = pl.ds(0, part // 2)
         rest = (policy_other_ref, reference_own_ref, reference_other_ref)
-        pairs = [(hidden_ref.at[:, :, :, columns], hidden.at[:, :, :, columns])]
+        pairs = [
+            (main_ref.at[:, low, columns], hidden.at[:, 0, low, columns]),
+            (main_ref.at[:, pl.ds(part // 2, part), columns], hidden.at[:, 1, :, columns]),
+        ]
         pairs += [(ref.at[:, columns], loaded.at[i, :, columns]) for i, ref in enumerate(rest)]
         return [pltpu.make_async_copy(*pair, sem.at[k, i]) for i, pair in enumerate(pairs)]
 
+    quarters = []
+    for i, ref in enumerate((quarter_0_ref, quarter_1_ref, quarter_2_ref, quarter_3_ref)):
+        start = pl.multiple_of((place_ref[2] ^ i) * (width // 4), 128)
+        target = hidden.at[:, 0, pl.ds(part // 2, part // 2), pl.ds(start, width // 4)]
+        quarters.append(pltpu.make_async_copy(ref, target, quarter_sem.at[i]))
+    for quarter in quarters:
+        quarter.start()
     for k in range(chunks):
         for load in loads(k):
             load.start()
+    for quarter in quarters:
+        quarter.wait()
     for k in range(chunks):
         for load in loads(k):
             load.wait()
@@ -132,7 +165,7 @@
             partial[k, rows, :] = sums[k]
         return carry
 
-    lax.fori_loop(0, seqs // 8, body, 0, unroll=2)
+    lax.fori_loop(0, seqs // 8, body, 0, unroll=8)
     sums = [jnp.sum(partial[k].T, axis=0, keepdims=True) for k in range(5)]
     whole = jnp.concatenate(sums[:2], axis=1)
     for shard in range(shards):
@@ -142,14 +175,15 @@
         )
 
 
-def mixture(hidden, policy_own, policy_other, reference_own, reference_other, weight, token):
-    shards, _, part, width = hidden.shape
+def mixture(place, main, quarters, policy_own, policy_other, reference_own, reference_other, weight, token):
+    shards, rows, width = main.shape
+    part = rows // 3 * 2
     vocab = policy_own.shape[0]
     seqs = shards * part
     chunks = 7
     return pl.pallas_call(
         mixture_kernel,
-        in_specs=[HBM, VMEM] + [HBM] * 3 + [VMEM] * 2,
+        in_specs=[pl.BlockSpec(memory_space=pltpu.SMEM)] + [HBM] * 5 + [VMEM] + [HBM] * 3 + [VMEM] * 2,
         out_specs=[VMEM] * 3,
         out_shape=[
             jax.ShapeDtypeStruct((seqs, vocab), jnp.float32),
@@ -162,12 +196,15 @@
             pltpu.VMEM((seqs, 2 * vocab), jnp.float32),
             pltpu.VMEM((seqs, 2 * vocab), jnp.float32),
             pltpu.VMEM((5, seqs, 128), jnp.float32),
-            pltpu.SemaphoreType.DMA((chunks, 4)),
+            pltpu.SemaphoreType.DMA((chunks, 5)),
+            pltpu.SemaphoreType.DMA((4,)),
         ],
         compiler_params=pltpu.CompilerParams(vmem_limit_bytes=32 * MIB),
         name="mixture",
     )(
-        in_hbm(hidden),
+        place,
+        in_hbm(main),
+        *map(in_hbm, quarters),
         pltpu.with_memory_space_constraint(policy_own, pltpu.VMEM),
         in_hbm(policy_other),
         in_hbm(reference_own),
@@ -185,7 +222,7 @@
 
     totals = [None, None]
     for j in range(blocks_ref.shape[0]):
-        k = (j // columns + j % columns) % 2
+        k = half_bit(j // columns, j % columns)
         totals[k] = blocks_ref[j] if totals[k] is None else totals[k] + blocks_ref[j]
     logs = [jnp.log(total[:, : 2 * seqs + 128]) for total in totals]
     deltas = [log[:, :seqs] - log[:, seqs : 2 * seqs] for log in logs]
@@ -263,13 +300,21 @@
     )(place, diff_own, diff_other, blocks, weight)
 
 
-def partners(z, y, x):
+def half_bit(row, column):
+    return ((row + 1) // 2 + (column + 1) // 2) % 2
+
+
+def beside(i, size):
+    return (i + 1) % size if i % 2 else (i - 1) % size
+
+
+def pairs_of(sizes, target):
+    z, y, x = sizes
     pairs = []
     for source in range(z * 2 * y * x):
         i, rest = divmod(source, 2 * y * x)
         c, rest = divmod(rest, y * x)
-        j, k = divmod(rest, x)
-        j, k = (j, k ^ 1) if c == 0 else (j ^ 1, k)
+        j, k = target(c, *divmod(rest, x))
         pairs.append((source, ((i * 2 + c) * y + j) * x + k))
     return pairs
 
@@ -294,7 +339,8 @@
     core = lax.axis_index("dp_1")
     row = lax.axis_index("mp_0")
     column = lax.axis_index("mp_1")
-    half = (row + column) % 2
+    half = half_bit(row, column)
+    quarter = 3 - 2 * (row % 2) - column % 2
     other_copy = jnp.where(
         core == 0,
         row * lax.axis_size("mp_1") + (column ^ 1),
@@ -302,16 +348,22 @@
     )
     first_own = (shard * copies + copy) * vocab
     first_other = (shard * copies + other_copy) * vocab
-    place = jnp.stack([half, shard]).astype(jnp.int32)
-    pairs = partners(lax.axis_size("dp_0"), lax.axis_size("mp_0"), lax.axis_size("mp_1"))
-
-    normed = normalize(place, policy_hidden, reference_hidden, policy_gain, reference_gain)
-    normed, policy_send, reference_send = lax.optimization_barrier(
-        (normed, policy_embedding, reference_embedding)
-    )
-    hidden = lax.all_gather(normed, DP, axis=0)
+    place = jnp.stack([half, shard, quarter]).astype(jnp.int32)
+    sizes = lax.axis_size("dp_0"), lax.axis_size("mp_0"), lax.axis_size("mp_1")
+    pairs = pairs_of(sizes, lambda c, j, k: (j, k ^ 1) if c == 0 else (j ^ 1, k))
+    across = pairs_of(sizes, lambda c, j, k: (j, beside(k, sizes[2])))
+    along = pairs_of(sizes, lambda c, j, k: (beside(j, sizes[1]), k))
+    aslant = pairs_of(sizes, lambda c, j, k: (beside(j, sizes[1]), beside(k, sizes[2])))
+
+    main, part_quarter = normalize(place, policy_hidden, reference_hidden, policy_gain, reference_gain)
+    main, part_quarter, policy_send, reference_send = lax.optimization_barrier(
+        (main, part_quarter, policy_embedding, reference_embedding)
+    )
+    main = lax.all_gather(main, DP, axis=0)
     policy_other = lax.ppermute(policy_send, DP_MP, pairs)
     reference_other = lax.ppermute(reference_send, DP_MP, pairs)
+    held = lax.all_gather(part_quarter, DP, axis=0)
+    quarters = [held] + [lax.ppermute(held, DP_MP, way) for way in (across, along, aslant)]
 
     seqs = shards * part
     weights = mixture_weight.reshape(shards, 2, part)
@@ -326,7 +378,7 @@
         (policy_other, reference_other, weight, token)
     )
     diff_own, diff_send, block = mixture(
-        hidden, policy_embedding, policy_other, reference_embedding, reference_other, weight, token
+        place, main, quarters, policy_embedding, policy_other, reference_embedding, reference_other, weight, token
     )
 
     block = lax.all_to_all(block, DP, 0, 0, tiled=True)

time: 124 us -> 124 us (level)
  waiting for transfers between devices: 63.6 us -> 25.6 us
  blocking collectives: 12.5 us -> 38.6 us
  starting transfers between devices: 17.5 us -> 28.4 us
    all_gather x0 -> x1, blocking collectives: none -> 26.1 us  [local(): held = lax.all_gather(part_quarter, DP, axis=0)]
    ppermute x1, waiting for transfers between devices: 19.7 us -> 0.87 us  [local(): reference_other = lax.ppermute(reference_send, DP_MP, pairs)]
    ppermute x1, waiting for transfers between devices: 18.5 us -> 0.01 us  [local(): policy_other = lax.ppermute(policy_send, DP_MP, pairs)]
    all_gather x1, waiting for transfers between devices: 15.8 us -> 0.01 us  [local(): main = lax.all_gather(main, DP, axis=0)]
    ppermute x0 -> x3, waiting for transfers between devices: none -> 15 us  [local(): lax.ppermute(held, DP_MP, way)]
    ppermute x0 -> x3, starting transfers between devices: none -> 11.4 us  [local(): lax.ppermute(held, DP_MP, way)]
  transfers between devices with their start and end apart: 5 -> 8, of which waited for: 4 -> 5; matrix products, arithmetic and copies ran while one was open for 1% -> 1% of each run, Pallas kernels for 0% -> 0%
where the time goes in v6:
time: 124 us; the launch traced here: 123 us
  blocking collectives  38.6 us (31%)
  starting transfers between devices  28.4 us (23%)
  waiting for transfers between devices  25.6 us (21%)
  between operations  14.3 us (12%)
  Pallas kernels  14.2 us (11%)
  local copies, waits for them, and re-layouts  1.59 us (1%)
    all_gather x1, blocking collectives, local(): held = lax.all_gather(part_quarter, DP, axis=0)  26.1 us
    ppermute x3, waiting for transfers between devices, local(): lax.ppermute(held, DP_MP, way)  15 us
    all_to_all x1, blocking collectives, local(): block = lax.all_to_all(block, DP, 0, 0, tiled=True)  12.5 us
    ppermute x3, starting transfers between devices, local(): lax.ppermute(held, DP_MP, way)  11.4 us
    all_to_all x1, waiting for transfers between devices, local(): blocks = lax.all_to_all(block, MP, 0, 0, tiled=True)  9.66 us
    pallas_call x1, Pallas kernels, mixture(): pl.pallas_call(mixture_kernel, in_specs=[pl.BlockSpec(memory_space=pltpu....  9.15 us
    all_to_all x1, starting transfers between devices, local(): blocks = lax.all_to_all(block, MP, 0, 0, tiled=True)  9.15 us
    ppermute x1, starting transfers between devices, local(): policy_other = lax.ppermute(policy_send, DP_MP, pairs)  4.04 us
  transfers between devices with their start and end apart: 8, of which 5 were waited for; matrix products, arithmetic and copies ran while one was open for 1% of the time, Pallas kernels for 0%

profile of v6, /device:TPU:1, one launch (start us, length us, event | category | flops | bytes accessed | tf_op | source)
XLA Modules:
  0.0 122.9 jit_solution(16466566687797190819)
XLA Ops:
  7.4 2.8 %normalize.1 = (bf16[48,3584]{1,0:T(8,128)(2,1)}, bf16[16,896]{1,0:T(8,128)(2,1)S(1)}) custom-call(s32[3]{0:T(128)S(1)} %pad_add_fusion.place_ref, bf16[64,3584]{1,0:T(8,128)(2,1)} %policy_ref.1, bf16[64,3584]{1,0:T(8,128)(2,1)} %reference_ref.1, f32[3584]{0:T(1024)} %policy_gain_ref.1, f32[3584]{0:T(1024)} %reference_gain_ref.1), custom_call_target="tpu_custom_call" | custom-call | tf_op jit(solution)/shard_map/normalize/pallas_call | solution.py:60
  10.2 4.0 %collective-permute-start.3 = (bf16[256,3584]{1,0:T(8,128)(2,1)}, bf16[256,3584]{1,0:T(8,128)(2,1)}, u32[]{:S(2)}, u32[]{:S(2)}) collective-permute-start(bf16[256,3584]{1,0:T(8,128)(2,1)} %policy_own_ref.1), channel_id=1, source_target_pairs={{0,1},{1,0},{2,3},{3,2},{4,5},{5,4},{6,7},{7,6},{8,9},{9,8},{10,11... | collective-permute-start | bytes 5505032 | tf_op jit(solution)/shard_map/ppermute | solution.py:363
  14.2 1.9 %collective-permute-start.4 = (bf16[256,3584]{1,0:T(8,128)(2,1)}, bf16[256,3584]{1,0:T(8,128)(2,1)}, u32[]{:S(2)}, u32[]{:S(2)}) collective-permute-start(bf16[256,3584]{1,0:T(8,128)(2,1)} %reference_own_ref.1), channel_id=1, source_target_pairs={{0,1},{1,0},{2,3},{3,2},{4,5},{5,4},{6,7},{7,6},{8,9},{9,8},{10,11... | collective-permute-start | bytes 5505032 | tf_op jit(solution)/shard_map/ppermute | solution.py:364
  16.1 26.1 %all-gather.1 = bf16[256,896]{1,0:T(8,128)(2,1)S(1)} all-gather(bf16[16,896]{1,0:T(8,128)(2,1)S(1)} %get-tuple-element.22), channel_id=3, replica_groups=mesh['dp_0'=8,'dp_1'=2,'mp_0'=8,'mp_1'=4] {'dp_0','dp_1'}, dimensions={0}, use_global_device_ids=true | all-gather | bytes 487424 | tf_op jit(solution)/shard_map/all_gather | solution.py:365
  42.2 7.3 %collective-permute-start.2 = (bf16[16,16,896]{2,1,0:T(8,128)(2,1)S(1)}, bf16[16,16,896]{2,1,0:T(8,128)(2,1)}, u32[]{:S(2)}, u32[]{:S(2)}) collective-permute-start(bf16[16,16,896]{2,1,0:T(8,128)(2,1)S(1)} %bitcast.13), channel_id=1, source_target_pairs={{0,31},{1,30},{2,29},{3,28},{4,11},{5,10},{6,9},{7,8},{8,7},{9,6},... | collective-permute-start | bytes 1376264 | tf_op jit(solution)/shard_map/ppermute | solution.py:366
  49.5 1.9 %collective-permute-start.1 = (bf16[16,16,896]{2,1,0:T(8,128)(2,1)S(1)}, bf16[16,16,896]{2,1,0:T(8,128)(2,1)}, u32[]{:S(2)}, u32[]{:S(2)}) collective-permute-start(bf16[16,16,896]{2,1,0:T(8,128)(2,1)S(1)} %bitcast.14), channel_id=1, source_target_pairs={{0,28},{1,29},{2,30},{3,31},{4,8},{5,9},{6,10},{7,11},{8,4},{9,5},... | collective-permute-start | bytes 1376264 | tf_op jit(solution)/shard_map/ppermute | solution.py:366
  51.4 2.2 %collective-permute-start = (bf16[16,16,896]{2,1,0:T(8,128)(2,1)S(1)}, bf16[16,16,896]{2,1,0:T(8,128)(2,1)}, u32[]{:S(2)}, u32[]{:S(2)}) collective-permute-start(bf16[16,16,896]{2,1,0:T(8,128)(2,1)S(1)} %bitcast.15), channel_id=1, source_target_pairs={{0,3},{1,2},{2,1},{3,0},{4,7},{5,6},{6,5},{7,4},{8,11},{9,10},{10,... | collective-permute-start | bytes 1376264 | tf_op jit(solution)/shard_map/ppermute | solution.py:366
  53.7 0.1 reshape.54
  53.8 0.1 sub.55
  53.9 0.1 sub.58
  54.0 0.1 reshape.53
  54.2 0.9 collective-permute-done.4.reference_other_ref
  55.1 0.1 broadcast_in_dim.24.weight_ref
  55.2 0.2 broadcast_in_dim.26.token_ref
  55.4 4.9 %collective-permute-done.2.quarter_3_ref = bf16[16,16,896]{2,1,0:T(8,128)(2,1)} collective-permute-done((bf16[16,16,896]{2,1,0:T(8,128)(2,1)S(1)}, bf16[16,16,896]{2,1,0:T(8,128)(2,1)}, u32[]{:S(2)}, u32[]{:S(2)}) %collective-permute-start.2) | collective-permute-done | bytes 458784 | tf_op jit(solution)/shard_map/ppermute | solution.py:366
  60.4 9.1 %collective-permute-done.1.quarter_2_ref = bf16[16,16,896]{2,1,0:T(8,128)(2,1)} collective-permute-done((bf16[16,16,896]{2,1,0:T(8,128)(2,1)S(1)}, bf16[16,16,896]{2,1,0:T(8,128)(2,1)}, u32[]{:S(2)}, u32[]{:S(2)}) %collective-permute-start.1) | collective-permute-done | bytes 458784 | tf_op jit(solution)/shard_map/ppermute | solution.py:366
  69.5 0.9 collective-permute-done.quarter_1_ref
  70.4 9.1 %mixture.1 = (f32[512,256]{1,0:T(8,128)S(1)}, f32[512,256]{1,0:T(8,128)}, f32[16,1,1408]{2,1,0:T(1,128)S(1)}) custom-call(s32[3]{0:T(128)S(1)} %pad_add_fusion.place_ref, bf16[16,48,3584]{2,1,0:T(8,128)(2,1)} %bitcast.12, bf16[16,16,896]{2,1,0:T(8,128)(2,1)} %bitcast.16, bf16[16,16,896]{2,1,0:T(8,128)(2,1)} %collective-permute-done.quarter_1_ref, ...), custom_call_target="tpu_custom_call" | custom-call | tf_op jit(solution)/shard_map/mixture/pallas_call | solution.py:184
  79.6 12.5 %all_to_all.10 = f32[16,1,1408]{2,1,0:T(1,128)S(1)} all-to-all(f32[16,1,1408]{2,1,0:T(1,128)S(1)} %get-tuple-element.30), channel_id=1, replica_groups=mesh['dp_0'=8,'dp_1'=2,'mp_0'=8,'mp_1'=4] {'dp_0','dp_1'}, dimensions={0} | all-to-all | bytes 180224 | tf_op jit(solution)/shard_map/all_to_all | solution.py:384
  92.1 1.9 %collective-permute-start.5 = (f32[512,256]{1,0:T(8,128)}, f32[512,256]{1,0:T(8,128)S(1)}, u32[]{:S(2)}, u32[]{:S(2)}) collective-permute-start(f32[512,256]{1,0:T(8,128)} %get-tuple-element.32), channel_id=1, source_target_pairs={{0,1},{1,0},{2,3},{3,2},{4,5},{5,4},{6,7},{7,6},{8,9},{9,8},{10,11... | collective-permute-start | bytes 1572872 | tf_op jit(solution)/shard_map/ppermute | solution.py:386
  94.1 0.7 broadcast_in_dim.27
  94.8 9.1 %all-to-all-start.1 = ((f32[32,1,1408]{2,1,0:T(1,128)}), f32[32,1,1408]{2,1,0:T(1,128)S(1)}, u32[]{:S(2)}, u32[]{:S(2)}) async-start(f32[32,1,1408]{2,1,0:T(1,128)} %broadcast_in_dim.27), calls=%async_computation.1 | async-start | bytes 360448 | tf_op jit(solution)/shard_map/all_to_all | solution.py:389
  104.1 9.7 %all-to-all-done.1.blocks_ref = f32[32,1,1408]{2,1,0:T(1,128)S(1)} async-done(((f32[32,1,1408]{2,1,0:T(1,128)}), f32[32,1,1408]{2,1,0:T(1,128)S(1)}, u32[]{:S(2)}, u32[]{:S(2)}) %all-to-all-start.1) | async-done | bytes 180256 | tf_op jit(solution)/shard_map/all_to_all | solution.py:389
  113.7 2.3 %finish.1 = (f32[16,2,32,256]{3,2,1,0:T(8,128)}, f32[3,64]{1,0:T(4,128)}) custom-call(s32[3]{0:T(128)S(1)} %pad_add_fusion.place_ref, f32[512,256]{1,0:T(8,128)S(1)} %get-tuple-element.29.own_ref, f32[512,256]{1,0:T(8,128)S(1)} %collective-permute-done.5.other_ref, f32[32,1,1408]{2,1,0:T(1,128)S(1)} %all-to-all-done.1.blocks_ref, ...), custom_call_target="tpu_custom_call" | custom-call | tf_op jit(solution)/shard_map/finish/pallas_call | solution.py:286
  (20 shorter events, 0.5 us)
Async XLA Ops:
  7.2 63.3 %copy-start = (bf16[256,3584]{1,0:T(8,128)(2,1)S(1)}, bf16[256,3584]{1,0:T(8,128)(2,1)}, u32[]{:S(2)}) copy-start(bf16[256,3584]{1,0:T(8,128)(2,1)} %policy_own_ref.1) | copy-start | bytes 5505028
  7.2 46.5 %copy-start.2 = (s32[1024]{0:T(1024)S(1)}, s32[1024]{0:T(1024)}, u32[]{:S(2)}) copy-start(s32[1024]{0:T(1024)} %param.15) | copy-start | bytes 12292
  7.2 46.8 %copy-start.3 = (f32[1024]{0:T(1024)S(1)}, f32[1024]{0:T(1024)}, u32[]{:S(2)}) copy-start(f32[1024]{0:T(1024)} %param.14) | copy-start | bytes 12292
  7.2 63.2 %all-gather.4.cloned.1.call-start = ((), (), s32[]{:S(2)}) async-start(), calls=%async_computation.2 | async-start | bytes 5849088 | tf_op jit(solution)/shard_map/all_gather | solution.py:362
  10.2 44.0 %collective-permute-start.3 = (bf16[256,3584]{1,0:T(8,128)(2,1)}, bf16[256,3584]{1,0:T(8,128)(2,1)}, u32[]{:S(2)}, u32[]{:S(2)}) collective-permute-start(bf16[256,3584]{1,0:T(8,128)(2,1)} %policy_own_ref.1), channel_id=1, source_target_pairs={{0,1},{1,0},{2,3},{3,2},{4,5},{5,4},{6,7},{7,6},{8,9},{9,8},{10,11... | collective-permute-start | bytes 5505032 | tf_op jit(solution)/shard_map/ppermute | solution.py:363
  14.2 40.9 %collective-permute-start.4 = (bf16[256,3584]{1,0:T(8,128)(2,1)}, bf16[256,3584]{1,0:T(8,128)(2,1)}, u32[]{:S(2)}, u32[]{:S(2)}) collective-permute-start(bf16[256,3584]{1,0:T(8,128)(2,1)} %reference_own_ref.1), channel_id=1, source_target_pairs={{0,1},{1,0},{2,3},{3,2},{4,5},{5,4},{6,7},{7,6},{8,9},{9,8},{10,11... | collective-permute-start | bytes 5505032 | tf_op jit(solution)/shard_map/ppermute | solution.py:364
  42.2 28.2 %copy-start.1 = (bf16[256,896]{1,0:T(8,128)(2,1)}, bf16[256,896]{1,0:T(8,128)(2,1)S(1)}, u32[]{:S(2)}) copy-start(bf16[256,896]{1,0:T(8,128)(2,1)S(1)} %all-gather.1) | copy-start | bytes 1376260
  42.2 18.1 %collective-permute-start.2 = (bf16[16,16,896]{2,1,0:T(8,128)(2,1)S(1)}, bf16[16,16,896]{2,1,0:T(8,128)(2,1)}, u32[]{:S(2)}, u32[]{:S(2)}) collective-permute-start(bf16[16,16,896]{2,1,0:T(8,128)(2,1)S(1)} %bitcast.13), channel_id=1, source_target_pairs={{0,31},{1,30},{2,29},{3,28},{4,11},{5,10},{6,9},{7,8},{8,7},{9,6},... | collective-permute-start | bytes 1376264 | tf_op jit(solution)/shard_map/ppermute | solution.py:366
  49.5 20.0 %collective-permute-start.1 = (bf16[16,16,896]{2,1,0:T(8,128)(2,1)S(1)}, bf16[16,16,896]{2,1,0:T(8,128)(2,1)}, u32[]{:S(2)}, u32[]{:S(2)}) collective-permute-start(bf16[16,16,896]{2,1,0:T(8,128)(2,1)S(1)} %bitcast.14), channel_id=1, source_target_pairs={{0,28},{1,29},{2,30},{3,31},{4,8},{5,9},{6,10},{7,11},{8,4},{9,5},... | collective-permute-start | bytes 1376264 | tf_op jit(solution)/shard_map/ppermute | solution.py:366
  51.4 19.0 %collective-permute-start = (bf16[16,16,896]{2,1,0:T(8,128)(2,1)S(1)}, bf16[16,16,896]{2,1,0:T(8,128)(2,1)}, u32[]{:S(2)}, u32[]{:S(2)}) collective-permute-start(bf16[16,16,896]{2,1,0:T(8,128)(2,1)S(1)} %bitcast.15), channel_id=1, source_target_pairs={{0,3},{1,2},{2,1},{3,0},{4,7},{5,6},{6,5},{7,4},{8,11},{9,10},{10,... | collective-permute-start | bytes 1376264 | tf_op jit(solution)/shard_map/ppermute | solution.py:366
  92.1 21.6 %collective-permute-start.5 = (f32[512,256]{1,0:T(8,128)}, f32[512,256]{1,0:T(8,128)S(1)}, u32[]{:S(2)}, u32[]{:S(2)}) collective-permute-start(f32[512,256]{1,0:T(8,128)} %get-tuple-element.32), channel_id=1, source_target_pairs={{0,1},{1,0},{2,3},{3,2},{4,5},{5,4},{6,7},{7,6},{8,9},{9,8},{10,11... | collective-permute-start | bytes 1572872 | tf_op jit(solution)/shard_map/ppermute | solution.py:386
  94.8 18.9 %all-to-all-start.1 = ((f32[32,1,1408]{2,1,0:T(1,128)}), f32[32,1,1408]{2,1,0:T(1,128)S(1)}, u32[]{:S(2)}, u32[]{:S(2)}) async-start(f32[32,1,1408]{2,1,0:T(1,128)} %broadcast_in_dim.27), calls=%async_computation.1 | async-start | bytes 360448 | tf_op jit(solution)/shard_map/all_to_all | solution.py:389
Sparse Core Ops, SparseCore 0:
  10.7 53.8 all-gather.3

commit v7 on v6

--- a/solution.py
+++ b/solution.py
@@ -113,8 +113,10 @@
         return [pltpu.make_async_copy(*pair, sem.at[k, i]) for i, pair in enumerate(pairs)]
 
     quarters = []
+    core = place_ref[1] % 2
+    flips = (0, 1 + core, 2 - core, 3)
     for i, ref in enumerate((quarter_0_ref, quarter_1_ref, quarter_2_ref, quarter_3_ref)):
-        start = pl.multiple_of((place_ref[2] ^ i) * (width // 4), 128)
+        start = pl.multiple_of((place_ref[2] ^ flips[i]) * (width // 4), 128)
         target = hidden.at[:, 0, pl.ds(part // 2, part // 2), pl.ds(start, width // 4)]
         quarters.append(pltpu.make_async_copy(ref, target, quarter_sem.at[i]))
     for quarter in quarters:
@@ -351,8 +353,9 @@
     place = jnp.stack([half, shard, quarter]).astype(jnp.int32)
     sizes = lax.axis_size("dp_0"), lax.axis_size("mp_0"), lax.axis_size("mp_1")
     pairs = pairs_of(sizes, lambda c, j, k: (j, k ^ 1) if c == 0 else (j ^ 1, k))
-    across = pairs_of(sizes, lambda c, j, k: (j, beside(k, sizes[2])))
-    along = pairs_of(sizes, lambda c, j, k: (beside(j, sizes[1]), k))
+    beyond = pairs_of(
+        sizes, lambda c, j, k: (j, beside(k, sizes[2])) if c == 0 else (beside(j, sizes[1]), k)
+    )
     aslant = pairs_of(sizes, lambda c, j, k: (beside(j, sizes[1]), beside(k, sizes[2])))
 
     main, part_quarter = normalize(place, policy_hidden, reference_hidden, policy_gain, reference_gain)
@@ -363,7 +366,10 @@
     policy_other = lax.ppermute(policy_send, DP_MP, pairs)
     reference_other = lax.ppermute(reference_send, DP_MP, pairs)
     held = lax.all_gather(part_quarter, DP, axis=0)
-    quarters = [held] + [lax.ppermute(held, DP_MP, way) for way in (across, along, aslant)]
+    fetched = lax.ppermute(held, DP_MP, beyond)
+    opposite = lax.ppermute(held, DP_MP, aslant)
+    swapped = lax.ppermute(fetched, "dp_1", [(0, 1), (1, 0)])
+    quarters = [held, fetched, swapped, opposite]
 
     seqs = shards * part
     weights = mixture_weight.reshape(shards, 2, part)

time: 124 us -> 121 us (0.976)
  waiting for transfers between devices: 25.6 us -> 20.4 us
  starting transfers between devices: 28.4 us -> 31.7 us
    ppermute x3, waiting for transfers between devices: 15 us -> 10.7 us  [the longest x1 8.57 us: local(): opposite = lax.ppermute(held, DP_MP, aslant)]
    ppermute x1, starting transfers between devices: 1.91 us -> 3.81 us  [local(): diff_other = lax.ppermute(diff_send, DP_MP, pairs)]
  transfers between devices with their start and end apart: 8 -> 8, of which waited for: 5 -> 3; matrix products, arithmetic and copies ran while one was open for 1% -> 1% of each run, Pallas kernels for 0% -> 0%
where the time goes in v7:
time: 121 us; the launch traced here: 120 us
  blocking collectives  38.1 us (31%)
  starting transfers between devices  31.7 us (26%)
  waiting for transfers between devices  20.4 us (17%)
  between operations  14.3 us (12%)
  Pallas kernels  14.1 us (12%)
  local copies, waits for them, and re-layouts  1.59 us (1%)
    all_gather x1, blocking collectives, local(): held = lax.all_gather(part_quarter, DP, axis=0)  26.1 us
    all_to_all x1, blocking collectives, local(): block = lax.all_to_all(block, DP, 0, 0, tiled=True)  12 us
    all_to_all x1, starting transfers between devices, local(): blocks = lax.all_to_all(block, MP, 0, 0, tiled=True)  10.4 us
    all_to_all x1, waiting for transfers between devices, local(): blocks = lax.all_to_all(block, MP, 0, 0, tiled=True)  9.66 us
    pallas_call x1, Pallas kernels, mixture(): pl.pallas_call(mixture_kernel, in_specs=[pl.BlockSpec(memory_space=pltpu....  9.11 us
    ppermute x1, waiting for transfers between devices, local(): opposite = lax.ppermute(held, DP_MP, aslant)  8.57 us
    ppermute x1, starting transfers between devices, local(): fetched = lax.ppermute(held, DP_MP, beyond)  5.09 us
    ppermute x1, starting transfers between devices, local(): opposite = lax.ppermute(held, DP_MP, aslant)  4.09 us
  transfers between devices with their start and end apart: 8, of which 3 were waited for; matrix products, arithmetic and copies ran while one was open for 1% of the time, Pallas kernels for 0%

profile of v7, /device:TPU:1, one launch (start us, length us, event | category | flops | bytes accessed | tf_op | source)
XLA Modules:
  0.0 120.5 jit_solution(4528840764764195658)
XLA Ops:
  7.4 2.8 %normalize.1 = (bf16[48,3584]{1,0:T(8,128)(2,1)}, bf16[16,896]{1,0:T(8,128)(2,1)S(1)}) custom-call(s32[3]{0:T(128)S(1)} %pad_add_fusion.place_ref, bf16[64,3584]{1,0:T(8,128)(2,1)} %policy_ref.1, bf16[64,3584]{1,0:T(8,128)(2,1)} %reference_ref.1, f32[3584]{0:T(1024)} %policy_gain_ref.1, f32[3584]{0:T(1024)} %reference_gain_ref.1), custom_call_target="tpu_custom_call" | custom-call | tf_op jit(solution)/shard_map/normalize/pallas_call | solution.py:60
  10.2 4.0 %collective-permute-start.3 = (bf16[256,3584]{1,0:T(8,128)(2,1)}, bf16[256,3584]{1,0:T(8,128)(2,1)}, u32[]{:S(2)}, u32[]{:S(2)}) collective-permute-start(bf16[256,3584]{1,0:T(8,128)(2,1)} %policy_own_ref.1), channel_id=1, source_target_pairs={{0,1},{1,0},{2,3},{3,2},{4,5},{5,4},{6,7},{7,6},{8,9},{9,8},{10,11... | collective-permute-start | bytes 5505032 | tf_op jit(solution)/shard_map/ppermute | solution.py:366
  14.2 1.9 %collective-permute-start.4 = (bf16[256,3584]{1,0:T(8,128)(2,1)}, bf16[256,3584]{1,0:T(8,128)(2,1)}, u32[]{:S(2)}, u32[]{:S(2)}) collective-permute-start(bf16[256,3584]{1,0:T(8,128)(2,1)} %reference_own_ref.1), channel_id=1, source_target_pairs={{0,1},{1,0},{2,3},{3,2},{4,5},{5,4},{6,7},{7,6},{8,9},{9,8},{10,11... | collective-permute-start | bytes 5505032 | tf_op jit(solution)/shard_map/ppermute | solution.py:367
  16.1 26.1 %all-gather.1 = bf16[256,896]{1,0:T(8,128)(2,1)S(1)} all-gather(bf16[16,896]{1,0:T(8,128)(2,1)S(1)} %get-tuple-element.22), channel_id=3, replica_groups=mesh['dp_0'=8,'dp_1'=2,'mp_0'=8,'mp_1'=4] {'dp_0','dp_1'}, dimensions={0}, use_global_device_ids=true | all-gather | bytes 487424 | tf_op jit(solution)/shard_map/all_gather | solution.py:368
  42.2 5.1 %collective-permute-start = (bf16[16,16,896]{2,1,0:T(8,128)(2,1)S(1)}, bf16[16,16,896]{2,1,0:T(8,128)(2,1)}, u32[]{:S(2)}, u32[]{:S(2)}) collective-permute-start(bf16[16,16,896]{2,1,0:T(8,128)(2,1)S(1)} %bitcast.13), channel_id=1, source_target_pairs={{0,3},{1,2},{2,1},{3,0},{4,7},{5,6},{6,5},{7,4},{8,11},{9,10},{10,... | collective-permute-start | bytes 1376264 | tf_op jit(solution)/shard_map/ppermute | solution.py:369
  47.3 4.1 %collective-permute-start.2 = (bf16[16,16,896]{2,1,0:T(8,128)(2,1)S(1)}, bf16[16,16,896]{2,1,0:T(8,128)(2,1)}, u32[]{:S(2)}, u32[]{:S(2)}) collective-permute-start(bf16[16,16,896]{2,1,0:T(8,128)(2,1)S(1)} %bitcast.14), channel_id=1, source_target_pairs={{0,31},{1,30},{2,29},{3,28},{4,11},{5,10},{6,9},{7,8},{8,7},{9,6},... | collective-permute-start | bytes 1376264 | tf_op jit(solution)/shard_map/ppermute | solution.py:370
  51.4 2.2 %collective-permute-done.quarter_1_ref = bf16[16,16,896]{2,1,0:T(8,128)(2,1)} collective-permute-done((bf16[16,16,896]{2,1,0:T(8,128)(2,1)S(1)}, bf16[16,16,896]{2,1,0:T(8,128)(2,1)}, u32[]{:S(2)}, u32[]{:S(2)}) %collective-permute-start) | collective-permute-done | bytes 458784 | tf_op jit(solution)/shard_map/ppermute | solution.py:369
  53.6 2.4 %collective-permute-start.1 = (bf16[16,16,896]{2,1,0:T(8,128)(2,1)}, bf16[16,16,896]{2,1,0:T(8,128)(2,1)}, u32[]{:S(2)}, u32[]{:S(2)}) collective-permute-start(bf16[16,16,896]{2,1,0:T(8,128)(2,1)} %collective-permute-done.quarter_1_ref), channel_id=1, source_target_pairs={{0,32},{32,0},{1,33},{33,1},{2,34},{34,2},{3,35},{35,3},{4,36},{36... | collective-permute-start | bytes 1376264 | tf_op jit(solution)/shard_map/ppermute | solution.py:371
  56.0 0.1 reshape.54
  56.2 0.1 sub.55
  56.3 0.1 sub.58
  56.3 0.1 reshape.53
  56.5 0.1 broadcast_in_dim.23
  56.6 0.1 broadcast_in_dim.24.weight_ref
  56.7 0.2 broadcast_in_dim.26.token_ref
  56.9 8.6 %collective-permute-done.2.quarter_3_ref = bf16[16,16,896]{2,1,0:T(8,128)(2,1)} collective-permute-done((bf16[16,16,896]{2,1,0:T(8,128)(2,1)S(1)}, bf16[16,16,896]{2,1,0:T(8,128)(2,1)}, u32[]{:S(2)}, u32[]{:S(2)}) %collective-permute-start.2) | collective-permute-done | bytes 458784 | tf_op jit(solution)/shard_map/ppermute | solution.py:370
  65.5 9.1 %mixture.1 = (f32[512,256]{1,0:T(8,128)S(1)}, f32[512,256]{1,0:T(8,128)}, f32[16,1,1408]{2,1,0:T(1,128)S(1)}) custom-call(s32[3]{0:T(128)S(1)} %pad_add_fusion.place_ref, bf16[16,48,3584]{2,1,0:T(8,128)(2,1)} %bitcast.12, bf16[16,16,896]{2,1,0:T(8,128)(2,1)} %bitcast.15, bf16[16,16,896]{2,1,0:T(8,128)(2,1)} %collective-permute-done.quarter_1_ref, ...), custom_call_target="tpu_custom_call" | custom-call | tf_op jit(solution)/shard_map/mixture/pallas_call | solution.py:186
  74.6 12.0 %all_to_all.10 = f32[16,1,1408]{2,1,0:T(1,128)S(1)} all-to-all(f32[16,1,1408]{2,1,0:T(1,128)S(1)} %get-tuple-element.30), channel_id=1, replica_groups=mesh['dp_0'=8,'dp_1'=2,'mp_0'=8,'mp_1'=4] {'dp_0','dp_1'}, dimensions={0} | all-to-all | bytes 180224 | tf_op jit(solution)/shard_map/all_to_all | solution.py:390
  86.6 3.8 %collective-permute-start.5 = (f32[512,256]{1,0:T(8,128)}, f32[512,256]{1,0:T(8,128)S(1)}, u32[]{:S(2)}, u32[]{:S(2)}) collective-permute-start(f32[512,256]{1,0:T(8,128)} %get-tuple-element.32), channel_id=1, source_target_pairs={{0,1},{1,0},{2,3},{3,2},{4,5},{5,4},{6,7},{7,6},{8,9},{9,8},{10,11... | collective-permute-start | bytes 1572872 | tf_op jit(solution)/shard_map/ppermute | solution.py:392
  90.5 0.7 broadcast_in_dim.27
  91.2 10.4 %all-to-all-start.1 = ((f32[32,1,1408]{2,1,0:T(1,128)}), f32[32,1,1408]{2,1,0:T(1,128)S(1)}, u32[]{:S(2)}, u32[]{:S(2)}) async-start(f32[32,1,1408]{2,1,0:T(1,128)} %broadcast_in_dim.27), calls=%async_computation.1 | async-start | bytes 360448 | tf_op jit(solution)/shard_map/all_to_all | solution.py:395
  101.6 0.1 dynamic-slice_bitcast_fusion.weight_ref
  101.7 9.7 %all-to-all-done.1.blocks_ref = f32[32,1,1408]{2,1,0:T(1,128)S(1)} async-done(((f32[32,1,1408]{2,1,0:T(1,128)}), f32[32,1,1408]{2,1,0:T(1,128)S(1)}, u32[]{:S(2)}, u32[]{:S(2)}) %all-to-all-start.1) | async-done | bytes 180256 | tf_op jit(solution)/shard_map/all_to_all | solution.py:395
  111.3 2.3 %finish.1 = (f32[16,2,32,256]{3,2,1,0:T(8,128)}, f32[3,64]{1,0:T(4,128)}) custom-call(s32[3]{0:T(128)S(1)} %pad_add_fusion.place_ref, f32[512,256]{1,0:T(8,128)S(1)} %get-tuple-element.29.own_ref, f32[512,256]{1,0:T(8,128)S(1)} %collective-permute-done.5.other_ref, f32[32,1,1408]{2,1,0:T(1,128)S(1)} %all-to-all-done.1.blocks_ref, ...), custom_call_target="tpu_custom_call" | custom-call | tf_op jit(solution)/shard_map/finish/pallas_call | solution.py:288
  (20 shorter events, 0.3 us)
Async XLA Ops:
  7.2 58.3 %copy-start = (bf16[256,3584]{1,0:T(8,128)(2,1)S(1)}, bf16[256,3584]{1,0:T(8,128)(2,1)}, u32[]{:S(2)}) copy-start(bf16[256,3584]{1,0:T(8,128)(2,1)} %policy_own_ref.1) | copy-start | bytes 5505028
  7.2 48.8 %copy-start.2 = (s32[1024]{0:T(1024)S(1)}, s32[1024]{0:T(1024)}, u32[]{:S(2)}) copy-start(s32[1024]{0:T(1024)} %param.15) | copy-start | bytes 12292
  7.2 49.1 %copy-start.3 = (f32[1024]{0:T(1024)S(1)}, f32[1024]{0:T(1024)}, u32[]{:S(2)}) copy-start(f32[1024]{0:T(1024)} %param.14) | copy-start | bytes 12292
  7.2 58.3 %all-gather.4.cloned.1.call-start = ((), (), s32[]{:S(2)}) async-start(), calls=%async_computation.2 | async-start | bytes 5849088 | tf_op jit(solution)/shard_map/all_gather | solution.py:365
  10.2 46.4 %collective-permute-start.3 = (bf16[256,3584]{1,0:T(8,128)(2,1)}, bf16[256,3584]{1,0:T(8,128)(2,1)}, u32[]{:S(2)}, u32[]{:S(2)}) collective-permute-start(bf16[256,3584]{1,0:T(8,128)(2,1)} %policy_own_ref.1), channel_id=1, source_target_pairs={{0,1},{1,0},{2,3},{3,2},{4,5},{5,4},{6,7},{7,6},{8,9},{9,8},{10,11... | collective-permute-start | bytes 5505032 | tf_op jit(solution)/shard_map/ppermute | solution.py:366
  14.2 42.4 %collective-permute-start.4 = (bf16[256,3584]{1,0:T(8,128)(2,1)}, bf16[256,3584]{1,0:T(8,128)(2,1)}, u32[]{:S(2)}, u32[]{:S(2)}) collective-permute-start(bf16[256,3584]{1,0:T(8,128)(2,1)} %reference_own_ref.1), channel_id=1, source_target_pairs={{0,1},{1,0},{2,3},{3,2},{4,5},{5,4},{6,7},{7,6},{8,9},{9,8},{10,11... | collective-permute-start | bytes 5505032 | tf_op jit(solution)/shard_map/ppermute | solution.py:367
  42.2 23.2 %copy-start.1 = (bf16[256,896]{1,0:T(8,128)(2,1)}, bf16[256,896]{1,0:T(8,128)(2,1)S(1)}, u32[]{:S(2)}) copy-start(bf16[256,896]{1,0:T(8,128)(2,1)S(1)} %all-gather.1) | copy-start | bytes 1376260
  42.2 11.4 %collective-permute-start = (bf16[16,16,896]{2,1,0:T(8,128)(2,1)S(1)}, bf16[16,16,896]{2,1,0:T(8,128)(2,1)}, u32[]{:S(2)}, u32[]{:S(2)}) collective-permute-start(bf16[16,16,896]{2,1,0:T(8,128)(2,1)S(1)} %bitcast.13), channel_id=1, source_target_pairs={{0,3},{1,2},{2,1},{3,0},{4,7},{5,6},{6,5},{7,4},{8,11},{9,10},{10,... | collective-permute-start | bytes 1376264 | tf_op jit(solution)/shard_map/ppermute | solution.py:369
  47.3 18.1 %collective-permute-start.2 = (bf16[16,16,896]{2,1,0:T(8,128)(2,1)S(1)}, bf16[16,16,896]{2,1,0:T(8,128)(2,1)}, u32[]{:S(2)}, u32[]{:S(2)}) collective-permute-start(bf16[16,16,896]{2,1,0:T(8,128)(2,1)S(1)} %bitcast.14), channel_id=1, source_target_pairs={{0,31},{1,30},{2,29},{3,28},{4,11},{5,10},{6,9},{7,8},{8,7},{9,6},... | collective-permute-start | bytes 1376264 | tf_op jit(solution)/shard_map/ppermute | solution.py:370
  53.6 11.9 %collective-permute-start.1 = (bf16[16,16,896]{2,1,0:T(8,128)(2,1)}, bf16[16,16,896]{2,1,0:T(8,128)(2,1)}, u32[]{:S(2)}, u32[]{:S(2)}) collective-permute-start(bf16[16,16,896]{2,1,0:T(8,128)(2,1)} %collective-permute-done.quarter_1_ref), channel_id=1, source_target_pairs={{0,32},{32,0},{1,33},{33,1},{2,34},{34,2},{3,35},{35,3},{4,36},{36... | collective-permute-start | bytes 1376264 | tf_op jit(solution)/shard_map/ppermute | solution.py:371
  86.6 24.8 %collective-permute-start.5 = (f32[512,256]{1,0:T(8,128)}, f32[512,256]{1,0:T(8,128)S(1)}, u32[]{:S(2)}, u32[]{:S(2)}) collective-permute-start(f32[512,256]{1,0:T(8,128)} %get-tuple-element.32), channel_id=1, source_target_pairs={{0,1},{1,0},{2,3},{3,2},{4,5},{5,4},{6,7},{7,6},{8,9},{9,8},{10,11... | collective-permute-start | bytes 1572872 | tf_op jit(solution)/shard_map/ppermute | solution.py:392
  91.2 20.1 %all-to-all-start.1 = ((f32[32,1,1408]{2,1,0:T(1,128)}), f32[32,1,1408]{2,1,0:T(1,128)S(1)}, u32[]{:S(2)}, u32[]{:S(2)}) async-start(f32[32,1,1408]{2,1,0:T(1,128)} %broadcast_in_dim.27), calls=%async_computation.1 | async-start | bytes 360448 | tf_op jit(solution)/shard_map/all_to_all | solution.py:395
Sparse Core Ops, SparseCore 0:
  10.7 53.8 all-gather.3

commit v8 on v7

--- a/solution.py
+++ b/solution.py
@@ -101,16 +101,21 @@
     vocab = policy_own_ref.shape[0]
     seqs = shards * part
 
-    def loads(k):
+    def loads(model, k):
         columns = pl.ds(k * depth, depth)
-        low = pl.ds(0, part // 2)
-        rest = (policy_other_ref, reference_own_ref, reference_other_ref)
-        pairs = [
-            (main_ref.at[:, low, columns], hidden.at[:, 0, low, columns]),
-            (main_ref.at[:, pl.ds(part // 2, part), columns], hidden.at[:, 1, :, columns]),
-        ]
-        pairs += [(ref.at[:, columns], loaded.at[i, :, columns]) for i, ref in enumerate(rest)]
-        return [pltpu.make_async_copy(*pair, sem.at[k, i]) for i, pair in enumerate(pairs)]
+        low, high = pl.ds(0, part // 2), pl.ds(part // 2, part)
+        if model == 0:
+            pairs = [
+                (main_ref.at[:, low, columns], hidden.at[:, 0, low, columns]),
+                (policy_other_ref.at[:, columns], loaded.at[0, :, columns]),
+            ]
+        else:
+            pairs = [
+                (main_ref.at[:, high, columns], hidden.at[:, 1, :, columns]),
+                (reference_own_ref.at[:, columns], loaded.at[1, :, columns]),
+                (reference_other_ref.at[:, columns], loaded.at[2, :, columns]),
+            ]
+        return [pltpu.make_async_copy(*pair, sem.at[model, k, i]) for i, pair in enumerate(pairs)]
 
     quarters = []
     core = place_ref[1] % 2
@@ -119,18 +124,22 @@
         start = pl.multiple_of((place_ref[2] ^ flips[i]) * (width // 4), 128)
         target = hidden.at[:, 0, pl.ds(part // 2, part // 2), pl.ds(start, width // 4)]
         quarters.append(pltpu.make_async_copy(ref, target, quarter_sem.at[i]))
+    for k in range(chunks):
+        for load in loads(1, k):
+            load.start()
     for quarter in quarters:
         quarter.start()
     for k in range(chunks):
-        for load in loads(k):
+        for load in loads(0, k):
             load.start()
-    for quarter in quarters:
-        quarter.wait()
-    for k in range(chunks):
-        for load in loads(k):
-            load.wait()
-        columns = pl.ds(k * depth, depth)
-        for model, acc in enumerate((policy_acc, reference_acc)):
+    for model, acc in ((1, reference_acc), (0, policy_acc)):
+        if model == 0:
+            for quarter in quarters:
+                quarter.wait()
+        for k in range(chunks):
+            for load in loads(model, k):
+                load.wait()
+            columns = pl.ds(k * depth, depth)
             left = hidden[:, model, :, columns].reshape(seqs, depth)
             for place in range(2):
                 index = 2 * model + place
@@ -198,7 +207,7 @@
             pltpu.VMEM((seqs, 2 * vocab), jnp.float32),
             pltpu.VMEM((seqs, 2 * vocab), jnp.float32),
             pltpu.VMEM((5, seqs, 128), jnp.float32),
-            pltpu.SemaphoreType.DMA((chunks, 5)),
+            pltpu.SemaphoreType.DMA((2, chunks, 3)),
             pltpu.SemaphoreType.DMA((4,)),
         ],
         compiler_params=pltpu.CompilerParams(vmem_limit_bytes=32 * MIB),

time: 121 us -> 122 us (level)
  no operation moved by 1% of the time
where the time goes in v8:
time: 122 us; the launch traced here: 121 us
  blocking collectives  38.1 us (31%)
  starting transfers between devices  31.7 us (26%)
  waiting for transfers between devices  20.4 us (17%)
  Pallas kernels  14.3 us (12%)
  between operations  14.3 us (12%)
  local copies, waits for them, and re-layouts  1.59 us (1%)
    all_gather x1, blocking collectives, local(): held = lax.all_gather(part_quarter, DP, axis=0)  26.1 us
    all_to_all x1, blocking collectives, local(): block = lax.all_to_all(block, DP, 0, 0, tiled=True)  12 us
    all_to_all x1, starting transfers between devices, local(): blocks = lax.all_to_all(block, MP, 0, 0, tiled=True)  10.4 us
    all_to_all x1, waiting for transfers between devices, local(): blocks = lax.all_to_all(block, MP, 0, 0, tiled=True)  9.66 us
    pallas_call x1, Pallas kernels, mixture(): pl.pallas_call(mixture_kernel, in_specs=[pl.BlockSpec(memory_space=pltpu....  9.23 us
    ppermute x1, waiting for transfers between devices, local(): opposite = lax.ppermute(held, DP_MP, aslant)  8.57 us
    ppermute x1, starting transfers between devices, local(): fetched = lax.ppermute(held, DP_MP, beyond)  5.09 us
    ppermute x1, starting transfers between devices, local(): opposite = lax.ppermute(held, DP_MP, aslant)  4.09 us
  transfers between devices with their start and end apart: 8, of which 3 were waited for; matrix products, arithmetic and copies ran while one was open for 1% of the time, Pallas kernels for 0%

profile of v8, /device:TPU:1, one launch (start us, length us, event | category | flops | bytes accessed | tf_op | source)
XLA Modules:
  0.0 120.6 jit_solution(6931411887005370686)
XLA Ops:
  7.4 2.8 %normalize.1 = (bf16[48,3584]{1,0:T(8,128)(2,1)}, bf16[16,896]{1,0:T(8,128)(2,1)S(1)}) custom-call(s32[3]{0:T(128)S(1)} %pad_add_fusion.place_ref, bf16[64,3584]{1,0:T(8,128)(2,1)} %policy_ref.1, bf16[64,3584]{1,0:T(8,128)(2,1)} %reference_ref.1, f32[3584]{0:T(1024)} %policy_gain_ref.1, f32[3584]{0:T(1024)} %reference_gain_ref.1), custom_call_target="tpu_custom_call" | custom-call | tf_op jit(solution)/shard_map/normalize/pallas_call | solution.py:60
  10.2 4.0 %collective-permute-start.3 = (bf16[256,3584]{1,0:T(8,128)(2,1)}, bf16[256,3584]{1,0:T(8,128)(2,1)}, u32[]{:S(2)}, u32[]{:S(2)}) collective-permute-start(bf16[256,3584]{1,0:T(8,128)(2,1)} %policy_own_ref.1), channel_id=1, source_target_pairs={{0,1},{1,0},{2,3},{3,2},{4,5},{5,4},{6,7},{7,6},{8,9},{9,8},{10,11... | collective-permute-start | bytes 5505032 | tf_op jit(solution)/shard_map/ppermute | solution.py:375
  14.2 1.9 %collective-permute-start.4 = (bf16[256,3584]{1,0:T(8,128)(2,1)}, bf16[256,3584]{1,0:T(8,128)(2,1)}, u32[]{:S(2)}, u32[]{:S(2)}) collective-permute-start(bf16[256,3584]{1,0:T(8,128)(2,1)} %reference_own_ref.1), channel_id=1, source_target_pairs={{0,1},{1,0},{2,3},{3,2},{4,5},{5,4},{6,7},{7,6},{8,9},{9,8},{10,11... | collective-permute-start | bytes 5505032 | tf_op jit(solution)/shard_map/ppermute | solution.py:376
  16.1 26.1 %all-gather.1 = bf16[256,896]{1,0:T(8,128)(2,1)S(1)} all-gather(bf16[16,896]{1,0:T(8,128)(2,1)S(1)} %get-tuple-element.22), channel_id=3, replica_groups=mesh['dp_0'=8,'dp_1'=2,'mp_0'=8,'mp_1'=4] {'dp_0','dp_1'}, dimensions={0}, use_global_device_ids=true | all-gather | bytes 487424 | tf_op jit(solution)/shard_map/all_gather | solution.py:377
  42.2 5.1 %collective-permute-start = (bf16[16,16,896]{2,1,0:T(8,128)(2,1)S(1)}, bf16[16,16,896]{2,1,0:T(8,128)(2,1)}, u32[]{:S(2)}, u32[]{:S(2)}) collective-permute-start(bf16[16,16,896]{2,1,0:T(8,128)(2,1)S(1)} %bitcast.13), channel_id=1, source_target_pairs={{0,3},{1,2},{2,1},{3,0},{4,7},{5,6},{6,5},{7,4},{8,11},{9,10},{10,... | collective-permute-start | bytes 1376264 | tf_op jit(solution)/shard_map/ppermute | solution.py:378
  47.3 4.1 %collective-permute-start.2 = (bf16[16,16,896]{2,1,0:T(8,128)(2,1)S(1)}, bf16[16,16,896]{2,1,0:T(8,128)(2,1)}, u32[]{:S(2)}, u32[]{:S(2)}) collective-permute-start(bf16[16,16,896]{2,1,0:T(8,128)(2,1)S(1)} %bitcast.14), channel_id=1, source_target_pairs={{0,31},{1,30},{2,29},{3,28},{4,11},{5,10},{6,9},{7,8},{8,7},{9,6},... | collective-permute-start | bytes 1376264 | tf_op jit(solution)/shard_map/ppermute | solution.py:379
  51.4 2.2 %collective-permute-done.quarter_1_ref = bf16[16,16,896]{2,1,0:T(8,128)(2,1)} collective-permute-done((bf16[16,16,896]{2,1,0:T(8,128)(2,1)S(1)}, bf16[16,16,896]{2,1,0:T(8,128)(2,1)}, u32[]{:S(2)}, u32[]{:S(2)}) %collective-permute-start) | collective-permute-done | bytes 458784 | tf_op jit(solution)/shard_map/ppermute | solution.py:378
  53.6 2.4 %collective-permute-start.1 = (bf16[16,16,896]{2,1,0:T(8,128)(2,1)}, bf16[16,16,896]{2,1,0:T(8,128)(2,1)}, u32[]{:S(2)}, u32[]{:S(2)}) collective-permute-start(bf16[16,16,896]{2,1,0:T(8,128)(2,1)} %collective-permute-done.quarter_1_ref), channel_id=1, source_target_pairs={{0,32},{32,0},{1,33},{33,1},{2,34},{34,2},{3,35},{35,3},{4,36},{36... | collective-permute-start | bytes 1376264 | tf_op jit(solution)/shard_map/ppermute | solution.py:380
  56.0 0.1 reshape.54
  56.2 0.1 sub.55
  56.3 0.1 sub.58
  56.3 0.1 reshape.53
  56.5 0.1 broadcast_in_dim.23
  56.6 0.1 broadcast_in_dim.24.weight_ref
  56.7 0.2 broadcast_in_dim.26.token_ref
  56.9 8.6 %collective-permute-done.2.quarter_3_ref = bf16[16,16,896]{2,1,0:T(8,128)(2,1)} collective-permute-done((bf16[16,16,896]{2,1,0:T(8,128)(2,1)S(1)}, bf16[16,16,896]{2,1,0:T(8,128)(2,1)}, u32[]{:S(2)}, u32[]{:S(2)}) %collective-permute-start.2) | collective-permute-done | bytes 458784 | tf_op jit(solution)/shard_map/ppermute | solution.py:379
  65.5 9.2 %mixture.1 = (f32[512,256]{1,0:T(8,128)S(1)}, f32[512,256]{1,0:T(8,128)}, f32[16,1,1408]{2,1,0:T(1,128)S(1)}) custom-call(s32[3]{0:T(128)S(1)} %pad_add_fusion.place_ref, bf16[16,48,3584]{2,1,0:T(8,128)(2,1)} %bitcast.12, bf16[16,16,896]{2,1,0:T(8,128)(2,1)} %bitcast.15, bf16[16,16,896]{2,1,0:T(8,128)(2,1)} %collective-permute-done.quarter_1_ref, ...), custom_call_target="tpu_custom_call" | custom-call | tf_op jit(solution)/shard_map/mixture/pallas_call | solution.py:195
  74.7 12.0 %all_to_all.10 = f32[16,1,1408]{2,1,0:T(1,128)S(1)} all-to-all(f32[16,1,1408]{2,1,0:T(1,128)S(1)} %get-tuple-element.30), channel_id=1, replica_groups=mesh['dp_0'=8,'dp_1'=2,'mp_0'=8,'mp_1'=4] {'dp_0','dp_1'}, dimensions={0} | all-to-all | bytes 180224 | tf_op jit(solution)/shard_map/all_to_all | solution.py:399
  86.7 3.8 %collective-permute-start.5 = (f32[512,256]{1,0:T(8,128)}, f32[512,256]{1,0:T(8,128)S(1)}, u32[]{:S(2)}, u32[]{:S(2)}) collective-permute-start(f32[512,256]{1,0:T(8,128)} %get-tuple-element.32), channel_id=1, source_target_pairs={{0,1},{1,0},{2,3},{3,2},{4,5},{5,4},{6,7},{7,6},{8,9},{9,8},{10,11... | collective-permute-start | bytes 1572872 | tf_op jit(solution)/shard_map/ppermute | solution.py:401
  90.6 0.7 broadcast_in_dim.27
  91.3 10.4 %all-to-all-start.1 = ((f32[32,1,1408]{2,1,0:T(1,128)}), f32[32,1,1408]{2,1,0:T(1,128)S(1)}, u32[]{:S(2)}, u32[]{:S(2)}) async-start(f32[32,1,1408]{2,1,0:T(1,128)} %broadcast_in_dim.27), calls=%async_computation.1 | async-start | bytes 360448 | tf_op jit(solution)/shard_map/all_to_all | solution.py:404
  101.7 0.1 dynamic-slice_bitcast_fusion.weight_ref
  101.8 9.7 %all-to-all-done.1.blocks_ref = f32[32,1,1408]{2,1,0:T(1,128)S(1)} async-done(((f32[32,1,1408]{2,1,0:T(1,128)}), f32[32,1,1408]{2,1,0:T(1,128)S(1)}, u32[]{:S(2)}, u32[]{:S(2)}) %all-to-all-start.1) | async-done | bytes 180256 | tf_op jit(solution)/shard_map/all_to_all | solution.py:404
  111.4 2.3 %finish.1 = (f32[16,2,32,256]{3,2,1,0:T(8,128)}, f32[3,64]{1,0:T(4,128)}) custom-call(s32[3]{0:T(128)S(1)} %pad_add_fusion.place_ref, f32[512,256]{1,0:T(8,128)S(1)} %get-tuple-element.29.own_ref, f32[512,256]{1,0:T(8,128)S(1)} %collective-permute-done.5.other_ref, f32[32,1,1408]{2,1,0:T(1,128)S(1)} %all-to-all-done.1.blocks_ref, ...), custom_call_target="tpu_custom_call" | custom-call | tf_op jit(solution)/shard_map/finish/pallas_call | solution.py:297
  (20 shorter events, 0.3 us)
Async XLA Ops:
  7.2 58.3 %copy-start = (bf16[256,3584]{1,0:T(8,128)(2,1)S(1)}, bf16[256,3584]{1,0:T(8,128)(2,1)}, u32[]{:S(2)}) copy-start(bf16[256,3584]{1,0:T(8,128)(2,1)} %policy_own_ref.1) | copy-start | bytes 5505028
  7.2 48.8 %copy-start.2 = (s32[1024]{0:T(1024)S(1)}, s32[1024]{0:T(1024)}, u32[]{:S(2)}) copy-start(s32[1024]{0:T(1024)} %param.15) | copy-start | bytes 12292
  7.2 49.1 %copy-start.3 = (f32[1024]{0:T(1024)S(1)}, f32[1024]{0:T(1024)}, u32[]{:S(2)}) copy-start(f32[1024]{0:T(1024)} %param.14) | copy-start | bytes 12292
  7.2 58.3 %all-gather.4.cloned.1.call-start = ((), (), s32[]{:S(2)}) async-start(), calls=%async_computation.2 | async-start | bytes 5849088 | tf_op jit(solution)/shard_map/all_gather | solution.py:374
  10.2 46.4 %collective-permute-start.3 = (bf16[256,3584]{1,0:T(8,128)(2,1)}, bf16[256,3584]{1,0:T(8,128)(2,1)}, u32[]{:S(2)}, u32[]{:S(2)}) collective-permute-start(bf16[256,3584]{1,0:T(8,128)(2,1)} %policy_own_ref.1), channel_id=1, source_target_pairs={{0,1},{1,0},{2,3},{3,2},{4,5},{5,4},{6,7},{7,6},{8,9},{9,8},{10,11... | collective-permute-start | bytes 5505032 | tf_op jit(solution)/shard_map/ppermute | solution.py:375
  14.2 42.4 %collective-permute-start.4 = (bf16[256,3584]{1,0:T(8,128)(2,1)}, bf16[256,3584]{1,0:T(8,128)(2,1)}, u32[]{:S(2)}, u32[]{:S(2)}) collective-permute-start(bf16[256,3584]{1,0:T(8,128)(2,1)} %reference_own_ref.1), channel_id=1, source_target_pairs={{0,1},{1,0},{2,3},{3,2},{4,5},{5,4},{6,7},{7,6},{8,9},{9,8},{10,11... | collective-permute-start | bytes 5505032 | tf_op jit(solution)/shard_map/ppermute | solution.py:376
  42.2 23.2 %copy-start.1 = (bf16[256,896]{1,0:T(8,128)(2,1)}, bf16[256,896]{1,0:T(8,128)(2,1)S(1)}, u32[]{:S(2)}) copy-start(bf16[256,896]{1,0:T(8,128)(2,1)S(1)} %all-gather.1) | copy-start | bytes 1376260
  42.2 11.4 %collective-permute-start = (bf16[16,16,896]{2,1,0:T(8,128)(2,1)S(1)}, bf16[16,16,896]{2,1,0:T(8,128)(2,1)}, u32[]{:S(2)}, u32[]{:S(2)}) collective-permute-start(bf16[16,16,896]{2,1,0:T(8,128)(2,1)S(1)} %bitcast.13), channel_id=1, source_target_pairs={{0,3},{1,2},{2,1},{3,0},{4,7},{5,6},{6,5},{7,4},{8,11},{9,10},{10,... | collective-permute-start | bytes 1376264 | tf_op jit(solution)/shard_map/ppermute | solution.py:378
  47.3 18.1 %collective-permute-start.2 = (bf16[16,16,896]{2,1,0:T(8,128)(2,1)S(1)}, bf16[16,16,896]{2,1,0:T(8,128)(2,1)}, u32[]{:S(2)}, u32[]{:S(2)}) collective-permute-start(bf16[16,16,896]{2,1,0:T(8,128)(2,1)S(1)} %bitcast.14), channel_id=1, source_target_pairs={{0,31},{1,30},{2,29},{3,28},{4,11},{5,10},{6,9},{7,8},{8,7},{9,6},... | collective-permute-start | bytes 1376264 | tf_op jit(solution)/shard_map/ppermute | solution.py:379
  53.6 11.9 %collective-permute-start.1 = (bf16[16,16,896]{2,1,0:T(8,128)(2,1)}, bf16[16,16,896]{2,1,0:T(8,128)(2,1)}, u32[]{:S(2)}, u32[]{:S(2)}) collective-permute-start(bf16[16,16,896]{2,1,0:T(8,128)(2,1)} %collective-permute-done.quarter_1_ref), channel_id=1, source_target_pairs={{0,32},{32,0},{1,33},{33,1},{2,34},{34,2},{3,35},{35,3},{4,36},{36... | collective-permute-start | bytes 1376264 | tf_op jit(solution)/shard_map/ppermute | solution.py:380
  86.7 24.8 %collective-permute-start.5 = (f32[512,256]{1,0:T(8,128)}, f32[512,256]{1,0:T(8,128)S(1)}, u32[]{:S(2)}, u32[]{:S(2)}) collective-permute-start(f32[512,256]{1,0:T(8,128)} %get-tuple-element.32), channel_id=1, source_target_pairs={{0,1},{1,0},{2,3},{3,2},{4,5},{5,4},{6,7},{7,6},{8,9},{9,8},{10,11... | collective-permute-start | bytes 1572872 | tf_op jit(solution)/shard_map/ppermute | solution.py:401
  91.3 20.1 %all-to-all-start.1 = ((f32[32,1,1408]{2,1,0:T(1,128)}), f32[32,1,1408]{2,1,0:T(1,128)S(1)}, u32[]{:S(2)}, u32[]{:S(2)}) async-start(f32[32,1,1408]{2,1,0:T(1,128)} %broadcast_in_dim.27), calls=%async_computation.1 | async-start | bytes 360448 | tf_op jit(solution)/shard_map/all_to_all | solution.py:404
Sparse Core Ops, SparseCore 0:
  10.7 53.8 all-gather.3

commit v9 on v7

--- a/solution.py
+++ b/solution.py
@@ -366,8 +366,8 @@
     policy_other = lax.ppermute(policy_send, DP_MP, pairs)
     reference_other = lax.ppermute(reference_send, DP_MP, pairs)
     held = lax.all_gather(part_quarter, DP, axis=0)
+    opposite = lax.ppermute(held, DP_MP, aslant)
     fetched = lax.ppermute(held, DP_MP, beyond)
-    opposite = lax.ppermute(held, DP_MP, aslant)
     swapped = lax.ppermute(fetched, "dp_1", [(0, 1), (1, 0)])
     quarters = [held, fetched, swapped, opposite]
 
@@ -387,10 +387,8 @@
         place, main, quarters, policy_embedding, policy_other, reference_embedding, reference_other, weight, token
     )
 
-    block = lax.all_to_all(block, DP, 0, 0, tiled=True)
-    block, diff_send = lax.optimization_barrier((block, diff_send))
     diff_other = lax.ppermute(diff_send, DP_MP, pairs)
-    block = jnp.sum(block, axis=0, keepdims=True)
+    block = jnp.sum(lax.all_to_all(block, DP, 0, 0, tiled=True), axis=0, keepdims=True)
     block = jnp.broadcast_to(block, (copies,) + block.shape[1:])
     blocks = lax.all_to_all(block, MP, 0, 0, tiled=True)
     mixture_shift, sampled_logprobs = finish(

time: 121 us -> 123 us (1.017)
  starting transfers between devices: 31.7 us -> 33.7 us
    all_to_all x1, starting transfers between devices: 10.4 us -> 11.8 us  [local(): blocks = lax.all_to_all(block, MP, 0, 0, tiled=True)]
where the time goes in v9:
time: 123 us; the launch traced here: 122 us
  blocking collectives  37.3 us (30%)
  starting transfers between devices  33.7 us (27%)
  waiting for transfers between devices  21.2 us (17%)
  between operations  14.3 us (12%)
  Pallas kernels  14.1 us (11%)
  local copies, waits for them, and re-layouts  1.59 us (1%)
    all_gather x1, blocking collectives, local(): held = lax.all_gather(part_quarter, DP, axis=0)  26.1 us
    all_to_all x1, starting transfers between devices, local(): blocks = lax.all_to_all(block, MP, 0, 0, tiled=True)  11.8 us
    all_to_all x1, blocking collectives, local(): lax.all_to_all(block, DP, 0, 0, tiled=True)  11.2 us
    all_to_all x1, waiting for transfers between devices, local(): blocks = lax.all_to_all(block, MP, 0, 0, tiled=True)  10.4 us
    pallas_call x1, Pallas kernels, mixture(): pl.pallas_call(mixture_kernel, in_specs=[pl.BlockSpec(memory_space=pltpu....  9.11 us
    ppermute x1, waiting for transfers between devices, local(): opposite = lax.ppermute(held, DP_MP, aslant)  8.57 us
    ppermute x1, starting transfers between devices, local(): fetched = lax.ppermute(held, DP_MP, beyond)  5.09 us
    ppermute x1, starting transfers between devices, local(): diff_other = lax.ppermute(diff_send, DP_MP, pairs)  4.31 us
  transfers between devices with their start and end apart: 8, of which 3 were waited for; matrix products, arithmetic and copies ran while one was open for 1% of the time, Pallas kernels for 0%

profile of v9, /device:TPU:1, one launch (start us, length us, event | category | flops | bytes accessed | tf_op | source)
XLA Modules:
  0.0 122.4 jit_solution(8388457193797051682)
XLA Ops:
  7.4 2.8 %normalize.1 = (bf16[48,3584]{1,0:T(8,128)(2,1)}, bf16[16,896]{1,0:T(8,128)(2,1)S(1)}) custom-call(s32[3]{0:T(128)S(1)} %pad_add_fusion.place_ref, bf16[64,3584]{1,0:T(8,128)(2,1)} %policy_ref.1, bf16[64,3584]{1,0:T(8,128)(2,1)} %reference_ref.1, f32[3584]{0:T(1024)} %policy_gain_ref.1, f32[3584]{0:T(1024)} %reference_gain_ref.1), custom_call_target="tpu_custom_call" | custom-call | tf_op jit(solution)/shard_map/normalize/pallas_call | solution.py:60
  10.2 4.0 %collective-permute-start.3 = (bf16[256,3584]{1,0:T(8,128)(2,1)}, bf16[256,3584]{1,0:T(8,128)(2,1)}, u32[]{:S(2)}, u32[]{:S(2)}) collective-permute-start(bf16[256,3584]{1,0:T(8,128)(2,1)} %policy_own_ref.1), channel_id=1, source_target_pairs={{0,1},{1,0},{2,3},{3,2},{4,5},{5,4},{6,7},{7,6},{8,9},{9,8},{10,11... | collective-permute-start | bytes 5505032 | tf_op jit(solution)/shard_map/ppermute | solution.py:366
  14.2 1.9 %collective-permute-start.4 = (bf16[256,3584]{1,0:T(8,128)(2,1)}, bf16[256,3584]{1,0:T(8,128)(2,1)}, u32[]{:S(2)}, u32[]{:S(2)}) collective-permute-start(bf16[256,3584]{1,0:T(8,128)(2,1)} %reference_own_ref.1), channel_id=1, source_target_pairs={{0,1},{1,0},{2,3},{3,2},{4,5},{5,4},{6,7},{7,6},{8,9},{9,8},{10,11... | collective-permute-start | bytes 5505032 | tf_op jit(solution)/shard_map/ppermute | solution.py:367
  16.1 26.1 %all-gather.1 = bf16[256,896]{1,0:T(8,128)(2,1)S(1)} all-gather(bf16[16,896]{1,0:T(8,128)(2,1)S(1)} %get-tuple-element.20), channel_id=3, replica_groups=mesh['dp_0'=8,'dp_1'=2,'mp_0'=8,'mp_1'=4] {'dp_0','dp_1'}, dimensions={0}, use_global_device_ids=true | all-gather | bytes 487424 | tf_op jit(solution)/shard_map/all_gather | solution.py:368
  42.2 5.1 %collective-permute-start = (bf16[16,16,896]{2,1,0:T(8,128)(2,1)S(1)}, bf16[16,16,896]{2,1,0:T(8,128)(2,1)}, u32[]{:S(2)}, u32[]{:S(2)}) collective-permute-start(bf16[16,16,896]{2,1,0:T(8,128)(2,1)S(1)} %bitcast.13), channel_id=1, source_target_pairs={{0,3},{1,2},{2,1},{3,0},{4,7},{5,6},{6,5},{7,4},{8,11},{9,10},{10,... | collective-permute-start | bytes 1376264 | tf_op jit(solution)/shard_map/ppermute | solution.py:370
  47.3 4.1 %collective-permute-start.2 = (bf16[16,16,896]{2,1,0:T(8,128)(2,1)S(1)}, bf16[16,16,896]{2,1,0:T(8,128)(2,1)}, u32[]{:S(2)}, u32[]{:S(2)}) collective-permute-start(bf16[16,16,896]{2,1,0:T(8,128)(2,1)S(1)} %bitcast.14), channel_id=1, source_target_pairs={{0,31},{1,30},{2,29},{3,28},{4,11},{5,10},{6,9},{7,8},{8,7},{9,6},... | collective-permute-start | bytes 1376264 | tf_op jit(solution)/shard_map/ppermute | solution.py:369
  51.4 2.2 %collective-permute-done.quarter_1_ref = bf16[16,16,896]{2,1,0:T(8,128)(2,1)} collective-permute-done((bf16[16,16,896]{2,1,0:T(8,128)(2,1)S(1)}, bf16[16,16,896]{2,1,0:T(8,128)(2,1)}, u32[]{:S(2)}, u32[]{:S(2)}) %collective-permute-start) | collective-permute-done | bytes 458784 | tf_op jit(solution)/shard_map/ppermute | solution.py:370
  53.6 2.4 %collective-permute-start.1 = (bf16[16,16,896]{2,1,0:T(8,128)(2,1)}, bf16[16,16,896]{2,1,0:T(8,128)(2,1)}, u32[]{:S(2)}, u32[]{:S(2)}) collective-permute-start(bf16[16,16,896]{2,1,0:T(8,128)(2,1)} %collective-permute-done.quarter_1_ref), channel_id=1, source_target_pairs={{0,32},{32,0},{1,33},{33,1},{2,34},{34,2},{3,35},{35,3},{4,36},{36... | collective-permute-start | bytes 1376264 | tf_op jit(solution)/shard_map/ppermute | solution.py:371
  56.0 0.1 reshape.54
  56.2 0.1 sub.55
  56.3 0.1 sub.58
  56.3 0.1 reshape.53
  56.5 0.1 broadcast_in_dim.23
  56.6 0.1 broadcast_in_dim.24.weight_ref
  56.7 0.2 broadcast_in_dim.26.token_ref
  56.9 8.6 %collective-permute-done.2.quarter_3_ref = bf16[16,16,896]{2,1,0:T(8,128)(2,1)} collective-permute-done((bf16[16,16,896]{2,1,0:T(8,128)(2,1)S(1)}, bf16[16,16,896]{2,1,0:T(8,128)(2,1)}, u32[]{:S(2)}, u32[]{:S(2)}) %collective-permute-start.2) | collective-permute-done | bytes 458784 | tf_op jit(solution)/shard_map/ppermute | solution.py:369
  65.5 9.1 %mixture.1 = (f32[512,256]{1,0:T(8,128)S(1)}, f32[512,256]{1,0:T(8,128)}, f32[16,1,1408]{2,1,0:T(1,128)S(1)}) custom-call(s32[3]{0:T(128)S(1)} %pad_add_fusion.place_ref, bf16[16,48,3584]{2,1,0:T(8,128)(2,1)} %bitcast.12, bf16[16,16,896]{2,1,0:T(8,128)(2,1)} %bitcast.15, bf16[16,16,896]{2,1,0:T(8,128)(2,1)} %collective-permute-done.quarter_1_ref, ...), custom_call_target="tpu_custom_call" | custom-call | tf_op jit(solution)/shard_map/mixture/pallas_call | solution.py:186
  74.6 4.3 %collective-permute-start.5 = (f32[512,256]{1,0:T(8,128)}, f32[512,256]{1,0:T(8,128)S(1)}, u32[]{:S(2)}, u32[]{:S(2)}) collective-permute-start(f32[512,256]{1,0:T(8,128)} %get-tuple-element.28), channel_id=1, source_target_pairs={{0,1},{1,0},{2,3},{3,2},{4,5},{5,4},{6,7},{7,6},{8,9},{9,8},{10,11... | collective-permute-start | bytes 1572872 | tf_op jit(solution)/shard_map/ppermute | solution.py:390
  78.9 11.2 %all_to_all.10 = f32[16,1,1408]{2,1,0:T(1,128)S(1)} all-to-all(f32[16,1,1408]{2,1,0:T(1,128)S(1)} %get-tuple-element.29), channel_id=1, replica_groups=mesh['dp_0'=8,'dp_1'=2,'mp_0'=8,'mp_1'=4] {'dp_0','dp_1'}, dimensions={0} | all-to-all | bytes 180224 | tf_op jit(solution)/shard_map/all_to_all | solution.py:391
  90.2 0.7 broadcast_in_dim.27
  91.0 11.8 %all-to-all-start.1 = ((f32[32,1,1408]{2,1,0:T(1,128)}), f32[32,1,1408]{2,1,0:T(1,128)S(1)}, u32[]{:S(2)}, u32[]{:S(2)}) async-start(f32[32,1,1408]{2,1,0:T(1,128)} %broadcast_in_dim.27), calls=%async_computation.1 | async-start | bytes 360448 | tf_op jit(solution)/shard_map/all_to_all | solution.py:393
  102.8 0.1 dynamic-slice_bitcast_fusion.weight_ref
  102.8 10.4 %all-to-all-done.1.blocks_ref = f32[32,1,1408]{2,1,0:T(1,128)S(1)} async-done(((f32[32,1,1408]{2,1,0:T(1,128)}), f32[32,1,1408]{2,1,0:T(1,128)S(1)}, u32[]{:S(2)}, u32[]{:S(2)}) %all-to-all-start.1) | async-done | bytes 180256 | tf_op jit(solution)/shard_map/all_to_all | solution.py:393
  113.3 2.3 %finish.1 = (f32[16,2,32,256]{3,2,1,0:T(8,128)}, f32[3,64]{1,0:T(4,128)}) custom-call(s32[3]{0:T(128)S(1)} %pad_add_fusion.place_ref, f32[512,256]{1,0:T(8,128)S(1)} %get-tuple-element.27.own_ref, f32[512,256]{1,0:T(8,128)S(1)} %collective-permute-done.5.other_ref, f32[32,1,1408]{2,1,0:T(1,128)S(1)} %all-to-all-done.1.blocks_ref, ...), custom_call_target="tpu_custom_call" | custom-call | tf_op jit(solution)/shard_map/finish/pallas_call | solution.py:288
  (20 shorter events, 0.3 us)
Async XLA Ops:
  7.2 58.3 %copy-start = (bf16[256,3584]{1,0:T(8,128)(2,1)S(1)}, bf16[256,3584]{1,0:T(8,128)(2,1)}, u32[]{:S(2)}) copy-start(bf16[256,3584]{1,0:T(8,128)(2,1)} %policy_own_ref.1) | copy-start | bytes 5505028
  7.2 48.8 %copy-start.2 = (s32[1024]{0:T(1024)S(1)}, s32[1024]{0:T(1024)}, u32[]{:S(2)}) copy-start(s32[1024]{0:T(1024)} %param.15) | copy-start | bytes 12292
  7.2 49.1 %copy-start.3 = (f32[1024]{0:T(1024)S(1)}, f32[1024]{0:T(1024)}, u32[]{:S(2)}) copy-start(f32[1024]{0:T(1024)} %param.14) | copy-start | bytes 12292
  7.2 58.3 %all-gather.4.cloned.1.call-start = ((), (), s32[]{:S(2)}) async-start(), calls=%async_computation.2 | async-start | bytes 5849088 | tf_op jit(solution)/shard_map/all_gather | solution.py:365
  10.2 46.4 %collective-permute-start.3 = (bf16[256,3584]{1,0:T(8,128)(2,1)}, bf16[256,3584]{1,0:T(8,128)(2,1)}, u32[]{:S(2)}, u32[]{:S(2)}) collective-permute-start(bf16[256,3584]{1,0:T(8,128)(2,1)} %policy_own_ref.1), channel_id=1, source_target_pairs={{0,1},{1,0},{2,3},{3,2},{4,5},{5,4},{6,7},{7,6},{8,9},{9,8},{10,11... | collective-permute-start | bytes 5505032 | tf_op jit(solution)/shard_map/ppermute | solution.py:366
  14.2 42.4 %collective-permute-start.4 = (bf16[256,3584]{1,0:T(8,128)(2,1)}, bf16[256,3584]{1,0:T(8,128)(2,1)}, u32[]{:S(2)}, u32[]{:S(2)}) collective-permute-start(bf16[256,3584]{1,0:T(8,128)(2,1)} %reference_own_ref.1), channel_id=1, source_target_pairs={{0,1},{1,0},{2,3},{3,2},{4,5},{5,4},{6,7},{7,6},{8,9},{9,8},{10,11... | collective-permute-start | bytes 5505032 | tf_op jit(solution)/shard_map/ppermute | solution.py:367
  42.2 23.2 %copy-start.1 = (bf16[256,896]{1,0:T(8,128)(2,1)}, bf16[256,896]{1,0:T(8,128)(2,1)S(1)}, u32[]{:S(2)}) copy-start(bf16[256,896]{1,0:T(8,128)(2,1)S(1)} %all-gather.1) | copy-start | bytes 1376260
  42.2 11.4 %collective-permute-start = (bf16[16,16,896]{2,1,0:T(8,128)(2,1)S(1)}, bf16[16,16,896]{2,1,0:T(8,128)(2,1)}, u32[]{:S(2)}, u32[]{:S(2)}) collective-permute-start(bf16[16,16,896]{2,1,0:T(8,128)(2,1)S(1)} %bitcast.13), channel_id=1, source_target_pairs={{0,3},{1,2},{2,1},{3,0},{4,7},{5,6},{6,5},{7,4},{8,11},{9,10},{10,... | collective-permute-start | bytes 1376264 | tf_op jit(solution)/shard_map/ppermute | solution.py:370
  47.3 18.1 %collective-permute-start.2 = (bf16[16,16,896]{2,1,0:T(8,128)(2,1)S(1)}, bf16[16,16,896]{2,1,0:T(8,128)(2,1)}, u32[]{:S(2)}, u32[]{:S(2)}) collective-permute-start(bf16[16,16,896]{2,1,0:T(8,128)(2,1)S(1)} %bitcast.14), channel_id=1, source_target_pairs={{0,31},{1,30},{2,29},{3,28},{4,11},{5,10},{6,9},{7,8},{8,7},{9,6},... | collective-permute-start | bytes 1376264 | tf_op jit(solution)/shard_map/ppermute | solution.py:369
  53.6 11.9 %collective-permute-start.1 = (bf16[16,16,896]{2,1,0:T(8,128)(2,1)}, bf16[16,16,896]{2,1,0:T(8,128)(2,1)}, u32[]{:S(2)}, u32[]{:S(2)}) collective-permute-start(bf16[16,16,896]{2,1,0:T(8,128)(2,1)} %collective-permute-done.quarter_1_ref), channel_id=1, source_target_pairs={{0,32},{32,0},{1,33},{33,1},{2,34},{34,2},{3,35},{35,3},{4,36},{36... | collective-permute-start | bytes 1376264 | tf_op jit(solution)/shard_map/ppermute | solution.py:371
  74.6 38.7 %collective-permute-start.5 = (f32[512,256]{1,0:T(8,128)}, f32[512,256]{1,0:T(8,128)S(1)}, u32[]{:S(2)}, u32[]{:S(2)}) collective-permute-start(f32[512,256]{1,0:T(8,128)} %get-tuple-element.28), channel_id=1, source_target_pairs={{0,1},{1,0},{2,3},{3,2},{4,5},{5,4},{6,7},{7,6},{8,9},{9,8},{10,11... | collective-permute-start | bytes 1572872 | tf_op jit(solution)/shard_map/ppermute | solution.py:390
  91.0 22.3 %all-to-all-start.1 = ((f32[32,1,1408]{2,1,0:T(1,128)}), f32[32,1,1408]{2,1,0:T(1,128)S(1)}, u32[]{:S(2)}, u32[]{:S(2)}) async-start(f32[32,1,1408]{2,1,0:T(1,128)} %broadcast_in_dim.27), calls=%async_computation.1 | async-start | bytes 360448 | tf_op jit(solution)/shard_map/all_to_all | solution.py:393
Sparse Core Ops, SparseCore 0:
  10.7 53.8 all-gather.3
